TPU v7x, 32 devices: a whole 2x2x4 slice. The times are simulated.
32 devices in a mesh: grp: 16 (over z, y, core), seq: 2 (over x).
Axes of the slice: x: 2, y: 2, z: 4, core: 2. Of those that a mesh axis runs over, the one named last changes fastest.
Arguments:
- prompt_x: bfloat16 [16, 1024, 1536], P('grp', 'seq'), may hold values from -6 to 6
- cont_x: bfloat16 [16, 8, 128, 1536], P('grp', 'seq'), may hold values from -6 to 6
- cont_len: int32 [16, 8], P('grp', 'seq'), may hold values from 1 to 128, 768 in all within a row
- prompt_cot: bfloat16 [16, 1024, 1536], P('grp', 'seq'), may hold values from -6 to 6
- cont_cot: bfloat16 [16, 8, 128, 1536], P('grp', 'seq'), may hold values from -6 to 6
- norm1_gain: float32 [1536], P(('grp', 'seq')), may hold values from 0.5 to 1.5
- q_weight: float32 [1536, 768], P(('grp', 'seq')), may hold values from -0.078125 to 0.078125
- k_weight: float32 [1536, 768], P(('grp', 'seq')), may hold values from -0.078125 to 0.078125
- v_weight: float32 [1536, 768], P(('grp', 'seq')), may hold values from -0.15625 to 0.15625
- o_weight: float32 [1536, 768], P(('grp', 'seq')), may hold values from -0.875 to 0.875
- bucket_table: float32 [32, 12], replicated, may hold values from -4 to 4
- norm2_gain: float32 [1536], P(('grp', 'seq')), may hold values from 0.5 to 1.5
- gate_weight: float32 [1536, 3968], P(('grp', 'seq')), may hold values from -0.15625 to 0.15625
- up_weight: float32 [1536, 3968], P(('grp', 'seq')), may hold values from -0.15625 to 0.15625
- down_weight: float32 [1536, 3968], P(('grp', 'seq')), may hold values from -0.125 to 0.125
Outputs:
- prompt_out: bfloat16 [16, 1024, 1536], P('grp', 'seq')
- cont_out: bfloat16 [16, 8, 128, 1536], P('grp', 'seq')
- prompt_grad: bfloat16 [16, 1024, 1536], P('grp', 'seq')
- cont_grad: bfloat16 [16, 8, 128, 1536], P('grp', 'seq')
- norm1_grad: float32 [1536], P(('grp', 'seq'))
- q_grad: float32 [1536, 768], P(('grp', 'seq'))
- k_grad: float32 [1536, 768], P(('grp', 'seq'))
- v_grad: float32 [1536, 768], P(('grp', 'seq'))
- o_grad: float32 [1536, 768], P(('grp', 'seq'))
- table_grad: float32 [32, 12], replicated
- norm2_grad: float32 [1536], P(('grp', 'seq'))
- gate_grad: float32 [1536, 3968], P(('grp', 'seq'))
- up_grad: float32 [1536, 3968], P(('grp', 'seq'))
- down_grad: float32 [1536, 3968], P(('grp', 'seq'))
Inputs may be any that keep to these rules, and one draw needn't show every extreme that they name: `cont_len`: live bytes of continuation c of group g; keys of the continuation at places at or past this length are not attended to. In each group the lengths sum to 768 and one of them equals 128.
All inputs are finite; a program needn't handle non-finite values.
Results may differ from a plain program's by a relative error of at most 0.018.
The roundings to bfloat16 on the way count: a program that leaves them out, or rounds other values in their place, can miss the bound.
Values may be sent and summed in bfloat16 or wider, within the bound.
A program may use at most 512 MiB of HBM per device.

v0:
```python
import jax
import jax.numpy as jnp
from jax import lax
from jax.sharding import PartitionSpec as P

EPS = 1e-06
HIGH = lax.Precision.HIGHEST
LIMITS = (8, 12, 16, 23, 32, 46, 64, 91)
NEGATIVE = -1e30


def bucket_ids(relative):
    distance = jnp.abs(relative)
    coarse = 7 + sum(((distance >= boundary).astype(jnp.int32) for boundary in LIMITS))
    return jnp.where(distance < 8, distance, coarse) + 16 * (relative > 0).astype(jnp.int32)


def rms_scale(values):
    return lax.rsqrt(jnp.mean(values * values, axis=-1, keepdims=True) + EPS)


def matmul(left, right):
    return jnp.dot(left, right, preferred_element_type=jnp.float32)


def matmul_nt(left, right):
    return lax.dot_general(
        left, right, (((1,), (1,)), ((), ())), preferred_element_type=jnp.float32
    )


def matmul_tn(left, right):
    return lax.dot_general(
        left, right, (((0,), (0,)), ((), ())), preferred_element_type=jnp.float32
    )


def gated_gelu(gate_pre, up_pre):
    return jax.nn.gelu(gate_pre, approximate=True) * up_pre


def norm_back(d_normed, unit, scale, gain):
    d_unit = d_normed * gain
    return scale * (d_unit - unit * jnp.mean(d_unit * unit, axis=-1, keepdims=True))


def lane_count(local_shard):
    entries = local_shard.size
    return 128


def flatten(values, lane_width):
    return values.reshape(values.size // lane_width, lane_width)


def unflat(values, columns):
    return values.reshape(values.size // columns, columns)


def masked_logits(queries, key_rows, position_bias, allowed):
    head_count = position_bias.shape[0]
    q_heads = queries.reshape(queries.shape[0], head_count, -1)
    k_heads = key_rows.reshape(key_rows.shape[0], head_count, -1)
    scores = jnp.einsum("qhe,khe->hqk", q_heads, k_heads, preferred_element_type=jnp.float32)
    return jnp.where(allowed[None], scores + position_bias, NEGATIVE)


def body(
    prompt_x,
    cont_x,
    cont_len,
    prompt_cot,
    cont_cot,
    norm1_gain,
    q_weight,
    k_weight,
    v_weight,
    o_weight,
    bucket_table,
    norm2_gain,
    gate_weight,
    up_weight,
    down_weight,
):
    groups, local_prompt, model_width = prompt_x.shape
    local_conts, cont_rows = (cont_x.shape[1], cont_x.shape[2])
    head_count = bucket_table.shape[1]
    num_buckets = bucket_table.shape[0]
    inner_width = q_weight.shape[1]
    inner_lanes = lane_count(q_weight)
    total_prompt = local_prompt * lax.axis_size("seq")
    group_rows = local_prompt + local_conts * cont_rows
    key_count = total_prompt + local_conts * cont_rows
    all_rows = groups * group_rows
    seq_index = lax.axis_index("seq")

    def attn_pack():
        return (
            norm1_gain.astype(jnp.bfloat16),
            norm2_gain.astype(jnp.bfloat16),
            flatten(q_weight.astype(jnp.bfloat16), inner_lanes),
            flatten(k_weight.astype(jnp.bfloat16), inner_lanes),
            flatten(v_weight.astype(jnp.bfloat16), inner_lanes),
            flatten(o_weight.astype(jnp.bfloat16), inner_lanes),
        )

    def attn_unpack(parts):
        return (
            parts[0],
            parts[1],
            unflat(parts[2], inner_width),
            unflat(parts[3], inner_width),
            unflat(parts[4], inner_width),
            unflat(parts[5], inner_width),
        )

    rows_in = jnp.concatenate(
        [prompt_x, cont_x.reshape(groups, local_conts * cont_rows, model_width)], axis=1
    ).reshape(all_rows, model_width)
    cot_rows = jnp.concatenate(
        [prompt_cot, cont_cot.reshape(groups, local_conts * cont_rows, model_width)], axis=1
    ).reshape(all_rows, model_width)
    cont_place = jnp.tile(jnp.arange(cont_rows, dtype=jnp.int32), local_conts)
    cont_owner = jnp.repeat(jnp.arange(local_conts, dtype=jnp.int32), cont_rows)
    query_pos = jnp.concatenate(
        [
            seq_index * local_prompt + jnp.arange(local_prompt, dtype=jnp.int32),
            total_prompt + cont_place,
        ]
    )
    key_pos = jnp.concatenate(
        [jnp.arange(total_prompt, dtype=jnp.int32), total_prompt + cont_place]
    )
    query_owner = jnp.concatenate([jnp.full((local_prompt,), -1, jnp.int32), cont_owner])
    key_owner = jnp.concatenate([jnp.full((total_prompt,), -1, jnp.int32), cont_owner])
    same_owner = (key_owner[None, :] < 0) | (key_owner[None, :] == query_owner[:, None])
    live_conts = cont_place[None, :] < jnp.repeat(cont_len, cont_rows, axis=1)
    key_live = jnp.concatenate([jnp.ones((groups, total_prompt), jnp.bool_), live_conts], axis=1)
    relative = key_pos[None, :] - query_pos[:, None]
    one_hot = (bucket_ids(relative)[:, :, None] == jnp.arange(num_buckets, dtype=jnp.int32)).astype(
        jnp.float32
    )
    position_bias = jnp.einsum("qkb,bh->hqk", one_hot, bucket_table, precision=HIGH)
    attn_parts = attn_pack()
    gain_one, gain_two, q_full, k_full, v_full, o_full = attn_unpack(
        (
            lax.all_gather(attn_parts[0], ("grp", "seq"), axis=0, tiled=True),
            lax.all_gather(attn_parts[1], ("grp", "seq"), axis=0, tiled=True),
            lax.all_gather(attn_parts[2], ("grp", "seq"), axis=0, tiled=True),
            lax.all_gather(attn_parts[3], ("grp", "seq"), axis=0, tiled=True),
            lax.all_gather(attn_parts[4], ("grp", "seq"), axis=0, tiled=True),
            lax.all_gather(attn_parts[5], ("grp", "seq"), axis=0, tiled=True),
        )
    )
    input_float = rows_in.astype(jnp.float32)
    scale_one = rms_scale(input_float)
    unit_one = input_float * scale_one
    normed_one = (unit_one * gain_one.astype(jnp.float32)).astype(jnp.bfloat16)
    queries = matmul(normed_one, q_full).astype(jnp.bfloat16).reshape(groups, group_rows, -1)
    key_local = matmul(normed_one, k_full).astype(jnp.bfloat16).reshape(groups, group_rows, -1)
    value_local = matmul(normed_one, v_full).astype(jnp.bfloat16).reshape(groups, group_rows, -1)
    prompt_keys, prompt_values = (
        lax.all_gather(key_local[:, :local_prompt], "seq", axis=1, tiled=True),
        lax.all_gather(value_local[:, :local_prompt], "seq", axis=1, tiled=True),
    )
    key_rows = jnp.concatenate([prompt_keys, key_local[:, local_prompt:]], axis=1)
    value_rows = jnp.concatenate([prompt_values, value_local[:, local_prompt:]], axis=1)

    def attend_forward(inputs):
        group_q, group_k, group_v, group_live = inputs
        logits = masked_logits(group_q, group_k, position_bias, same_owner & group_live[None, :])
        row_max = jnp.max(logits, axis=-1, keepdims=True)
        exponent = jnp.exp(logits - row_max)
        row_sum = jnp.sum(exponent, axis=-1, keepdims=True)
        prob_low = (exponent / row_sum).astype(jnp.bfloat16)
        v_heads = group_v.reshape(key_count, head_count, -1)
        mixture = jnp.einsum("hqk,khe->qhe", prob_low, v_heads, preferred_element_type=jnp.float32)
        return (mixture.reshape(group_rows, -1).astype(jnp.bfloat16), row_max + jnp.log(row_sum))

    attended, log_norm = lax.map(attend_forward, (queries, key_rows, value_rows, key_live))
    attended_flat = attended.reshape(all_rows, -1)
    middle = input_float + matmul_nt(attended_flat, o_full)
    scale_two = rms_scale(middle)
    unit_two = middle * scale_two
    normed_two = (unit_two * gain_two.astype(jnp.float32)).astype(jnp.bfloat16)
    column_parts = (
        lax.all_to_all(
            gate_weight.astype(jnp.bfloat16), "seq", split_axis=1, concat_axis=0, tiled=True
        ),
        lax.all_to_all(
            up_weight.astype(jnp.bfloat16), "seq", split_axis=1, concat_axis=0, tiled=True
        ),
        lax.all_to_all(
            down_weight.astype(jnp.bfloat16), "seq", split_axis=1, concat_axis=0, tiled=True
        ),
    )
    gate_cols, up_cols, down_cols = (
        lax.all_gather(column_parts[0], "grp", axis=0, tiled=True),
        lax.all_gather(column_parts[1], "grp", axis=0, tiled=True),
        lax.all_gather(column_parts[2], "grp", axis=0, tiled=True),
    )
    normed_group, cot_group = (
        lax.all_gather(normed_two, "seq", axis=0, tiled=True),
        lax.all_gather(cot_rows, "seq", axis=0, tiled=True),
    )
    gate_pre = matmul(normed_group, gate_cols)
    up_pre = matmul(normed_group, up_cols)
    hidden = gated_gelu(gate_pre, up_pre).astype(jnp.bfloat16)
    final_float = middle + lax.psum_scatter(
        matmul_nt(hidden, down_cols).astype(jnp.bfloat16), "seq", scatter_dimension=0, tiled=True
    ).astype(jnp.float32)
    final = final_float.astype(jnp.bfloat16).reshape(groups, group_rows, model_width)
    prompt_out = final[:, :local_prompt]
    cont_out = final[:, local_prompt:].reshape(groups, local_conts, cont_rows, model_width)
    attn_parts_back = attn_pack()
    gain_first, gain_back, q_back, k_back, v_back, o_back = attn_unpack(
        (
            lax.all_gather(attn_parts_back[0], ("grp", "seq"), axis=0, tiled=True),
            lax.all_gather(attn_parts_back[1], ("grp", "seq"), axis=0, tiled=True),
            lax.all_gather(attn_parts_back[2], ("grp", "seq"), axis=0, tiled=True),
            lax.all_gather(attn_parts_back[3], ("grp", "seq"), axis=0, tiled=True),
            lax.all_gather(attn_parts_back[4], ("grp", "seq"), axis=0, tiled=True),
            lax.all_gather(attn_parts_back[5], ("grp", "seq"), axis=0, tiled=True),
        )
    )
    d_hidden = matmul(cot_group, down_cols)
    d_down = matmul_tn(cot_group, hidden)
    _, pullback = jax.vjp(gated_gelu, gate_pre, up_pre)
    d_gate, d_up = pullback(d_hidden)
    d_gate = d_gate.astype(jnp.bfloat16)
    d_up = d_up.astype(jnp.bfloat16)
    d_normed_part = matmul_nt(d_gate, gate_cols) + matmul_nt(d_up, up_cols)
    d_normed_two = lax.psum_scatter(
        d_normed_part.astype(jnp.bfloat16), "seq", scatter_dimension=0, tiled=True
    ).astype(jnp.float32)
    d_gate_w = matmul_tn(normed_group, d_gate)
    d_up_w = matmul_tn(normed_group, d_up)
    column_sums = (
        lax.psum_scatter(
            d_gate_w.astype(jnp.bfloat16), "grp", scatter_dimension=0, tiled=True
        ).astype(jnp.float32),
        lax.psum_scatter(
            d_up_w.astype(jnp.bfloat16), "grp", scatter_dimension=0, tiled=True
        ).astype(jnp.float32),
        lax.psum_scatter(
            d_down.astype(jnp.bfloat16), "grp", scatter_dimension=0, tiled=True
        ).astype(jnp.float32),
    )
    gate_grad, up_grad, down_grad = (
        lax.all_to_all(
            column_sums[0].astype(jnp.bfloat16), "seq", split_axis=0, concat_axis=1, tiled=True
        ).astype(jnp.float32),
        lax.all_to_all(
            column_sums[1].astype(jnp.bfloat16), "seq", split_axis=0, concat_axis=1, tiled=True
        ).astype(jnp.float32),
        lax.all_to_all(
            column_sums[2].astype(jnp.bfloat16), "seq", split_axis=0, concat_axis=1, tiled=True
        ).astype(jnp.float32),
    )
    d_gain_two = jnp.sum(d_normed_two * unit_two, axis=0)
    d_middle = cot_rows.astype(jnp.float32) + norm_back(
        d_normed_two, unit_two, scale_two, gain_back.astype(jnp.float32)
    )
    d_branch = d_middle.astype(jnp.bfloat16)
    d_attended = matmul(d_branch, o_back).astype(jnp.bfloat16).reshape(groups, group_rows, -1)
    d_out_weight = matmul_tn(d_branch, attended_flat)

    def attend_back(score_total, inputs):
        group_q, group_k, group_v, group_live, group_norm, group_grad = inputs
        logits = masked_logits(group_q, group_k, position_bias, same_owner & group_live[None, :])
        probs = jnp.exp(logits - group_norm)
        prob_low = probs.astype(jnp.bfloat16)
        d_heads = group_grad.reshape(group_rows, head_count, -1)
        q_heads = group_q.reshape(group_rows, head_count, -1)
        k_heads = group_k.reshape(key_count, head_count, -1)
        v_heads = group_v.reshape(key_count, head_count, -1)
        d_value = jnp.einsum("hqk,qhe->khe", prob_low, d_heads, preferred_element_type=jnp.float32)
        d_probs = jnp.einsum("qhe,khe->hqk", d_heads, v_heads, preferred_element_type=jnp.float32)
        d_scores = probs * (d_probs - jnp.sum(probs * d_probs, axis=-1, keepdims=True))
        score_low = d_scores.astype(jnp.bfloat16)
        d_query = jnp.einsum("hqk,khe->qhe", score_low, k_heads, preferred_element_type=jnp.float32)
        d_key = jnp.einsum("hqk,qhe->khe", score_low, q_heads, preferred_element_type=jnp.float32)
        return (
            score_total + d_scores,
            (
                d_query.reshape(group_rows, -1),
                d_key.reshape(key_count, -1),
                d_value.reshape(key_count, -1),
            ),
        )

    score_start = jnp.zeros((head_count, group_rows, key_count), jnp.float32)
    score_sum, (d_queries, d_keys, d_values) = lax.scan(
        attend_back, score_start, (queries, key_rows, value_rows, key_live, log_norm, d_attended)
    )
    d_table = jnp.einsum("hqk,qkb->bh", score_sum, one_hot, precision=HIGH)
    prompt_dkey, prompt_dvalue = (
        lax.psum_scatter(
            d_keys[:, :total_prompt].astype(jnp.bfloat16), "seq", scatter_dimension=1, tiled=True
        ).astype(jnp.float32),
        lax.psum_scatter(
            d_values[:, :total_prompt].astype(jnp.bfloat16), "seq", scatter_dimension=1, tiled=True
        ).astype(jnp.float32),
    )
    d_key_low = (
        jnp.concatenate([prompt_dkey, d_keys[:, total_prompt:]], axis=1)
        .astype(jnp.bfloat16)
        .reshape(all_rows, -1)
    )
    d_value_low = (
        jnp.concatenate([prompt_dvalue, d_values[:, total_prompt:]], axis=1)
        .astype(jnp.bfloat16)
        .reshape(all_rows, -1)
    )
    d_query_low = d_queries.astype(jnp.bfloat16).reshape(all_rows, -1)
    d_normed_one = (
        matmul_nt(d_query_low, q_back)
        + matmul_nt(d_key_low, k_back)
        + matmul_nt(d_value_low, v_back)
    )
    d_q_weight = matmul_tn(normed_one, d_query_low)
    d_k_weight = matmul_tn(normed_one, d_key_low)
    d_v_weight = matmul_tn(normed_one, d_value_low)
    d_gain_one = jnp.sum(d_normed_one * unit_one, axis=0)
    d_input = d_middle + norm_back(
        d_normed_one, unit_one, scale_one, gain_first.astype(jnp.float32)
    )
    d_input = d_input.astype(jnp.bfloat16).reshape(groups, group_rows, model_width)
    prompt_grad = d_input[:, :local_prompt]
    cont_grad = d_input[:, local_prompt:].reshape(groups, local_conts, cont_rows, model_width)
    summed = (
        lax.psum_scatter(d_gain_one, ("grp", "seq"), scatter_dimension=0, tiled=True),
        lax.psum_scatter(d_gain_two, ("grp", "seq"), scatter_dimension=0, tiled=True),
        lax.psum_scatter(
            flatten(d_q_weight, inner_lanes), ("grp", "seq"), scatter_dimension=0, tiled=True
        ),
        lax.psum_scatter(
            flatten(d_k_weight, inner_lanes), ("grp", "seq"), scatter_dimension=0, tiled=True
        ),
        lax.psum_scatter(
            flatten(d_v_weight, inner_lanes), ("grp", "seq"), scatter_dimension=0, tiled=True
        ),
        lax.psum_scatter(
            flatten(d_out_weight, inner_lanes), ("grp", "seq"), scatter_dimension=0, tiled=True
        ),
    )
    norm1_grad, norm2_grad, q_grad, k_grad, v_grad, o_grad = attn_unpack(summed)
    table_grad = lax.psum(d_table, ("grp", "seq"))
    return (
        prompt_out,
        cont_out,
        prompt_grad,
        cont_grad,
        norm1_grad,
        q_grad,
        k_grad,
        v_grad,
        o_grad,
        table_grad,
        norm2_grad,
        gate_grad,
        up_grad,
        down_grad,
    )


def solution(mesh):
    in_specs = (
        P("grp", "seq", None),
        P("grp", "seq", None, None),
        P("grp", "seq"),
        P("grp", "seq", None),
        P("grp", "seq", None, None),
        P(("grp", "seq")),
        P(("grp", "seq"), None),
        P(("grp", "seq"), None),
        P(("grp", "seq"), None),
        P(("grp", "seq"), None),
        P(),
        P(("grp", "seq")),
        P(("grp", "seq"), None),
        P(("grp", "seq"), None),
        P(("grp", "seq"), None),
    )
    out_specs = (
        P("grp", "seq", None),
        P("grp", "seq", None, None),
        P("grp", "seq", None),
        P("grp", "seq", None, None),
        P(("grp", "seq")),
        P(("grp", "seq"), None),
        P(("grp", "seq"), None),
        P(("grp", "seq"), None),
        P(("grp", "seq"), None),
        P(),
        P(("grp", "seq")),
        P(("grp", "seq"), None),
        P(("grp", "seq"), None),
        P(("grp", "seq"), None),
    )
    return jax.shard_map(body, mesh=mesh, in_specs=in_specs, out_specs=out_specs, check_vma=False)
```

profile of v0, /device:TPU:0, one launch (start us, length us, event | category | flops | bytes accessed | tf_op | source)
XLA Modules:
  0.0 1847.8 jit_solution(1282213986116333848)
XLA Ops:
  25.6 42.1 %all-reduce.8 = (bf16[1536]{0:T(1024)(128)(2,1)}, bf16[1536]{0:T(1024)(128)(2,1)}) all-reduce(bf16[1536]{0:T(1024)(128)(2,1)S(1)} %dynamic-update-slice, bf16[1536]{0:T(1024)(128)(2,1)S(1)} %dynamic-update-slice.1), channel_id=1, replica_groups=mesh['grp'=16,'seq'=2] {'grp','seq'}, use_global_device_ids=true, to_apply=%add.3 | all-reduce | flops 3072 | bytes 12288
  91.8 39.2 %all-gather.19.cloned.1.call-done = bf16[9216,128]{1,0:T(8,128)(2,1)} async-done(((bf16[288,128]{1,0:T(8,128)(2,1)}), bf16[9216,128]{1,0:T(8,128)(2,1)}) %all-gather.19.cloned.1.call-update) | async-done | bytes 2359312 | tf_op jit(solution)/shard_map/all_gather | solution.py:150
  142.3 90.9 %fusion.1 = f32[1024,1536,12]{0,2,1:T(8,128)} fusion(s32[1024,1536]{0,1:T(8,128)} %fusion.48, f32[32,12]{0,1:T(8,128)S(1)} %copy-done), kind=kOutput, calls=%fused_computation.2 | convolution fusion | flops 7298088960 | bytes 81790464 | tf_op jit(solution)/shard_map/qkb,bh->hqk/dot_general | solution.py:143
  235.0 89.4 %copy.59 = f32[1024,1536,12]{1,0,2:T(8,128)} copy(f32[1024,1536,12]{0,2,1:T(8,128)} %fusion.1) | data formatting | bytes 150994944 | tf_op jit(solution)/shard_map/qkb,bh->hqk/dot_general | solution.py:143
  358.3 49.3 %fusion.86 = (f32[12,1024]{1,0:T(8,128)S(1)}, f32[12,1024,1536]{2,1,0:T(8,128)}) fusion(f32[1024,1536,12]{1,0,2:T(8,128)} %copy.59, bf16[1024,12,64]{0,2,1:T(8,128)(2,1)S(1)} %bitcast.152, bf16[1536,12,64]{0,2,1:T(8,128)(2,1)} %bitcast.144, pred[1024,1536]{1,0:T(8,128)(4,1)S(1)} %or_and_fusion), kind=kOutput, calls=%fused_computation.137 | convolution fusion | flops 2472529920 | bytes 156549120 | tf_op jit(solution)/shard_map/while/body/eval_jaxpr/qhe,khe->hqk/dot_general | solution.py:64
  432.0 27.5 %fusion.63 = bf16[12,64,1024]{2,1,0:T(8,128)(2,1)} fusion(bf16[1536,12,64]{0,2,1:T(8,128)(2,1)S(1)} %bitcast.150, f32[12,1024,1536]{2,1,0:T(8,128)} %get-tuple-element.103, f32[12,1024]{1,0:T(8,128)S(1)} %fusion.5, f32[12,1024]{1,0:T(8,128)S(1)} %get-tuple-element.102), kind=kOutput, calls=%fused_computation.95 | convolution fusion | flops 2473328640 | bytes 79527936 | tf_op jit(solution)/shard_map/while/body/eval_jaxpr/hqk,khe->qhe/dot_general | solution.py:177
  505.1 50.9 %all-gather.25.cloned.1.call-done = bf16[2048,1536]{1,0:T(8,128)(2,1)} async-done(((bf16[1024,1536]{1,0:T(8,128)(2,1)}), bf16[2048,1536]{1,0:T(8,128)(2,1)}) %all-gather.25.cloned.1.call-update) | async-done | bytes 6291472 | tf_op jit(solution)/shard_map/all_gather | solution.py:203
  576.1 42.8 %all-gather.29.cloned.1.call-done = bf16[1536,1984]{1,0:T(8,128)(2,1)} async-done(((bf16[96,1984]{1,0:T(8,128)(2,1)}), bf16[1536,1984]{1,0:T(8,128)(2,1)}) %all-gather.29.cloned.1.call-update) | async-done | bytes 6094864 | tf_op jit(solution)/shard_map/all_gather | solution.py:199
  639.1 60.2 %all-gather.33.cloned.1.call-done = bf16[1,2048,1536]{2,1,0:T(8,128)(2,1)} async-done(((bf16[1,1024,1536]{2,1,0:T(8,128)(2,1)}), bf16[1,2048,1536]{2,1,0:T(8,128)(2,1)}) %all-gather.33.cloned.1.call-update) | async-done | bytes 6291472 | tf_op jit(solution)/shard_map/all_gather | solution.py:204
  699.3 63.7 %all-gather.31.cloned.1.call-done = bf16[1536,1984]{1,0:T(8,128)(2,1)} async-done(((bf16[96,1984]{1,0:T(8,128)(2,1)}), bf16[1536,1984]{1,0:T(8,128)(2,1)}) %all-gather.31.cloned.1.call-update) | async-done | bytes 6094864 | tf_op jit(solution)/shard_map/all_gather | solution.py:200
  763.1 36.1 %multiply_convert_fusion = (bf16[2048,1984]{0,1:T(8,128)(2,1)}, bf16[2048,1984]{0,1:T(8,128)(2,1)}, bf16[2048,1984]{0,1:T(8,128)(2,1)}) fusion(f32[2048,1984]{0,1:T(8,128)} %fusion.87, f32[2048,1984]{0,1:T(8,128)} %fusion.88, bf16[1536,1984]{1,0:T(8,128)(2,1)} %all-gather.31.cloned.1.call-done, bf16[1,2048,1536]{2,1,0:T(8,128)(2,1)} %all-gather.33.cloned.1.call-done), kind=kOutput, calls=%fused_computation.31 | convolution fusion | flops 12587892736 | bytes 69271552 | tf_op jit(solution)/shard_map/dot_general | solution.py:23
  877.8 36.7 %reduce-scatter.14.cloned.1.call-done = bf16[1024,1536]{1,0:T(8,128)(2,1)} async-done(((bf16[2048,1536]{1,0:T(8,128)(2,1)}), bf16[1024,1536]{1,0:T(8,128)(2,1)}) %reduce-scatter.14.cloned.1.call-update) | async-done | bytes 3145744 | tf_op jit(solution)/shard_map/reduce_scatter | solution.py:233
  920.2 73.7 %reduce-scatter.12.cloned.1.call-done = bf16[1024,1536]{1,0:T(8,128)(2,1)} async-done(((bf16[2048,1536]{1,0:T(8,128)(2,1)}), bf16[1024,1536]{1,0:T(8,128)(2,1)}) %reduce-scatter.12.cloned.1.call-update) | async-done | bytes 3145744 | tf_op jit(solution)/shard_map/reduce_scatter | solution.py:209
  1007.0 53.1 %multiply_reduce_fusion = (f32[12,1024]{1,0:T(8,128)S(1)}, f32[12,1024,1536]{2,1,0:T(8,128)}) fusion(f32[12,1024,1536]{2,1,0:T(8,128)} %get-tuple-element.103, f32[12,1024]{1,0:T(8,128)S(1)} %log_add_fusion, bf16[1024,12,64]{0,2,1:T(8,128)(2,1)} %bitcast.154, bf16[1536,12,64]{0,2,1:T(8,128)(2,1)S(1)} %bitcast.151), kind=kOutput, calls=%fused_computation.8 | convolution fusion | flops 2472529920 | bytes 155025408 | tf_op jit(solution)/shard_map/while/body/eval_jaxpr/qhe,khe->hqk/dot_general | solution.py:278
  1060.1 72.1 %subtract_multiply_fusion = f32[12,1024,1536]{2,1,0:T(8,128)} fusion(f32[12,1024,1536]{2,1,0:T(8,128)} %get-tuple-element.107, f32[12,1024,1536]{2,1,0:T(8,128)} %get-tuple-element.103, f32[12,1024]{1,0:T(8,128)S(1)} %get-tuple-element.106, f32[12,1024]{1,0:T(8,128)S(1)} %log_add_fusion), kind=kLoop, calls=%fused_computation.7 | loop fusion | flops 56623104 | bytes 226590720 | tf_op jit(solution)/shard_map/while/body/eval_jaxpr/mul | solution.py:279
  1132.2 24.9 %fusion.52 = bf16[12,64,1536]{2,1,0:T(8,128)(2,1)S(1)} fusion(bf16[1024,12,64]{0,2,1:T(8,128)(2,1)} %bitcast.153, f32[12,1024,1536]{2,1,0:T(8,128)} %subtract_multiply_fusion), kind=kOutput, calls=%fused_computation.82 | convolution fusion | flops 2435973120 | bytes 79429632 | tf_op jit(solution)/shard_map/while/body/eval_jaxpr/hqk,qhe->khe/dot_general | solution.py:282
  1198.9 30.6 %fusion.55 = bf16[12,64,1536]{2,1,0:T(8,128)(2,1)} fusion(bf16[1024,12,64]{0,2,1:T(8,128)(2,1)S(1)} %bitcast.155, f32[12,1024,1536]{2,1,0:T(8,128)} %get-tuple-element.103, f32[12,1024]{1,0:T(8,128)S(1)} %log_add_fusion), kind=kOutput, calls=%fused_computation.83 | convolution fusion | flops 2454847488 | bytes 79478784 | tf_op jit(solution)/shard_map/while/body/eval_jaxpr/hqk,qhe->khe/dot_general | solution.py:277
  1232.4 27.8 %fusion.60 = bf16[12,64,1024]{2,1,0:T(8,128)(2,1)} fusion(bf16[1536,12,64]{0,2,1:T(8,128)(2,1)S(1)} %bitcast.145, f32[12,1024,1536]{2,1,0:T(8,128)} %subtract_multiply_fusion), kind=kOutput, calls=%fused_computation.90 | convolution fusion | flops 2435579904 | bytes 79429632 | tf_op jit(solution)/shard_map/while/body/eval_jaxpr/hqk,khe->qhe/dot_general | solution.py:281
  1306.2 32.2 %iota_compare_fusion.10 = pred[1024,1536,32]{0,2,1:T(32,128)(4,1)} fusion(s32[1024,1536]{0,1:T(8,128)} %fusion.48), kind=kLoop, calls=%fused_computation.clone.clone.clone.clone.1 | loop fusion | flops 50331648 | bytes 56623104 | tf_op jit(solution)/shard_map/hqk,qkb->bh/dot_general | solution.py:296
  1383.0 86.9 %copy.63 = f32[12,1024,1536]{1,0,2:T(8,128)} copy(f32[12,1024,1536]{2,1,0:T(8,128)} %subtract_multiply_fusion) | data formatting | bytes 150994944 | tf_op jit(solution)/shard_map/while/body/eval_jaxpr/mul | solution.py:279
  1491.8 97.8 %fusion.69 = f32[32,12]{0,1:T(8,128)S(1)} fusion(f32[12,1024,1536]{1,0,2:T(8,128)} %copy.63, pred[1024,1536,32]{0,2,1:T(32,128)(4,1)} %iota_compare_fusion.10), kind=kOutput, calls=%fused_computation.103 | convolution fusion | flops 7247757312 | bytes 125830656 | tf_op jit(solution)/shard_map/hqk,qkb->bh/dot_general | solution.py:296
  1604.2 40.5 %all-reduce.7 = (f32[1536]{0:T(1024)S(1)}, f32[32,12]{0,1:T(8,128)}, f32[1536]{0:T(1024)S(1)}) all-reduce(f32[1536]{0:T(1024)S(1)} %get-tuple-element.69, f32[32,12]{0,1:T(8,128)S(1)} %fusion.69, f32[1536]{0:T(1024)S(1)} %copy-done.32), channel_id=7, replica_groups=mesh['grp'=16,'seq'=2] {'grp','seq'}, use_global_device_ids=true, to_apply=%region_12.13.clone | all-reduce | flops 3456 | bytes 27648
  1658.4 68.9 %reduce-scatter.22.cloned.1.call-done = f32[288,128]{1,0:T(8,128)} async-done(((f32[9216,128]{1,0:T(8,128)}), f32[288,128]{1,0:T(8,128)}) %reduce-scatter.22.cloned.1.call-update) | async-done | bytes 147472 | tf_op jit(solution)/shard_map/reduce_scatter | solution.py:337
  1728.9 110.3 %reduce-scatter.24.cloned.1.call-done = f32[288,128]{1,0:T(8,128)} async-done(((f32[9216,128]{1,0:T(8,128)}), f32[288,128]{1,0:T(8,128)}) %reduce-scatter.24.cloned.1.call-update) | async-done | bytes 147472 | tf_op jit(solution)/shard_map/reduce_scatter | solution.py:340
  (254 shorter events, 484.8 us)
Async XLA Ops:
  7.2 64.4 %all-gather.13.cloned.1.call-start = ((), (), s32[]{:S(2)}) async-start(), calls=%async_computation.17 | async-start | bytes 2433024 | tf_op jit(solution)/shard_map/all_gather | solution.py:151
  9.1 121.9 %all-gather.19.cloned.1.call-start = ((), (), s32[]{:S(2)}) async-start(), calls=%async_computation.20 | async-start | bytes 2433024 | tf_op jit(solution)/shard_map/all_gather | solution.py:150
  10.8 315.4 %all-gather.17.cloned.1.call-start = ((), (), s32[]{:S(2)}) async-start(), calls=%async_computation.19 | async-start | bytes 2433024 | tf_op jit(solution)/shard_map/all_gather | solution.py:149
  12.5 324.9 %all-gather.23.cloned.1.call-start = ((), (), s32[]{:S(2)}) async-start(), calls=%async_computation.22 | async-start | bytes 2433024 | tf_op jit(solution)/shard_map/all_gather | solution.py:152
  18.5 306.5 %all-to-all-start = ((bf16[48,2,1984]{2,0,1:T(8,128)(2,1)}), bf16[48,2,1984]{2,0,1:T(8,128)(2,1)S(1)}, u32[]{:S(2)}, u32[]{:S(2)}) async-start(bf16[48,2,1984]{2,0,1:T(8,128)(2,1)} %copy.60), calls=%async_computation | async-start | bytes 786432 | tf_op jit(solution)/shard_map/all_to_all | solution.py:187
  22.7 320.5 %all-gather.15.cloned.1.call-start = ((), (), s32[]{:S(2)}) async-start(), calls=%async_computation.18 | async-start | bytes 2359296 | tf_op jit(solution)/shard_map/all_gather | solution.py:164
  82.5 268.1 %all-gather.21.cloned.1.call-start = ((), (), s32[]{:S(2)}) async-start(), calls=%async_computation.21 | async-start | bytes 2359296 | tf_op jit(solution)/shard_map/all_gather | solution.py:163
  142.0 363.1 %all-gather.27.cloned.1.call-start = ((), (), s32[]{:S(2)}) async-start(), calls=%async_computation.24 | async-start | bytes 6684672 | tf_op jit(solution)/shard_map/all_gather | solution.py:198
  325.7 230.4 %all-gather.25.cloned.1.call-start = ((), (), s32[]{:S(2)}) async-start(), calls=%async_computation.23 | async-start | bytes 9437184 | tf_op jit(solution)/shard_map/all_gather | solution.py:203
  470.4 148.5 %all-gather.29.cloned.1.call-start = ((), (), s32[]{:S(2)}) async-start(), calls=%async_computation.25 | async-start | bytes 6684672 | tf_op jit(solution)/shard_map/all_gather | solution.py:199
  487.0 212.4 %all-gather.33.cloned.1.call-start = ((), (), s32[]{:S(2)}) async-start(), calls=%async_computation.38 | async-start | bytes 9437184 | tf_op jit(solution)/shard_map/all_gather | solution.py:204
  488.9 274.2 %all-gather.31.cloned.1.call-start = ((), (), s32[]{:S(2)}) async-start(), calls=%async_computation.26 | async-start | bytes 6684672 | tf_op jit(solution)/shard_map/all_gather | solution.py:200
  505.1 409.4 %reduce-scatter.14.cloned.1.call-start = ((), (), s32[]{:S(2)}) async-start(), calls=%async_computation.28 | async-start | bytes 9437184 | tf_op jit(solution)/shard_map/reduce_scatter | solution.py:233
  838.5 155.5 %reduce-scatter.12.cloned.1.call-start = ((), (), s32[]{:S(2)}) async-start(), calls=%async_computation.27 | async-start | bytes 9437184 | tf_op jit(solution)/shard_map/reduce_scatter | solution.py:209
  857.8 430.0 %reduce-scatter.28.cloned.1.call-start = ((), (), s32[]{:S(2)}) async-start(), calls=%async_computation.35 | async-start | bytes 6684672 | tf_op jit(solution)/shard_map/reduce_scatter | solution.py:239
  877.7 416.2 %reduce-scatter.16.cloned.1.call-start = ((), (), s32[]{:S(2)}) async-start(), calls=%async_computation.29 | async-start | bytes 2359296 | tf_op jit(solution)/shard_map/reduce_scatter | solution.py:298
  1158.7 179.7 %reduce-scatter.30.cloned.1.call-start = ((), (), s32[]{:S(2)}) async-start(), calls=%async_computation.36 | async-start | bytes 6684672 | tf_op jit(solution)/shard_map/reduce_scatter | solution.py:242
  1178.2 183.9 %reduce-scatter.32.cloned.1.call-start = ((), (), s32[]{:S(2)}) async-start(), calls=%async_computation.37 | async-start | bytes 6684672 | tf_op jit(solution)/shard_map/reduce_scatter | solution.py:245
  1197.4 282.2 %reduce-scatter.18.cloned.1.call-start = ((), (), s32[]{:S(2)}) async-start(), calls=%async_computation.30 | async-start | bytes 2359296 | tf_op jit(solution)/shard_map/reduce_scatter | solution.py:301
  1232.4 422.8 %reduce-scatter.20.cloned.1.call-start = ((), (), s32[]{:S(2)}) async-start(), calls=%async_computation.31 | async-start | bytes 4866048 | tf_op jit(solution)/shard_map/reduce_scatter | solution.py:334
  1273.6 383.2 %reduce-scatter.26.cloned.1.call-start = ((), (), s32[]{:S(2)}) async-start(), calls=%async_computation.34 | async-start | bytes 4866048 | tf_op jit(solution)/shard_map/reduce_scatter | solution.py:343
  1287.8 50.7 %all-to-all-start.3 = ((bf16[2,48,1984]{2,1,0:T(8,128)(2,1)}), bf16[2,48,1984]{2,1,0:T(8,128)(2,1)S(1)}, u32[]{:S(2)}, u32[]{:S(2)}) async-start(bf16[2,48,1984]{2,1,0:T(8,128)(2,1)} %bitcast.179), calls=%async_computation.12 | async-start | bytes 786432 | tf_op jit(solution)/shard_map/all_to_all | solution.py:250
  1291.3 435.9 %reduce-scatter.22.cloned.1.call-start = ((), (), s32[]{:S(2)}) async-start(), calls=%async_computation.32 | async-start | bytes 4866048 | tf_op jit(solution)/shard_map/reduce_scatter | solution.py:337
  1365.6 473.6 %reduce-scatter.24.cloned.1.call-start = ((), (), s32[]{:S(2)}) async-start(), calls=%async_computation.33 | async-start | bytes 4866048 | tf_op jit(solution)/shard_map/reduce_scatter | solution.py:340
  (43 other events, 1351.3 us)
Sparse Core Ops, SparseCore 0:
  11.5 60.0 all-gather.12
  75.1 55.8 all-gather.18
  134.5 55.8 all-gather.16
  193.8 55.9 all-gather.22
  251.7 26.0 all-gather.14
  279.8 27.1 all-gather.20
  325.9 60.5 all-gather.26
  470.5 85.5 all-gather.24
  558.4 60.4 all-gather.28
  620.2 79.0 all-gather.32
  701.6 61.3 all-gather.30
  838.6 75.8 reduce-scatter.13
  916.8 77.1 reduce-scatter.11
  997.7 85.0 reduce-scatter.27
  1158.8 26.3 reduce-scatter.15
  1189.0 85.0 reduce-scatter.29
  1277.9 84.1 reduce-scatter.31
  1364.8 25.2 reduce-scatter.17
  1395.5 107.4 reduce-scatter.19
  1508.4 106.6 reduce-scatter.25
  1620.5 106.6 reduce-scatter.21
  1732.7 106.3 reduce-scatter.23
where the time goes:
time: 1860 us; the launch traced here: 1850 us
  matrix products  669 us (36%)
  waiting for transfers between devices  566 us (30%)
  local copies, waits for them, and re-layouts  282 us (15%)
  other arithmetic  189 us (10%)
  blocking collectives  110 us (6%)
    reduce_scatter x1, waiting for transfers between devices, body(): lax.psum_scatter(flatten(d_v_weight, inner_lanes), ('grp', 'seq'), scatte...  110 us
    dot_general x1, matrix products, body(): d_table = jnp.einsum('hqk,qkb->bh', score_sum, one_hot, precision=HIGH)  97.8 us
    dot_general x7, matrix products, matmul(): return jnp.dot(left, right, preferred_element_type=jnp.float32)  94.7 us
    dot_general x1, matrix products, body(): jnp.einsum('qkb,bh->hqk', one_hot, bucket_table, precision=HIGH)  90.9 us
    dot_general x1, local copies, waits for them, and re-layouts, body(): jnp.einsum('qkb,bh->hqk', one_hot, bucket_table, precision=HIGH)  89.4 us
    mul x1, local copies, waits for them, and re-layouts, attend_back(): probs * (d_probs - jnp.sum(probs * d_probs, axis=-1, keepdims=True))  86.9 us
    dot_general x7, matrix products, matmul_nt(): lax.dot_general(left, right, (((1,), (1,)), ((), ())), preferred_element_...  86.5 us
    dot_general x7, matrix products, matmul_tn(): lax.dot_general(left, right, (((0,), (0,)), ((), ())), preferred_element_...  85.7 us
  transfers between devices with their start and end apart: 26, of which 11 were waited for; matrix products, arithmetic and copies ran while one was open for 57% of the time, Pallas kernels for 0%

commit v1 on v0

v1 whole, which is shorter than its diff:
```python
import functools

import jax
import jax.numpy as jnp
from jax import lax
from jax.experimental import pallas as pl
from jax.experimental.pallas import tpu as pltpu
from jax.sharding import PartitionSpec as P

EPS = 1e-06
LIMITS = (8, 12, 16, 23, 32, 46, 64, 91)
NEGATIVE = -1e30
MESH = pl.DeviceIdType.MESH
T = 128
HEAD = 64
BANDS = 5
BF = jnp.bfloat16
F32 = jnp.float32
VMEM_LIMIT = 63 * 2**20
Y = 2
C = 2


def nn(left, right):
    return jnp.dot(left, right, preferred_element_type=F32)


def nt(left, right):
    return lax.dot_general(left, right, (((1,), (1,)), ((), ())), preferred_element_type=F32)


def tn(left, right):
    return lax.dot_general(left, right, (((0,), (0,)), ((), ())), preferred_element_type=F32)


def bucket_ids(relative):
    distance = jnp.abs(relative)
    coarse = 7 + sum(((distance >= boundary).astype(jnp.int32) for boundary in LIMITS))
    return jnp.where(distance < 8, distance, coarse) + 16 * (relative > 0).astype(jnp.int32)


def band_one_hot(num_buckets):
    band = jnp.arange(BANDS)[:, None, None] - 2
    query = jnp.arange(T)[None, :, None]
    key = jnp.arange(T)[None, None, :]
    ids = bucket_ids(band * T + key - query)
    return (ids[..., None] == jnp.arange(num_buckets)).astype(F32)


class Place:
    def __init__(self, zs, xs):
        grp = lax.axis_index("grp")
        self.zs, self.xs = zs, xs
        self.x = lax.axis_index("seq")
        self.z = grp // (Y * C)
        self.y = (grp // C) % Y
        self.c = grp % C

    def device(self, z=None, y=None, c=None, x=None):
        z = self.z if z is None else z
        y = self.y if y is None else y
        c = self.c if c is None else c
        x = self.x if x is None else x
        return (z * (Y * C) + y * C + c, x)

    def peers(self):
        around = [self.device(z=(self.z + d) % self.zs) for d in range(1, self.zs)]
        return around + [
            self.device(y=1 - self.y),
            self.device(x=1 - self.x),
            self.device(c=1 - self.c),
        ]

    def barrier(self):
        sem = pltpu.get_barrier_semaphore()
        peers = self.peers()
        for peer in peers:
            pl.semaphore_signal(sem, inc=1, device_id=peer, device_id_type=MESH)
        pl.semaphore_wait(sem, len(peers))


def remote(src, dst, send_sem, recv_sem, device):
    return pltpu.make_async_remote_copy(
        src_ref=src,
        dst_ref=dst,
        send_sem=send_sem,
        recv_sem=recv_sem,
        device_id=device,
        device_id_type=MESH,
    )


def staged(step, offset, count, action):
    @pl.when((step >= offset) & (step < count + offset))
    def _():
        action(step - offset)


class Gather:
    def __init__(self, place, own, whole, send, recv):
        self.p, self.own, self.whole, self.send, self.recv = place, own, whole, send, recv

    def copy(self, k, half, index, src, dst, device):
        return remote(src, dst, self.send.at[k, half, index], self.recv.at[k, half, index], device)

    def along_z(self, k, half, d):
        p = self.p
        dst = self.whole.at[k, half, :, p.z, p.y, p.c * p.xs + p.x]
        return self.copy(k, half, d - 1, self.own.at[k, half], dst, p.device(z=(p.z + d) % p.zs))

    def second(self, k, half):
        p = self.p
        view = self.whole.at[k, half, :, :, p.y, p.c * p.xs + p.x]
        peer = p.device(x=1 - p.x) if half == 0 else p.device(y=1 - p.y)
        return self.copy(k, half, p.zs - 1, view, view, peer)

    def third(self, k, half):
        p = self.p
        if half == 0:
            view = self.whole.at[k, half, :, :, p.y, pl.ds(p.c * p.xs, p.xs)]
            peer = p.device(y=1 - p.y)
        else:
            view = self.whole.at[k, half, :, :, :, p.c * p.xs + p.x]
            peer = p.device(x=1 - p.x)
        return self.copy(k, half, p.zs, view, view, peer)

    def fourth(self, k, half):
        p = self.p
        view = self.whole.at[k, half, :, :, :, pl.ds(p.c * p.xs, p.xs)]
        return self.copy(k, half, p.zs + 1, view, view, p.device(c=1 - p.c))

    def tick(self, step, count):
        def start_z(k):
            for half in (0, 1):
                for d in range(1, self.p.zs):
                    self.along_z(k, half, d).start()

        def start_second(k):
            for half in (0, 1):
                for d in range(1, self.p.zs):
                    self.along_z(k, half, d).wait_recv()
                self.second(k, half).start()

        def start_third(k):
            for half in (0, 1):
                self.second(k, half).wait_recv()
                self.third(k, half).start()

        def start_fourth(k):
            for half in (0, 1):
                self.third(k, half).wait_recv()
                self.fourth(k, half).start()

        def finish(k):
            for half in (0, 1):
                self.fourth(k, half).wait_recv()
                for d in range(1, self.p.zs):
                    self.along_z(k, half, d).wait_send()
                self.second(k, half).wait_send()
                self.third(k, half).wait_send()
                self.fourth(k, half).wait_send()

        staged(step, 0, count, start_z)
        staged(step, 1, count, start_second)
        staged(step, 2, count, start_third)
        staged(step, 3, count, start_fourth)
        staged(step, 4, count, finish)


def gather_kernel(zs, xs, own, whole, held, local, send, recv):
    place = Place(zs, xs)
    step = pl.program_id(0)

    @pl.when(step == 0)
    def _():
        place.barrier()
        load = pltpu.make_async_copy(own, held, local.at[0])
        load.start()
        load.wait()
        mine = whole.at[:, :, :, place.z, place.y, place.c * place.xs + place.x]
        store = pltpu.make_async_copy(held, mine, local.at[1])
        store.start()
        store.wait()

    Gather(place, held, whole, send, recv).tick(step, own.shape[0])


def gather(own, sizes, collective_id):
    grp, seq = sizes
    chunks, halves, n, rows, lanes = own.shape
    if rows % 16 or seq != 2 or grp % (Y * C):
        whole = lax.all_gather(own, ("grp", "seq"), axis=3, tiled=True)
        return whole
    zs = grp // (Y * C)
    slots = (chunks, 2, zs + 2)
    whole = pl.pallas_call(
        functools.partial(gather_kernel, zs, seq),
        grid=(chunks + 4,),
        out_shape=jax.ShapeDtypeStruct((chunks, 2, n, zs, Y, C * seq, rows, lanes), own.dtype),
        in_specs=[pl.BlockSpec(memory_space=pl.ANY)],
        out_specs=pl.BlockSpec(memory_space=pl.ANY),
        scratch_shapes=[
            pltpu.VMEM(own.shape, own.dtype),
            pltpu.SemaphoreType.DMA((2,)),
            pltpu.SemaphoreType.DMA(slots),
            pltpu.SemaphoreType.DMA(slots),
        ],
        compiler_params=pltpu.CompilerParams(collective_id=collective_id, has_side_effects=True),
    )(own)
    return whole.reshape(chunks, 2, n, grp * seq * rows, lanes)


class Scatter:
    def __init__(self, place, bufs, send, recv, out):
        self.p, self.send, self.recv, self.out = place, send, recv, out
        (self.in1, self.in2, self.in3, self.in4, self.sum1, self.sum2, self.sum3) = bufs

    def copy(self, k, half, index, src, dst, device):
        slot = k % 2
        return remote(
            src, dst, self.send.at[slot, half, index], self.recv.at[slot, half, index], device
        )

    def first(self, k, half, part):
        p = self.p
        src = part.at[half, :, :, :, pl.ds((1 - p.c) * p.xs, p.xs)]
        return self.copy(k, half, 0, src, self.in1.at[k % 2, half], p.device(c=1 - p.c))

    def second(self, k, half):
        p = self.p
        if half == 0:
            src, peer = self.sum1.at[k % 2, half, :, :, 1 - p.y], p.device(y=1 - p.y)
        else:
            src, peer = self.sum1.at[k % 2, half, :, :, :, 1 - p.x], p.device(x=1 - p.x)
        return self.copy(k, half, 1, src, self.in2.at[k % 2, half], peer)

    def third(self, k, half):
        p = self.p
        other = 1 - p.x if half == 0 else 1 - p.y
        peer = p.device(x=1 - p.x) if half == 0 else p.device(y=1 - p.y)
        src = self.sum2.at[k % 2, half, :, :, other]
        return self.copy(k, half, 2, src, self.in3.at[k % 2, half], peer)

    def fourth(self, k, half, d):
        p = self.p
        target = (p.z + d) % p.zs
        src = self.sum3.at[k % 2, half, :, target]
        dst = self.in4.at[k % 2, half, d - 1]
        return self.copy(k, half, 2 + d, src, dst, p.device(z=target))

    def finish(self, k):
        p = self.p
        slot = k % 2
        for half in (0, 1):
            total = self.sum3[slot, half, :, p.z].astype(F32)
            for d in range(1, p.zs):
                copy = self.fourth(k, half, d)
                copy.wait_recv()
                copy.wait_send()
                total = total + self.in4[slot, half, d - 1].astype(F32)
            self.out[k, half] = total

    def start_fourth(self, k):
        p = self.p
        slot = k % 2
        for half in (0, 1):
            copy = self.third(k, half)
            copy.wait_recv()
            copy.wait_send()
            keep = p.x if half == 0 else p.y
            for i in range(self.sum3.shape[2]):
                total = self.sum2[slot, half, i, :, keep].astype(F32)
                total = total + self.in3[slot, half, i].astype(F32)
                self.sum3[slot, half, i] = total.astype(BF)
            for d in range(1, p.zs):
                self.fourth(k, half, d).start()

    def start_third(self, k):
        p = self.p
        slot = k % 2
        for half in (0, 1):
            copy = self.second(k, half)
            copy.wait_recv()
            copy.wait_send()
            for i in range(self.sum2.shape[2]):
                if half == 0:
                    mine = self.sum1[slot, half, i, :, p.y]
                else:
                    mine = self.sum1[slot, half, i, :, :, p.x]
                total = mine.astype(F32) + self.in2[slot, half, i].astype(F32)
                self.sum2[slot, half, i] = total.astype(BF)
            self.third(k, half).start()

    def start_second(self, k, part):
        p = self.p
        slot = k % 2
        for half in (0, 1):
            copy = self.first(k, half, part)
            copy.wait_recv()
            copy.wait_send()

            def add(z, _, half=half):
                for i in range(self.sum1.shape[2]):
                    mine = part[half, i, z, :, pl.ds(p.c * p.xs, p.xs)]
                    total = mine.astype(F32) + self.in1[slot, half, i, z].astype(F32)
                    self.sum1[slot, half, i, z] = total.astype(BF)
                return 0

            lax.fori_loop(0, p.zs, add, 0)
            self.second(k, half).start()

    def start_first(self, k, part):
        for half in (0, 1):
            self.first(k, half, part).start()


def scatter_buffers(n, zs, xs, rows, lanes):
    shapes = [
        (2, 2, n, zs, Y, xs, rows, lanes),
        (2, 2, n, zs, 2, rows, lanes),
        (2, 2, n, zs, rows, lanes),
        (2, 2, zs - 1, n, rows, lanes),
        (2, 2, n, zs, Y, xs, rows, lanes),
        (2, 2, n, zs, 2, rows, lanes),
        (2, 2, n, zs, rows, lanes),
    ]
    return [pltpu.VMEM(shape, BF) for shape in shapes]


def scatter_kernel(zs, xs, chunks, parts, out, held, local, *rest):
    bufs, (send, recv) = rest[:7], rest[7:]
    place = Place(zs, xs)
    step = pl.program_id(0)
    engine = Scatter(place, bufs, send, recv, out)

    @pl.when(step == 0)
    def _():
        place.barrier()

    def load(k):
        return pltpu.make_async_copy(parts.at[k], held.at[k % 3], local.at[k % 3])

    def first(k):
        load(k).wait()
        engine.start_first(k, held.at[k % 3])

    staged(step, 5, chunks, engine.finish)
    staged(step, 4, chunks, engine.start_fourth)
    staged(step, 3, chunks, engine.start_third)
    staged(step, 2, chunks, lambda k: engine.start_second(k, held.at[k % 3]))
    staged(step, 1, chunks, first)
    staged(step, 0, chunks, lambda k: load(k).start())


def scatter(parts, sizes, rows, collective_id):
    grp, seq = sizes
    chunks, halves, n, _, lanes = parts.shape
    if rows % 16 or seq != 2 or grp % (Y * C):
        return lax.psum_scatter(parts, ("grp", "seq"), scatter_dimension=3, tiled=True).astype(F32)
    zs = grp // (Y * C)
    view = parts.reshape(chunks, 2, n, zs, Y, C * seq, rows, lanes)
    sems = (2, 2, zs + 2)
    return pl.pallas_call(
        functools.partial(scatter_kernel, zs, seq, chunks),
        grid=(chunks + 5,),
        out_shape=jax.ShapeDtypeStruct((chunks, 2, n, rows, lanes), F32),
        in_specs=[pl.BlockSpec(memory_space=pl.ANY)],
        out_specs=pl.BlockSpec((chunks, 2, n, rows, lanes), lambda step: (0, 0, 0, 0, 0)),
        scratch_shapes=[
            pltpu.VMEM((3, 2, n, zs, Y, C * seq, rows, lanes), BF),
            pltpu.SemaphoreType.DMA((3,)),
        ]
        + scatter_buffers(n, zs, seq, rows, lanes)
        + [pltpu.SemaphoreType.DMA(sems), pltpu.SemaphoreType.DMA(sems)],
        compiler_params=pltpu.CompilerParams(
            collective_id=collective_id, has_side_effects=True, vmem_limit_bytes=VMEM_LIMIT
        ),
    )(view)


def band_of(key_tile, query_tile):
    return jnp.clip(key_tile - query_tile, -2, 2) + 2


def attend_kernel(tiles, local_tiles, conts, live, base, q, k, v, bias, out, norm):
    first_half = lax.broadcasted_iota(jnp.int32, (T, 2 * HEAD), 1) < HEAD
    place = lax.broadcasted_iota(jnp.int32, (T, T), 1)

    def tile(i, is_cont):
        rows = pl.ds(pl.multiple_of(i * T, T), T)
        queries = q[rows, :]
        query_tile = tiles if is_cont else base[0] + i
        cont = i - local_tiles
        cont_keys = pl.ds(pl.multiple_of((tiles + cont) * T, T), T)
        mixed = []
        for h in range(2):
            mine = first_half if h == 0 else ~first_half
            masked = jnp.where(mine, queries, jnp.zeros_like(queries))
            scores = nt(masked, k[0 : tiles * T, :])
            parts = []
            for j in range(tiles):
                band = band_of(lax.rem(base[1] + j, tiles), query_tile)
                parts.append(scores[:, j * T : (j + 1) * T] + bias[h, band])
            if is_cont:
                own = nt(masked, k[cont_keys, :]) + bias[h, 2]
                parts.append(jnp.where(place < live[0, cont], own, NEGATIVE))
            top = jnp.max(functools.reduce(jnp.maximum, parts), axis=1, keepdims=True)
            weights = [jnp.exp(part - top) for part in parts]
            total = jnp.sum(functools.reduce(jnp.add, weights), axis=1, keepdims=True)
            inverse = 1.0 / total
            probs = [(weight * inverse).astype(BF) for weight in weights]
            result = nn(jnp.concatenate(probs[:tiles], axis=1), v[0 : tiles * T, :])
            if is_cont:
                result = result + nn(probs[tiles], v[cont_keys, :])
            mixed.append(result)
            norm[h, rows, :] = top + jnp.log(total)
        out[rows, :] = jnp.where(first_half, mixed[0], mixed[1]).astype(BF)

    def prompt_tile(i, carry):
        tile(i, False)
        return carry

    def cont_tile(i, carry):
        tile(i, True)
        return carry

    lax.fori_loop(0, local_tiles, prompt_tile, 0)
    lax.fori_loop(local_tiles, local_tiles + conts, cont_tile, 0)


def attend(q, k, v, bias, live, base, tiles, local_tiles, conts):
    rows, width = q.shape
    keys = k.shape[0]
    pairs = width // (2 * HEAD)
    block = lambda n: pl.BlockSpec((n, 2 * HEAD), lambda h, *_: (0, h))
    return pl.pallas_call(
        functools.partial(attend_kernel, tiles, local_tiles, conts),
        grid_spec=pltpu.PrefetchScalarGridSpec(
            num_scalar_prefetch=2,
            grid=(pairs,),
            in_specs=[
                block(rows),
                block(keys),
                block(keys),
                pl.BlockSpec((2, BANDS, T, T), lambda h, *_: (h, 0, 0, 0)),
            ],
            out_specs=[block(rows), pl.BlockSpec((2, rows, 1), lambda h, *_: (h, 0, 0))],
        ),
        out_shape=[
            jax.ShapeDtypeStruct((rows, width), BF),
            jax.ShapeDtypeStruct((2 * pairs, rows, 1), F32),
        ],
        compiler_params=pltpu.CompilerParams(vmem_limit_bytes=VMEM_LIMIT),
    )(live, base, q, k, v, bias)


def attend_back_kernel(
    tiles,
    local_tiles,
    conts,
    live,
    base,
    q,
    k,
    v,
    bias,
    grad,
    out,
    norm,
    d_q,
    d_k,
    d_v,
    d_bias,
    k_sum,
    v_sum,
):
    first_half = lax.broadcasted_iota(jnp.int32, (T, 2 * HEAD), 1) < HEAD
    place = lax.broadcasted_iota(jnp.int32, (T, T), 1)
    k_sum[...] = jnp.zeros_like(k_sum)
    v_sum[...] = jnp.zeros_like(v_sum)
    d_bias[...] = jnp.zeros_like(d_bias)

    def tile(i, is_cont):
        rows = pl.ds(pl.multiple_of(i * T, T), T)
        queries = q[rows, :]
        grads = grad[rows, :]
        query_tile = tiles if is_cont else base[0] + i
        overlap = grads.astype(F32) * out[rows, :].astype(F32)
        mixed = []
        for h in range(2):
            mine = first_half if h == 0 else ~first_half
            masked = jnp.where(mine, queries, jnp.zeros_like(queries))
            masked_grad = jnp.where(mine, grads, jnp.zeros_like(grads))
            inner = jnp.sum(jnp.where(mine, overlap, 0.0), axis=1, keepdims=True)
            log_norm = norm[h, rows, :]

            def piece(keys, bands, allowed):
                scores = nt(masked, k[keys, :])
                d_probs = nt(masked_grad, v[keys, :])
                probs_low, scores_low = [], []
                for j, band in enumerate(bands):
                    cols = slice(j * T, (j + 1) * T)
                    logits = scores[:, cols] + bias[h, band]
                    if allowed is not None:
                        logits = jnp.where(allowed, logits, NEGATIVE)
                    probs = jnp.exp(logits - log_norm)
                    d_scores = probs * (d_probs[:, cols] - inner)
                    d_bias[h, band] += d_scores
                    probs_low.append(probs.astype(BF))
                    scores_low.append(d_scores.astype(BF))
                probs_low = jnp.concatenate(probs_low, axis=1)
                scores_low = jnp.concatenate(scores_low, axis=1)
                v_sum[keys, :] += tn(probs_low, masked_grad)
                k_sum[keys, :] += tn(scores_low, masked)
                return nn(scores_low, k[keys, :])

            bands = [band_of(lax.rem(base[1] + j, tiles), query_tile) for j in range(tiles)]
            result = piece(pl.ds(0, tiles * T), bands, None)
            if is_cont:
                cont = i - local_tiles
                cont_keys = pl.ds(pl.multiple_of((tiles + cont) * T, T), T)
                result = result + piece(cont_keys, [2], place < live[0, cont])
            mixed.append(result)
        d_q[rows, :] = jnp.where(first_half, mixed[0], mixed[1]).astype(BF)

    def prompt_tile(i, carry):
        tile(i, False)
        return carry

    def cont_tile(i, carry):
        tile(i, True)
        return carry

    lax.fori_loop(0, local_tiles, prompt_tile, 0)
    lax.fori_loop(local_tiles, local_tiles + conts, cont_tile, 0)
    d_k[...] = k_sum[...].astype(BF)
    d_v[...] = v_sum[...].astype(BF)


def attend_back(q, k, v, bias, grad, out, norm, live, base, tiles, local_tiles, conts):
    rows, width = q.shape
    keys = k.shape[0]
    pairs = width // (2 * HEAD)
    block = lambda n: pl.BlockSpec((n, 2 * HEAD), lambda h, *_: (0, h))
    bands = pl.BlockSpec((2, BANDS, T, T), lambda h, *_: (h, 0, 0, 0))
    return pl.pallas_call(
        functools.partial(attend_back_kernel, tiles, local_tiles, conts),
        grid_spec=pltpu.PrefetchScalarGridSpec(
            num_scalar_prefetch=2,
            grid=(pairs,),
            in_specs=[
                block(rows),
                block(keys),
                block(keys),
                bands,
                block(rows),
                block(rows),
                pl.BlockSpec((2, rows, 1), lambda h, *_: (h, 0, 0)),
            ],
            out_specs=[block(rows), block(keys), block(keys), bands],
            scratch_shapes=[pltpu.VMEM((keys, 2 * HEAD), F32), pltpu.VMEM((keys, 2 * HEAD), F32)],
        ),
        out_shape=[
            jax.ShapeDtypeStruct((rows, width), BF),
            jax.ShapeDtypeStruct((keys, width), BF),
            jax.ShapeDtypeStruct((keys, width), BF),
            jax.ShapeDtypeStruct((2 * pairs, BANDS, T, T), F32),
        ],
        compiler_params=pltpu.CompilerParams(vmem_limit_bytes=VMEM_LIMIT),
    )(live, base, q, k, v, bias, grad, out, norm)


GELU_SCALE = 0.7978845608028654
GELU_CUBIC = 0.044715


def gelu_and_slope(a):
    square = a * a
    tanh = jnp.tanh(GELU_SCALE * a * (1.0 + GELU_CUBIC * square))
    half = 0.5 * (1.0 + tanh)
    slope = half + 0.5 * a * (1.0 - tanh * tanh) * (
        GELU_SCALE * (1.0 + 3.0 * GELU_CUBIC * square)
    )
    return a * half, slope


def feed_kernel(
    x_hbm,
    dy_hbm,
    weights,
    out,
    d_x,
    grads,
    x,
    x_t,
    dy,
    dy_t,
    out_sum,
    d_x_sum,
    hidden,
    d_gate,
    d_up,
    sem,
):
    step = pl.program_id(0)
    rows = x.shape[0]
    row_block = min(rows, 256)
    width = x.shape[1]
    width_block = 512

    @pl.when(step == 0)
    def _():
        load_x = pltpu.make_async_copy(x_hbm, x, sem.at[0])
        load_dy = pltpu.make_async_copy(dy_hbm, dy, sem.at[1])
        load_x.start()
        load_dy.start()
        load_x.wait()
        load_dy.wait()

        def turn(i, carry):
            part = pl.ds(pl.multiple_of(i * T, T), T)
            x_t[:, part] = x[part, :].T
            dy_t[:, part] = dy[part, :].T
            return carry

        lax.fori_loop(0, rows // T, turn, 0)
        out_sum[...] = jnp.zeros_like(out_sum)
        d_x_sum[...] = jnp.zeros_like(d_x_sum)

    w_gate, w_up, w_down = [
        jnp.concatenate([weights[0, 0, i], weights[0, 1, i]], axis=1) for i in range(3)
    ]

    def by_rows(i, carry):
        part = pl.ds(pl.multiple_of(i * row_block, row_block), row_block)
        gate = nn(x[part, :], w_gate)
        up = nn(x[part, :], w_up)
        d_hidden = nn(dy[part, :], w_down)
        active, slope = gelu_and_slope(gate)
        hidden_low = (active * up).astype(BF)
        d_gate_low = (d_hidden * up * slope).astype(BF)
        d_up_low = (d_hidden * active).astype(BF)
        hidden[part, :] = hidden_low
        d_gate[part, :] = d_gate_low
        d_up[part, :] = d_up_low
        out_sum[part, :] += nt(hidden_low, w_down)
        d_x_sum[part, :] += nt(d_gate_low, w_gate) + nt(d_up_low, w_up)
        return carry

    lax.fori_loop(0, rows // row_block, by_rows, 0)

    def by_width(i, carry):
        part = pl.ds(pl.multiple_of(i * width_block, width_block), width_block)
        pairs = ((x_t, d_gate), (x_t, d_up), (dy_t, hidden))
        for index, (left, right) in enumerate(pairs):
            total = nn(left[part, :], right[...]).astype(BF)
            grads[0, 0, index, part, :] = total[:, :T]
            grads[0, 1, index, part, :] = total[:, T:]
        return carry

    lax.fori_loop(0, width // width_block, by_width, 0)

    @pl.when(step == pl.num_programs(0) - 1)
    def _():
        out[...] = out_sum[...]
        d_x[...] = d_x_sum[...]


def feed(x, dy, weights):
    rows, width = x.shape
    chunks = weights.shape[0]
    chunk = pl.BlockSpec((1, 2, 3, width, T), lambda j: (j, 0, 0, 0, 0))
    whole = pl.BlockSpec((rows, width), lambda j: (0, 0), pipeline_mode=pl.Buffered(1))
    return pl.pallas_call(
        feed_kernel,
        grid=(chunks,),
        in_specs=[pl.BlockSpec(memory_space=pl.ANY)] * 2 + [chunk],
        out_specs=[whole, whole, chunk],
        out_shape=[
            jax.ShapeDtypeStruct((rows, width), F32),
            jax.ShapeDtypeStruct((rows, width), F32),
            jax.ShapeDtypeStruct((chunks, 2, 3, width, T), BF),
        ],
        scratch_shapes=[
            pltpu.VMEM((rows, width), BF),
            pltpu.VMEM((width, rows), BF),
            pltpu.VMEM((rows, width), BF),
            pltpu.VMEM((width, rows), BF),
            pltpu.VMEM((rows, width), F32),
            pltpu.VMEM((rows, width), F32),
            pltpu.VMEM((rows, 2 * T), BF),
            pltpu.VMEM((rows, 2 * T), BF),
            pltpu.VMEM((rows, 2 * T), BF),
            pltpu.SemaphoreType.DMA((2,)),
        ],
        compiler_params=pltpu.CompilerParams(vmem_limit_bytes=VMEM_LIMIT),
    )(x, dy, weights)


def rms_scale(values):
    return lax.rsqrt(jnp.mean(values * values, axis=-1, keepdims=True) + EPS)


def norm_back(d_normed, unit, scale, gain):
    d_unit = d_normed * gain
    return scale * (d_unit - unit * jnp.mean(d_unit * unit, axis=-1, keepdims=True))


def pieces_of(matrix):
    rows, columns = matrix.shape
    return jnp.swapaxes(matrix.reshape(rows, columns // T, T), 0, 1)


def joined(pieces):
    count, rows, _ = pieces.shape
    return jnp.swapaxes(pieces, 0, 1).reshape(rows, count * T)


def attention_chunks(matrices):
    flat = jnp.concatenate([pieces_of(m) for m in matrices], axis=0)
    pad = -flat.shape[0] % 6
    flat = jnp.pad(flat, ((0, pad), (0, 0), (0, 0)))
    return flat.reshape(-1, 2, 3, *flat.shape[1:])


def feed_chunks(matrices):
    stacked = jnp.stack([pieces_of(m) for m in matrices], axis=1)
    pad = -stacked.shape[0] % 2
    stacked = jnp.pad(stacked, ((0, pad), (0, 0), (0, 0), (0, 0)))
    return stacked.reshape(-1, 2, *stacked.shape[1:])


def body(sizes, *args):
    (
        prompt_x,
        cont_x,
        cont_len,
        prompt_cot,
        cont_cot,
        norm1_gain,
        q_weight,
        k_weight,
        v_weight,
        o_weight,
        bucket_table,
        norm2_gain,
        gate_weight,
        up_weight,
        down_weight,
    ) = args
    _, local_prompt, width = prompt_x.shape
    conts, cont_rows = cont_x.shape[1], cont_x.shape[2]
    assert prompt_x.shape[0] == 1 and cont_rows == T and local_prompt % T == 0
    seq = sizes[1]
    num_buckets, heads = bucket_table.shape
    inner = q_weight.shape[1]
    assert inner == heads * HEAD
    shard = q_weight.shape[0]
    hidden_width = gate_weight.shape[1]
    local_tiles = local_prompt // T
    tiles = local_tiles * seq
    seq_index = lax.axis_index("seq")

    x_low = jnp.concatenate([prompt_x[0], cont_x[0].reshape(-1, width)], axis=0)
    dy_low = jnp.concatenate([prompt_cot[0], cont_cot[0].reshape(-1, width)], axis=0)
    x = x_low.astype(F32)
    dy = dy_low.astype(F32)

    lanes = jnp.zeros((shard, T - 2), F32)
    gains = jnp.concatenate([norm1_gain[:, None], norm2_gain[:, None], lanes], axis=1)
    own_attention = attention_chunks([q_weight, k_weight, v_weight, o_weight, gains]).astype(BF)
    own_feed = feed_chunks([gate_weight, up_weight, down_weight]).astype(BF)
    attention_whole = gather(own_attention, sizes, 0)
    count = inner // T
    flat = attention_whole.reshape(-1, width, T)
    q_full, k_full, v_full, o_full = [
        joined(flat[i * count : (i + 1) * count]) for i in range(4)
    ]
    gain_one = flat[4 * count, :, 0].astype(F32)
    gain_two = flat[4 * count, :, 1].astype(F32)
    feed_whole = gather(own_feed, sizes, 1)

    scale_one = rms_scale(x)
    unit_one = x * scale_one
    normed_one = (unit_one * gain_one).astype(BF)
    kv = nn(normed_one, jnp.concatenate([k_full, v_full], axis=1)).astype(BF)
    queries = nn(normed_one, q_full).astype(BF)
    prompt_kv = kv[:local_prompt]
    if seq == 2:
        other = lax.ppermute(prompt_kv, "seq", [(0, 1), (1, 0)])
        every = jnp.concatenate([kv[:local_prompt], other, kv[local_prompt:]], axis=0)
        first_tile = seq_index * local_tiles
    else:
        gathered = lax.all_gather(prompt_kv, "seq", axis=0, tiled=True)
        every = jnp.concatenate([gathered, kv[local_prompt:]], axis=0)
        first_tile = jnp.zeros((), jnp.int32)
    keys, values = every[:, :inner], every[:, inner:]
    base = jnp.stack([seq_index * local_tiles, first_tile]).astype(jnp.int32)

    one_hot = band_one_hot(num_buckets)
    bias = jnp.einsum("cqkb,bh->hcqk", one_hot, bucket_table, precision=lax.Precision.HIGHEST)
    attended, log_norm = attend(
        queries, keys, values, bias, cont_len, base, tiles, local_tiles, conts
    )
    middle = x + nt(attended, o_full)
    scale_two = rms_scale(middle)
    unit_two = middle * scale_two
    normed_two = (unit_two * gain_two).astype(BF)

    out_sum, d_normed_two, feed_grads = feed(normed_two, dy_low, feed_whole)
    final = (middle + out_sum).astype(BF)

    d_gain_two = jnp.sum(d_normed_two * unit_two, axis=0)
    d_middle = dy + norm_back(d_normed_two, unit_two, scale_two, gain_two)
    d_branch = d_middle.astype(BF)
    d_attended = nn(d_branch, o_full).astype(BF)
    d_o = tn(d_branch, attended)

    d_queries, d_keys, d_values, d_bias = attend_back(
        queries,
        keys,
        values,
        bias,
        d_attended,
        attended,
        log_norm,
        cont_len,
        base,
        tiles,
        local_tiles,
        conts,
    )
    d_table = jnp.einsum("hcqk,cqkb->bh", d_bias, one_hot, precision=lax.Precision.HIGHEST)
    d_kv = jnp.concatenate([d_keys, d_values], axis=1)
    prompt_rows = local_prompt * seq
    if seq == 2:
        back = lax.ppermute(d_kv[local_prompt:prompt_rows], "seq", [(0, 1), (1, 0)])
        d_prompt = (d_kv[:local_prompt].astype(F32) + back.astype(F32)).astype(BF)
    else:
        d_prompt = lax.psum_scatter(
            d_kv[:prompt_rows], "seq", scatter_dimension=0, tiled=True
        )
    d_kv = jnp.concatenate([d_prompt, d_kv[prompt_rows:]], axis=0)
    d_normed_one = nt(d_queries, q_full) + nt(d_kv, jnp.concatenate([k_full, v_full], axis=1))
    d_q = tn(normed_one, d_queries)
    d_kv_weight = tn(normed_one, d_kv)
    d_gain_one = jnp.sum(d_normed_one * unit_one, axis=0)
    d_x = d_middle + norm_back(d_normed_one, unit_one, scale_one, gain_one)
    d_x = d_x.astype(BF)

    attention_parts = attention_chunks([d_q, d_kv_weight, d_o]).astype(BF)
    parts = jnp.concatenate([feed_grads, attention_parts], axis=0)
    sums = scatter(parts, sizes, shard, 2)
    feed_sums = sums[: feed_grads.shape[0]].reshape(-1, 3, shard, T)
    feed_sums = feed_sums[: hidden_width // T]
    gate_grad, up_grad, down_grad = [joined(feed_sums[:, i]) for i in range(3)]
    attention_sums = sums[feed_grads.shape[0] :].reshape(-1, shard, T)
    q_grad, k_grad, v_grad, o_grad = [
        joined(attention_sums[i * count : (i + 1) * count]) for i in range(4)
    ]
    norm1_grad = lax.psum_scatter(d_gain_one, ("grp", "seq"), scatter_dimension=0, tiled=True)
    norm2_grad = lax.psum_scatter(d_gain_two, ("grp", "seq"), scatter_dimension=0, tiled=True)
    table_grad = lax.psum(d_table, ("grp", "seq"))
    split = lambda rows: (
        rows[:local_prompt][None],
        rows[local_prompt:].reshape(1, conts, cont_rows, width),
    )
    return (
        *split(final),
        *split(d_x),
        norm1_grad,
        q_grad,
        k_grad,
        v_grad,
        o_grad,
        table_grad,
        norm2_grad,
        gate_grad,
        up_grad,
        down_grad,
    )


def solution(mesh):
    sizes = (mesh.shape["grp"], mesh.shape["seq"])
    rows = P("grp", "seq", None)
    conts = P("grp", "seq", None, None)
    shard = P(("grp", "seq"), None)
    gain = P(("grp", "seq"))
    in_specs = (rows, conts, P("grp", "seq"), rows, conts, gain, shard, shard, shard, shard)
    in_specs += (P(), gain, shard, shard, shard)
    out_specs = (rows, conts, rows, conts, gain, shard, shard, shard, shard, P(), gain)
    out_specs += (shard, shard, shard)
    return jax.shard_map(
        functools.partial(body, sizes),
        mesh=mesh,
        in_specs=in_specs,
        out_specs=out_specs,
        check_vma=False,
    )
```

time: 1860 us -> 1080 us (0.58)
  Pallas kernels: 0 us -> 785 us
  matrix products: 669 us -> 72 us
  waiting for transfers between devices: 566 us -> 3.72 us
  local copies, waits for them, and re-layouts: 282 us -> 88.3 us
  other arithmetic: 189 us -> 75.6 us
  blocking collectives: 110 us -> 39.4 us
    pallas_call x0 -> x6, Pallas kernels: none -> 785 us  [the longest x2 247 us: gather(): pl.pallas_call(functools.partial(gather_kernel, zs, seq), grid=(chunks +...]
    dot_general x29 -> x11, matrix products: 669 us -> 72 us  [the longest x3 21 us: nt(): lax.dot_general(left, right, (((1,), (1,)), ((), ())), preferred_element_...]
    reduce_scatter x11 -> x0, waiting for transfers between devices: 308 us -> none  [the longest x1 110 us: body(): lax.psum_scatter(flatten(d_v_weight, inner_lanes), ('grp', 'seq'), scatte...]
    all_gather x11 -> x0, waiting for transfers between devices: 258 us -> none  [the longest x1 63.7 us: body(): lax.all_gather(column_parts[2], 'grp', axis=0, tiled=True)]
    mul x1 -> x0, local copies, waits for them, and re-layouts: 86.9 us -> none  [attend_back(): probs * (d_probs - jnp.sum(probs * d_probs, axis=-1, keepdims=True))]
    dot_general x1, local copies, waits for them, and re-layouts: 89.4 us -> 6.03 us  [body(): jnp.einsum('cqkb,bh->hcqk', one_hot, bucket_table, precision=lax.Precisio...]
    mul x1, other arithmetic: 72.1 us -> 0.01 us  [band_one_hot(): ids = bucket_ids(band * T + key - query)]
    unnamed x2 -> x1, blocking collectives: 82.5 us -> 39.4 us
  transfers between devices with their start and end apart: 26 -> 2, of which waited for: 11 -> 1; matrix products, arithmetic and copies ran while one was open for 57% -> 6% of each run, Pallas kernels for 0% -> 16%
where the time goes in v1:
time: 1080 us; the launch traced here: 1070 us
  Pallas kernels  785 us (73%)
  local copies, waits for them, and re-layouts  88.3 us (8%)
  other arithmetic  75.6 us (7%)
  matrix products  72 us (7%)
  blocking collectives  39.4 us (4%)
    pallas_call x2, Pallas kernels, gather(): pl.pallas_call(functools.partial(gather_kernel, zs, seq), grid=(chunks +...  247 us
    pallas_call x1, Pallas kernels, scatter(): pl.pallas_call(functools.partial(scatter_kernel, zs, seq, chunks), grid=(...  238 us
    pallas_call x1, Pallas kernels, feed(): pl.pallas_call(feed_kernel, grid=(chunks,), in_specs=[pl.BlockSpec(memory...  165 us
    pallas_call x1, Pallas kernels, attend_back(): pl.pallas_call(functools.partial(attend_back_kernel, tiles, local_tiles,...  79.5 us
    pallas_call x1, Pallas kernels, attend(): pl.pallas_call(functools.partial(attend_kernel, tiles, local_tiles, conts...  56.5 us
    unnamed x1, blocking collectives  39.4 us
    concatenate x1, other arithmetic, body(): parts = jnp.concatenate([feed_grads, attention_parts], axis=0)  31.7 us
    slice x5, local copies, waits for them, and re-layouts, body(): flat[i * count:(i + 1) * count]  21.9 us
  transfers between devices with their start and end apart: 2, of which 1 were waited for; matrix products, arithmetic and copies ran while one was open for 6% of the time, Pallas kernels for 16%

profile of v1, /device:TPU:0, one launch (start us, length us, event | category | flops | bytes accessed | tf_op | source)
XLA Modules:
  0.0 1070.0 jit_solution(11350500195515003551)
XLA Ops:
  6.3 70.9 %shard_map.254 = bf16[5,2,3,4,2,4,48,128]{7,6,5,4,3,2,1,0:T(8,128)(2,1)} custom-call(bf16[5,2,3,48,128]{4,3,2,1,0:T(8,128)(2,1)} %bitcast.175), custom_call_target="tpu_custom_call" | custom-call | tf_op jit(solution)/shard_map/pallas_call | solution.py:196
  77.2 6.6 fusion.40
  93.9 8.4 convolution_convert_fusion.1
  116.0 6.0 copy.107
  129.6 175.8 %shard_map.256 = bf16[16,2,3,4,2,4,48,128]{7,6,5,4,3,2,1,0:T(8,128)(2,1)} custom-call(bf16[16,2,3,48,128]{4,3,2,1,0:T(8,128)(2,1)} %bitcast.155), custom_call_target="tpu_custom_call" | custom-call | tf_op jit(solution)/shard_map/pallas_call | solution.py:196
  319.6 56.5 %shard_map.255 = (bf16[1024,768]{1,0:T(8,128)(2,1)}, f32[12,1024,1]{2,1,0:T(8,128)}) custom-call(s32[1,4]{1,0:T(1,128)} %live.3, s32[2]{0:T(128)} %pad_add_fusion.base, bf16[1024,768]{1,0:T(8,128)(2,1)} %convolution_convert_fusion.5.q, bf16[1536,768]{1,0:T(8,128)(2,1)} %get-tuple-element.50.k, bf16[1536,768]{1,0:T(8,128)(2,1)} %get-tuple-element.49.v, ...), custom_call_target="tpu_custom_call" | custom-call | tf_op jit(solution)/shard_map/pallas_call | solution.py:436
  376.1 5.8 multiply_reduce_fusion.2
  385.7 164.9 %shard_map.257 = (f32[1024,1536]{1,0:T(8,128)}, f32[1024,1536]{1,0:T(8,128)}, bf16[16,2,3,1536,128]{4,3,2,1,0:T(8,128)(2,1)}) custom-call(bf16[1024,1536]{1,0:T(8,128)(2,1)} %multiply_convert_fusion.x_hbm, bf16[1024,1536]{1,0:T(8,128)(2,1)} %pad_maximum_fusion.5.dy_hbm, bf16[16,2,3,1536,128]{4,3,2,1,0:T(8,128)(2,1)} %bitcast.118), custom_call_target="tpu_custom_call" | custom-call | tf_op jit(solution)/shard_map/pallas_call | solution.py:674
  550.6 6.8 multiply_reduce_fusion
  558.9 6.4 multiply_add_fusion
  565.2 7.1 convolution_convert_fusion.4.grad
  572.3 79.5 %shard_map.258 = (bf16[1024,768]{1,0:T(8,128)(2,1)}, bf16[1536,768]{1,0:T(8,128)(2,1)}, bf16[1536,768]{1,0:T(8,128)(2,1)}, f32[12,5,128,128]{3,2,1,0:T(8,128)}) custom-call(s32[1,4]{1,0:T(1,128)} %live.3, s32[2]{0:T(128)} %pad_add_fusion.base, bf16[1024,768]{1,0:T(8,128)(2,1)} %convolution_convert_fusion.5.q, bf16[1536,768]{1,0:T(8,128)(2,1)} %get-tuple-element.50.k, ...), custom_call_target="tpu_custom_call" | custom-call | tf_op jit(solution)/shard_map/pallas_call | solution.py:546
  667.2 6.7 convolution_convert_fusion.3
  678.2 6.1 copy.118
  684.4 7.3 fusion.19
  697.7 7.4 convolution_convert_fusion
  705.1 6.6 copy.112
  711.7 8.3 pad_maximum_fusion.1
  720.0 31.7 %pad_maximum_fusion = bf16[20,2,3,1536,128]{4,3,2,1,0:T(8,128)(2,1)} fusion(bf16[4,2,3,1536,128]{4,3,2,1,0:T(8,128)(2,1)} %bitcast.122, bf16[16,2,3,1536,128]{4,3,2,1,0:T(8,128)(2,1)} %get-tuple-element.30), kind=kLoop, calls=%fused_computation | loop fusion | flops 23592960 | bytes 94371840 | tf_op jit(solution)/shard_map/concatenate | solution.py:852
  751.8 237.6 %shard_map.259 = f32[20,2,3,48,128]{4,3,2,1,0:T(8,128)} custom-call(bf16[20,2,3,4,2,4,48,128]{7,6,5,4,3,2,1,0:T(8,128)(2,1)} %bitcast.117), custom_call_target="tpu_custom_call" | custom-call | tf_op jit(solution)/shard_map/pallas_call | solution.py:363
  992.0 7.8 fusion.16
  1005.3 7.4 fusion.12
  1012.8 39.4 %all-reduce.4 = (f32[1536]{0:T(1024)}, f32[32,12]{0,1:T(8,128)}, f32[1536]{0:T(1024)}) all-reduce(f32[1536]{0:T(1024)} %get-tuple-element.34, f32[32,12]{0,1:T(8,128)S(1)} %fusion.19, f32[1536]{0:T(1024)} %get-tuple-element.32), channel_id=2, replica_groups=mesh['grp'=16,'seq'=2] {'grp','seq'}, use_global_device_ids=true, to_apply=%region_5.6.clone | all-reduce | flops 3456 | bytes 27648
  1060.5 6.2 fusion.11
  (166 shorter events, 100.9 us)
Async XLA Ops:
  0.6 110.4 %copy-start = (f32[32,12]{0,1:T(8,128)S(1)}, f32[32,12]{0,1:T(8,128)}, u32[]{:S(2)}) copy-start(f32[32,12]{0,1:T(8,128)} %param.25) | copy-start | bytes 4612
  3.4 694.3 %copy-start.31 = (f32[1024]{0:T(1024)}, f32[1024]{0:T(1024)S(1)}, u32[]{:S(2)}) copy-start(f32[1024]{0:T(1024)S(1)} %add_rsqrt_fusion.1) | copy-start | bytes 12292
  104.2 210.9 %collective-permute-start = (bf16[512,1536]{1,0:T(8,128)(2,1)}, bf16[512,1536]{1,0:T(8,128)(2,1)}, u32[]{:S(2)}, u32[]{:S(2)}) collective-permute-start(bf16[512,1536]{1,0:T(8,128)(2,1)} %get-tuple-element.55), channel_id=1, source_target_pairs={{0,1},{1,0},{2,3},{3,2},{4,5},{5,4},{6,7},{7,6},{8,9},{9,8},{10,11... | collective-permute-start | bytes 4718600 | tf_op jit(solution)/shard_map/ppermute | solution.py:790
  129.6 176.5 %copy-start.8 = (bf16[1,4,128,1536]{3,2,1,0:T(8,128)(2,1)S(1)}, bf16[1,4,128,1536]{3,2,1,0:T(8,128)(2,1)}, u32[]{:S(2)}) copy-start(bf16[1,4,128,1536]{3,2,1,0:T(8,128)(2,1)} %param.19) | copy-start | bytes 4718596
  129.6 176.5 %copy-start.9 = (bf16[1,512,1536]{2,1,0:T(8,128)(2,1)S(1)}, bf16[1,512,1536]{2,1,0:T(8,128)(2,1)}, u32[]{:S(2)}) copy-start(bf16[1,512,1536]{2,1,0:T(8,128)(2,1)} %param.18) | copy-start | bytes 4718596
  309.9 5.2 copy-start.10
  550.5 6.9 slice-start
  550.6 6.8 slice-start.1
  550.6 8.3 copy-start.4
  565.2 7.1 copy-start.3
  651.8 8.3 slice-start.2
  654.2 6.0 slice-start.3
  654.4 5.8 copy-start.21
  658.2 37.2 %collective-permute-start.1 = (bf16[512,1536]{1,0:T(8,128)(2,1)}, bf16[512,1536]{1,0:T(8,128)(2,1)}, u32[]{:S(2)}, u32[]{:S(2)}) collective-permute-start(bf16[512,1536]{1,0:T(8,128)(2,1)} %get-tuple-element.47), channel_id=1, source_target_pairs={{0,1},{1,0},{2,3},{3,2},{4,5},{5,4},{6,7},{7,6},{8,9},{9,8},{10,11... | collective-permute-start | bytes 4718600 | tf_op jit(solution)/shard_map/ppermute | solution.py:837
  691.7 6.0 copy-start.12
  691.7 6.0 copy-start.15
  691.7 6.0 copy-start.22
  697.7 7.4 copy-start.23
  991.9 7.8 slice-start.4
  999.9 5.4 copy-start.34
  1052.1 6.9 copy-start.24
  1052.1 7.6 copy-start.25
  1052.1 8.4 copy-start.33
  1060.5 6.2 copy-start.5
  (20 other events, 64.4 us)

commit v2 on v1

--- a/solution.py
+++ b/solution.py
@@ -47,6 +47,10 @@
     return (ids[..., None] == jnp.arange(num_buckets)).astype(F32)
 
 
+def can_move(sizes, rows):
+    return rows % 16 == 0 and sizes[1] == 2 and sizes[0] % (Y * C) == 0 and sizes[0] > Y * C
+
+
 class Place:
     def __init__(self, zs, xs):
         grp = lax.axis_index("grp")
@@ -129,7 +133,7 @@
         view = self.whole.at[k, half, :, :, :, pl.ds(p.c * p.xs, p.xs)]
         return self.copy(k, half, p.zs + 1, view, view, p.device(c=1 - p.c))
 
-    def tick(self, step, count):
+    def tick(self, step, first, end):
         def start_z(k):
             for half in (0, 1):
                 for d in range(1, self.p.zs):
@@ -160,11 +164,8 @@
                 self.third(k, half).wait_send()
                 self.fourth(k, half).wait_send()
 
-        staged(step, 0, count, start_z)
-        staged(step, 1, count, start_second)
-        staged(step, 2, count, start_third)
-        staged(step, 3, count, start_fourth)
-        staged(step, 4, count, finish)
+        for offset, action in enumerate((start_z, start_second, start_third, start_fourth, finish)):
+            staged(step, offset, end - first, lambda k, action=action: action(first + k))
 
 
 def gather_kernel(zs, xs, own, whole, held, local, send, recv):
@@ -182,13 +183,13 @@
         store.start()
         store.wait()
 
-    Gather(place, held, whole, send, recv).tick(step, own.shape[0])
+    Gather(place, held, whole, send, recv).tick(step, 0, own.shape[0])
 
 
 def gather(own, sizes, collective_id):
     grp, seq = sizes
     chunks, halves, n, rows, lanes = own.shape
-    if rows % 16 or seq != 2 or grp % (Y * C):
+    if not can_move(sizes, rows):
         whole = lax.all_gather(own, ("grp", "seq"), axis=3, tiled=True)
         return whole
     zs = grp // (Y * C)
@@ -355,7 +356,7 @@
 def scatter(parts, sizes, rows, collective_id):
     grp, seq = sizes
     chunks, halves, n, _, lanes = parts.shape
-    if rows % 16 or seq != 2 or grp % (Y * C):
+    if not can_move(sizes, rows):
         return lax.psum_scatter(parts, ("grp", "seq"), scatter_dimension=3, tiled=True).astype(F32)
     zs = grp // (Y * C)
     view = parts.reshape(chunks, 2, n, zs, Y, C * seq, rows, lanes)
@@ -584,52 +585,28 @@
     return a * half, slope
 
 
-def feed_kernel(
-    x_hbm,
-    dy_hbm,
-    weights,
-    out,
-    d_x,
-    grads,
-    x,
-    x_t,
-    dy,
-    dy_t,
-    out_sum,
-    d_x_sum,
-    hidden,
-    d_gate,
-    d_up,
-    sem,
-):
-    step = pl.program_id(0)
-    rows = x.shape[0]
+def feed_load(x_hbm, dy_hbm, x, x_t, dy, dy_t, sem):
+    load_x = pltpu.make_async_copy(x_hbm, x, sem.at[0])
+    load_dy = pltpu.make_async_copy(dy_hbm, dy, sem.at[1])
+    load_x.start()
+    load_dy.start()
+    load_x.wait()
+    load_dy.wait()
+
+    def turn(i, carry):
+        part = pl.ds(pl.multiple_of(i * T, T), T)
+        x_t[:, part] = x[part, :].T
+        dy_t[:, part] = dy[part, :].T
+        return carry
+
+    lax.fori_loop(0, x.shape[0] // T, turn, 0)
+
+
+def feed_chunk(read, write, blocks, out, d_x, x, x_t, dy, dy_t, hidden, d_gate, d_up):
+    rows, width = x.shape
     row_block = min(rows, 256)
-    width = x.shape[1]
-    width_block = 512
-
-    @pl.when(step == 0)
-    def _():
-        load_x = pltpu.make_async_copy(x_hbm, x, sem.at[0])
-        load_dy = pltpu.make_async_copy(dy_hbm, dy, sem.at[1])
-        load_x.start()
-        load_dy.start()
-        load_x.wait()
-        load_dy.wait()
-
-        def turn(i, carry):
-            part = pl.ds(pl.multiple_of(i * T, T), T)
-            x_t[:, part] = x[part, :].T
-            dy_t[:, part] = dy[part, :].T
-            return carry
-
-        lax.fori_loop(0, rows // T, turn, 0)
-        out_sum[...] = jnp.zeros_like(out_sum)
-        d_x_sum[...] = jnp.zeros_like(d_x_sum)
-
-    w_gate, w_up, w_down = [
-        jnp.concatenate([weights[0, 0, i], weights[0, 1, i]], axis=1) for i in range(3)
-    ]
+    width_block = width // blocks
+    w_gate, w_up, w_down = [jnp.concatenate([read(0, i), read(1, i)], axis=1) for i in range(3)]
 
     def by_rows(i, carry):
         part = pl.ds(pl.multiple_of(i * row_block, row_block), row_block)
@@ -643,8 +620,8 @@
         hidden[part, :] = hidden_low
         d_gate[part, :] = d_gate_low
         d_up[part, :] = d_up_low
-        out_sum[part, :] += nt(hidden_low, w_down)
-        d_x_sum[part, :] += nt(d_gate_low, w_gate) + nt(d_up_low, w_up)
+        out[part, :] += nt(hidden_low, w_down)
+        d_x[part, :] += nt(d_gate_low, w_gate) + nt(d_up_low, w_up)
         return carry
 
     lax.fori_loop(0, rows // row_block, by_rows, 0)
@@ -654,16 +631,43 @@
         pairs = ((x_t, d_gate), (x_t, d_up), (dy_t, hidden))
         for index, (left, right) in enumerate(pairs):
             total = nn(left[part, :], right[...]).astype(BF)
-            grads[0, 0, index, part, :] = total[:, :T]
-            grads[0, 1, index, part, :] = total[:, T:]
+            write(0, index, i, total[:, :T])
+            write(1, index, i, total[:, T:])
         return carry
 
-    lax.fori_loop(0, width // width_block, by_width, 0)
-
-    @pl.when(step == pl.num_programs(0) - 1)
+    lax.fori_loop(0, blocks, by_width, 0)
+
+
+def feed_kernel(x_hbm, dy_hbm, weights, out, d_x, grads, x, x_t, dy, dy_t, *rest):
+    *work, sem = rest
+    width_block = 512
+
+    @pl.when(pl.program_id(0) == 0)
     def _():
-        out[...] = out_sum[...]
-        d_x[...] = d_x_sum[...]
+        feed_load(x_hbm, dy_hbm, x, x_t, dy, dy_t, sem)
+        out[...] = jnp.zeros_like(out)
+        d_x[...] = jnp.zeros_like(d_x)
+
+    def write(half, index, block, value):
+        part = pl.ds(pl.multiple_of(block * width_block, width_block), width_block)
+        grads[0, half, index, part, :] = value
+
+    read = lambda half, index: weights[0, half, index]
+    blocks = x.shape[1] // width_block
+    feed_chunk(read, write, blocks, out, d_x, x, x_t, dy, dy_t, *work)
+
+
+def feed_scratch(rows, width):
+    return [
+        pltpu.VMEM((rows, width), BF),
+        pltpu.VMEM((width, rows), BF),
+        pltpu.VMEM((rows, width), BF),
+        pltpu.VMEM((width, rows), BF),
+        pltpu.VMEM((rows, 2 * T), BF),
+        pltpu.VMEM((rows, 2 * T), BF),
+        pltpu.VMEM((rows, 2 * T), BF),
+        pltpu.SemaphoreType.DMA((2,)),
+    ]
 
 
 def feed(x, dy, weights):
@@ -681,20 +685,150 @@
             jax.ShapeDtypeStruct((rows, width), F32),
             jax.ShapeDtypeStruct((chunks, 2, 3, width, T), BF),
         ],
-        scratch_shapes=[
-            pltpu.VMEM((rows, width), BF),
-            pltpu.VMEM((width, rows), BF),
-            pltpu.VMEM((rows, width), BF),
-            pltpu.VMEM((width, rows), BF),
-            pltpu.VMEM((rows, width), F32),
-            pltpu.VMEM((rows, width), F32),
-            pltpu.VMEM((rows, 2 * T), BF),
-            pltpu.VMEM((rows, 2 * T), BF),
-            pltpu.VMEM((rows, 2 * T), BF),
-            pltpu.SemaphoreType.DMA((2,)),
-        ],
+        scratch_shapes=feed_scratch(rows, width),
         compiler_params=pltpu.CompilerParams(vmem_limit_bytes=VMEM_LIMIT),
     )(x, dy, weights)
+
+
+def feed_moving_kernel(zs, xs, early, kept, *refs):
+    x_hbm, dy_hbm, own, ready, out, d_x, whole, parts, sums = refs[:9]
+    x, x_t, dy, dy_t, hidden, d_gate, d_up, sem = refs[9:17]
+    held, w_buf, g_buf, local = refs[17:21]
+    gather_sems, bufs, scatter_sems = refs[21:23], refs[23:30], refs[30:32]
+    chunks = own.shape[0]
+    place = Place(zs, xs)
+    step = pl.program_id(0)
+    lag = max(0, 5 - early)
+    first_kept, end_kept = kept
+    width = x.shape[1]
+
+    @pl.when(step == 0)
+    def _():
+        place.barrier()
+
+    fetch = Gather(place, own, whole, *gather_sems)
+    fetch.tick(step, early, chunks)
+
+    @pl.when(step == 0)
+    def _():
+        load = pltpu.make_async_copy(own, held, local.at[0])
+        load.start()
+        load.wait()
+        mine = whole.at[:, :, :, place.z, place.y, place.c * place.xs + place.x]
+        store = pltpu.make_async_copy(held, mine, local.at[1])
+        store.start()
+        store.wait()
+        feed_load(x_hbm, dy_hbm, x, x_t, dy, dy_t, sem)
+        out[...] = jnp.zeros_like(out)
+        d_x[...] = jnp.zeros_like(d_x)
+
+    def weight_load(j, source):
+        return pltpu.make_async_copy(source.at[j], w_buf.at[j % 2], local.at[2 + j % 2])
+
+    def start_load(j):
+        if early > 0:
+
+            @pl.when(j < early)
+            def _():
+                weight_load(j, ready).start()
+
+        @pl.when(j >= early)
+        def _():
+            weight_load(j, whole).start()
+
+    def part_store(j):
+        return pltpu.make_async_copy(g_buf.at[j % 2], parts.at[j], local.at[4 + j % 2])
+
+    def is_kept(j):
+        return (j >= first_kept) & (j < end_kept)
+
+    engine = Scatter(place, bufs, *scatter_sems, sums)
+    due = lag + first_kept
+    number = end_kept - first_kept
+    grads_of = lambda k: g_buf.at[(k + first_kept) % 2]
+    staged(step, due + 5, number, engine.finish)
+    staged(step, due + 4, number, engine.start_fourth)
+    staged(step, due + 3, number, engine.start_third)
+    staged(step, due + 2, number, lambda k: engine.start_second(k, grads_of(k)))
+    staged(step, due + 1, number, lambda k: engine.start_first(k, grads_of(k)))
+
+    chunk = step - lag
+    if lag == 0:
+
+        @pl.when(step == 0)
+        def _():
+            start_load(0)
+
+    @pl.when((chunk >= (0 if lag == 0 else -1)) & (chunk + 1 < chunks))
+    def _():
+        start_load(chunk + 1)
+
+    @pl.when((chunk >= 2) & (chunk < chunks + 2) & ~is_kept(chunk - 2))
+    def _():
+        part_store(chunk - 2).wait()
+
+    @pl.when((chunk >= 0) & (chunk < chunks))
+    def _():
+        weight_load(chunk, whole).wait()
+        slot = chunk % 2
+
+        def read(half, index):
+            return w_buf[slot, half, index].reshape(width, T)
+
+        def write(half, index, block, value):
+            shape = g_buf.shape[4:]
+            g_buf[slot, half, index, block] = value.reshape(shape)
+
+        work = (hidden, d_gate, d_up)
+        feed_chunk(read, write, zs, out, d_x, x, x_t, dy, dy_t, *work)
+
+        @pl.when(~is_kept(chunk))
+        def _():
+            part_store(chunk).start()
+
+
+def feed_moving(x, dy, own, ready, sizes, early, kept, collective_id):
+    grp, seq = sizes
+    rows, width = x.shape
+    chunks, _, n, shard, lanes = own.shape
+    zs = grp // (Y * C)
+    tile = (2, n, zs, Y, C * seq, shard, lanes)
+    whole = pl.BlockSpec((rows, width), lambda j: (0, 0), pipeline_mode=pl.Buffered(1))
+    number = kept[1] - kept[0]
+    sums = pl.BlockSpec(
+        (number, 2, n, shard, lanes), lambda j: (0,) * 5, pipeline_mode=pl.Buffered(1)
+    )
+    lag = max(0, 5 - early)
+    steps = lag + max(chunks + 2, kept[1] + 5)
+    anywhere = pl.BlockSpec(memory_space=pl.ANY)
+    sems = lambda *shape: pltpu.SemaphoreType.DMA(shape)
+    return pl.pallas_call(
+        functools.partial(feed_moving_kernel, zs, seq, early, kept),
+        grid=(steps,),
+        in_specs=[anywhere] * 4,
+        out_specs=[whole, whole, anywhere, anywhere, sums],
+        out_shape=[
+            jax.ShapeDtypeStruct((rows, width), F32),
+            jax.ShapeDtypeStruct((rows, width), F32),
+            jax.ShapeDtypeStruct((chunks, *tile), BF),
+            jax.ShapeDtypeStruct((chunks, *tile), BF),
+            jax.ShapeDtypeStruct((number, 2, n, shard, lanes), F32),
+        ],
+        scratch_shapes=feed_scratch(rows, width)
+        + [
+            pltpu.VMEM(own.shape, BF),
+            pltpu.VMEM((2, *tile), BF),
+            pltpu.VMEM((2, *tile), BF),
+            sems(6),
+            sems(chunks, 2, zs + 2),
+            sems(chunks, 2, zs + 2),
+        ]
+        + scatter_buffers(n, zs, seq, shard, lanes)
+        + [sems(2, 2, zs + 2), sems(2, 2, zs + 2)],
+        compiler_params=pltpu.CompilerParams(
+            collective_id=collective_id, has_side_effects=True, vmem_limit_bytes=VMEM_LIMIT
+        ),
+    )(x, dy, own, ready)
 
 
 def rms_scale(values):
@@ -778,7 +912,6 @@
     ]
     gain_one = flat[4 * count, :, 0].astype(F32)
     gain_two = flat[4 * count, :, 1].astype(F32)
-    feed_whole = gather(own_feed, sizes, 1)
 
     scale_one = rms_scale(x)
     unit_one = x * scale_one
@@ -807,7 +940,16 @@
     unit_two = middle * scale_two
     normed_two = (unit_two * gain_two).astype(BF)
 
-    out_sum, d_normed_two, feed_grads = feed(normed_two, dy_low, feed_whole)
+    moving = can_move(sizes, shard)
+    if moving:
+        kept = (0, own_feed.shape[0])
+        out_sum, d_normed_two, _, _, feed_sums = feed_moving(
+            normed_two, dy_low, own_feed, own_feed, sizes, 0, kept, 1
+        )
+    else:
+        feed_whole = gather(own_feed, sizes, 1)
+        out_sum, d_normed_two, feed_grads = feed(normed_two, dy_low, feed_whole)
+        feed_sums = scatter(feed_grads, sizes, shard, 3)
     final = (middle + out_sum).astype(BF)
 
     d_gain_two = jnp.sum(d_normed_two * unit_two, axis=0)
@@ -849,12 +991,10 @@
     d_x = d_x.astype(BF)
 
     attention_parts = attention_chunks([d_q, d_kv_weight, d_o]).astype(BF)
-    parts = jnp.concatenate([feed_grads, attention_parts], axis=0)
-    sums = scatter(parts, sizes, shard, 2)
-    feed_sums = sums[: feed_grads.shape[0]].reshape(-1, 3, shard, T)
+    attention_sums = scatter(attention_parts, sizes, shard, 2).reshape(-1, shard, T)
+    feed_sums = feed_sums.reshape(-1, 3, shard, T)
     feed_sums = feed_sums[: hidden_width // T]
     gate_grad, up_grad, down_grad = [joined(feed_sums[:, i]) for i in range(3)]
-    attention_sums = sums[feed_grads.shape[0] :].reshape(-1, shard, T)
     q_grad, k_grad, v_grad, o_grad = [
         joined(attention_sums[i * count : (i + 1) * count]) for i in range(4)
     ]

time: 1080 us -> 881 us (0.82)
  Pallas kernels: 785 us -> 615 us
  other arithmetic: 75.6 us -> 45.5 us
    pallas_call x1, Pallas kernels: 165 us -> 351 us  [feed_moving(): pl.pallas_call(functools.partial(feed_moving_kernel, zs, seq, early, kept...]
    pallas_call x1, Pallas kernels: 238 us -> 57.5 us  [scatter(): pl.pallas_call(functools.partial(scatter_kernel, zs, seq, chunks), grid=(...]
    pallas_call x2 -> x1, Pallas kernels: 247 us -> 71 us  [gather(): pl.pallas_call(functools.partial(gather_kernel, zs, seq), grid=(chunks +...]
    concatenate x1 -> x0, other arithmetic: 31.7 us -> none  [body(): parts = jnp.concatenate([feed_grads, attention_parts], axis=0)]
  transfers between devices with their start and end apart: 2 -> 2, of which waited for: 1 -> 0; matrix products, arithmetic and copies ran while one was open for 6% -> 8% of each run, Pallas kernels for 16% -> 0%
where the time goes in v2:
time: 881 us; the launch traced here: 870 us
  Pallas kernels  615 us (70%)
  local copies, waits for them, and re-layouts  92.5 us (10%)
  matrix products  73.4 us (8%)
  other arithmetic  45.5 us (5%)
  blocking collectives  39.6 us (4%)
    pallas_call x1, Pallas kernels, feed_moving(): pl.pallas_call(functools.partial(feed_moving_kernel, zs, seq, early, kept...  351 us
    pallas_call x1, Pallas kernels, attend_back(): pl.pallas_call(functools.partial(attend_back_kernel, tiles, local_tiles,...  79.5 us
    pallas_call x1, Pallas kernels, gather(): pl.pallas_call(functools.partial(gather_kernel, zs, seq), grid=(chunks +...  71 us
    pallas_call x1, Pallas kernels, scatter(): pl.pallas_call(functools.partial(scatter_kernel, zs, seq, chunks), grid=(...  57.5 us
    pallas_call x1, Pallas kernels, attend(): pl.pallas_call(functools.partial(attend_kernel, tiles, local_tiles, conts...  56.5 us
    unnamed x1, blocking collectives  39.6 us
    dot_general x3, matrix products, nt(): lax.dot_general(left, right, (((1,), (1,)), ((), ())), preferred_element_...  24.1 us
    slice x5, local copies, waits for them, and re-layouts, body(): flat[i * count:(i + 1) * count]  21.9 us
  transfers between devices with their start and end apart: 2, of which 0 were waited for; matrix products, arithmetic and copies ran while one was open for 8% of the time, Pallas kernels for 0%

profile of v2, /device:TPU:0, one launch (start us, length us, event | category | flops | bytes accessed | tf_op | source)
XLA Modules:
  0.0 870.0 jit_solution(3226507222549065455)
XLA Ops:
  6.3 71.0 %shard_map.254 = bf16[5,2,3,4,2,4,48,128]{7,6,5,4,3,2,1,0:T(8,128)(2,1)} custom-call(bf16[5,2,3,48,128]{4,3,2,1,0:T(8,128)(2,1)} %bitcast.170), custom_call_target="tpu_custom_call" | custom-call | tf_op jit(solution)/shard_map/pallas_call | solution.py:197
  77.3 6.6 fusion.40
  94.0 8.4 convolution_convert_fusion.1
  111.0 4.9 fusion.1
  115.9 6.0 copy.107
  137.6 5.6 convolution_convert_fusion.5.q
  147.6 56.5 %shard_map.255 = (bf16[1024,768]{1,0:T(8,128)(2,1)}, f32[12,1024,1]{2,1,0:T(8,128)}) custom-call(s32[1,4]{1,0:T(1,128)} %live.3, s32[2]{0:T(128)} %pad_add_fusion.base, bf16[1024,768]{1,0:T(8,128)(2,1)} %convolution_convert_fusion.5.q, bf16[1536,768]{1,0:T(8,128)(2,1)} %get-tuple-element.50.k, bf16[1536,768]{1,0:T(8,128)(2,1)} %get-tuple-element.49.v, ...), custom_call_target="tpu_custom_call" | custom-call | tf_op jit(solution)/shard_map/pallas_call | solution.py:437
  204.2 5.8 multiply_reduce_fusion.2
  213.6 350.9 %shard_map.256 = (f32[1024,1536]{1,0:T(8,128)}, f32[1024,1536]{1,0:T(8,128)}, bf16[16,2,3,4,2,4,48,128]{7,6,5,4,3,2,1,0:T(8,128)(2,1)}, bf16[16,2,3,4,2,4,48,128...) custom-call(bf16[1024,1536]{1,0:T(8,128)(2,1)} %multiply_convert_fusion.refs_0_, ...), custom_call_target="tpu_custom_call" | custom-call | tf_op jit(solution)/shard_map/pallas_call | solution.py:805
  564.5 7.0 multiply_reduce_fusion
  572.8 6.4 multiply_add_fusion
  579.2 7.3 convolution_convert_fusion.4.grad
  590.4 79.5 %shard_map.257 = (bf16[1024,768]{1,0:T(8,128)(2,1)}, bf16[1536,768]{1,0:T(8,128)(2,1)}, bf16[1536,768]{1,0:T(8,128)(2,1)}, f32[12,5,128,128]{3,2,1,0:T(8,128)}) custom-call(s32[1,4]{1,0:T(1,128)} %live.3, s32[2]{0:T(128)} %pad_add_fusion.base, bf16[1024,768]{1,0:T(8,128)(2,1)} %convolution_convert_fusion.5.q, bf16[1536,768]{1,0:T(8,128)(2,1)} %get-tuple-element.50.k, ...), custom_call_target="tpu_custom_call" | custom-call | tf_op jit(solution)/shard_map/pallas_call | solution.py:547
  677.5 4.4 convolution_convert_fusion.3
  692.5 6.1 copy.118
  701.4 7.4 fusion.19
  713.4 7.4 convolution_convert_fusion
  720.8 7.0 fusion.16
  727.8 6.6 copy.112
  734.4 8.3 pad_maximum_fusion
  742.7 57.5 %shard_map.258 = f32[4,2,3,48,128]{4,3,2,1,0:T(8,128)} custom-call(bf16[4,2,3,4,2,4,48,128]{7,6,5,4,3,2,1,0:T(8,128)(2,1)} %bitcast.118), custom_call_target="tpu_custom_call" | custom-call | tf_op jit(solution)/shard_map/pallas_call | solution.py:364
  802.9 11.3 %fusion.12 = (f32[1536]{0:T(1024)}, f32[1024]{0:T(1024)}, f32[1024,1536]{1,0:T(8,128)}) fusion(f32[1024]{0:T(1024)} %copy-done.32, bf16[512,1536]{1,0:T(8,128)(2,1)} %bitcast.137, bf16[512,1536]{1,0:T(8,128)(2,1)} %bitcast.145, f32[1536]{0:T(1024)S(1)} %convert_reduce_fusion.1, f32[1024,1536]{1,0:T(8,128)} %fusion.16, ...), kind=kOutput, calls=%fused_computation.18 | convolution fusion | flops 2433218048 | bytes 19681280 | tf_op jit(solution)/shard_map/dot_general | solution.py:29
  814.2 39.6 %all-reduce.4 = (f32[1536]{0:T(1024)}, f32[32,12]{0,1:T(8,128)}, f32[1536]{0:T(1024)}) all-reduce(f32[1536]{0:T(1024)} %get-tuple-element.34, f32[32,12]{0,1:T(8,128)S(1)} %fusion.19, f32[1536]{0:T(1024)} %get-tuple-element.32), channel_id=2, replica_groups=mesh['grp'=16,'seq'=2] {'grp','seq'}, use_global_device_ids=true, to_apply=%region_5.6.clone | all-reduce | flops 3456 | bytes 27648
  860.5 6.3 fusion.11
  (155 shorter events, 90.4 us)
Async XLA Ops:
  0.6 110.4 %copy-start = (f32[32,12]{0,1:T(8,128)S(1)}, f32[32,12]{0,1:T(8,128)}, u32[]{:S(2)}) copy-start(f32[32,12]{0,1:T(8,128)} %param.25) | copy-start | bytes 4612
  3.4 709.9 %copy-start.32 = (f32[1024]{0:T(1024)}, f32[1024]{0:T(1024)S(1)}, u32[]{:S(2)}) copy-start(f32[1024]{0:T(1024)S(1)} %add_rsqrt_fusion.1) | copy-start | bytes 12292
  104.3 38.9 %collective-permute-start = (bf16[512,1536]{1,0:T(8,128)(2,1)}, bf16[512,1536]{1,0:T(8,128)(2,1)}, u32[]{:S(2)}, u32[]{:S(2)}) collective-permute-start(bf16[512,1536]{1,0:T(8,128)(2,1)} %get-tuple-element.55), channel_id=1, source_target_pairs={{0,1},{1,0},{2,3},{3,2},{4,5},{5,4},{6,7},{7,6},{8,9},{9,8},{10,11... | collective-permute-start | bytes 4718600 | tf_op jit(solution)/shard_map/ppermute | solution.py:923
  124.4 4.6 copy-start.27
  137.6 5.6 copy-start.9
  564.4 7.1 slice-start
  564.4 7.1 slice-start.1
  564.4 8.3 copy-start.4
  579.2 7.3 copy-start.3
  579.2 7.3 copy-start.25
  672.4 4.1 copy-start.15
  672.4 5.1 copy-start.33
  676.3 34.8 %collective-permute-start.1 = (bf16[512,1536]{1,0:T(8,128)(2,1)}, bf16[512,1536]{1,0:T(8,128)(2,1)}, u32[]{:S(2)}, u32[]{:S(2)}) collective-permute-start(bf16[512,1536]{1,0:T(8,128)(2,1)} %get-tuple-element.47), channel_id=1, source_target_pairs={{0,1},{1,0},{2,3},{3,2},{4,5},{5,4},{6,7},{7,6},{8,9},{9,8},{10,11... | collective-permute-start | bytes 4718600 | tf_op jit(solution)/shard_map/ppermute | solution.py:979
  677.5 4.4 copy-start.24
  701.4 7.4 copy-start.18
  701.4 7.4 copy-start.19
  708.8 4.5 copy-start.12
  708.8 4.5 copy-start.16
  708.9 4.5 copy-start.26
  713.4 7.4 copy-start.21
  713.4 7.4 copy-start.22
  802.9 57.5 %copy-start.13 = (bf16[1,4,128,1536]{3,2,1,0:T(8,128)(2,1)S(1)}, bf16[1,4,128,1536]{3,2,1,0:T(8,128)(2,1)}, u32[]{:S(2)}) copy-start(bf16[1,4,128,1536]{3,2,1,0:T(8,128)(2,1)} %param.16) | copy-start | bytes 4718596
  802.9 57.5 %copy-start.17 = (bf16[1,512,1536]{2,1,0:T(8,128)(2,1)S(1)}, bf16[1,512,1536]{2,1,0:T(8,128)(2,1)}, u32[]{:S(2)}) copy-start(bf16[1,512,1536]{2,1,0:T(8,128)(2,1)} %param.15) | copy-start | bytes 4718596
  860.5 6.3 copy-start.5
  (16 other events, 51.1 us)

commit v3 on v2

--- a/solution.py
+++ b/solution.py
@@ -48,7 +48,8 @@
 
 
 def can_move(sizes, rows):
-    return rows % 16 == 0 and sizes[1] == 2 and sizes[0] % (Y * C) == 0 and sizes[0] > Y * C
+    zs = sizes[0] // (Y * C)
+    return rows % 16 == 0 and sizes[1] == 2 and sizes[0] % (Y * C) == 0 and zs in (2, 4, 8, 16)
 
 
 class Place:
@@ -379,73 +380,102 @@
     )(view)
 
 
+class Shape:
+    def __init__(self, tiles, local_tiles, conts):
+        self.tiles, self.local_tiles, self.conts = tiles, local_tiles, conts
+        self.rows = (local_tiles + conts) * T
+        self.keys = self.rows + (tiles - local_tiles) * T
+        self.parts = [(0, range(local_tiles)), (self.rows, range(local_tiles, tiles))]
+        self.parts = [(start, js) for start, js in self.parts if len(js)]
+
+
 def band_of(key_tile, query_tile):
     return jnp.clip(key_tile - query_tile, -2, 2) + 2
 
 
-def attend_kernel(tiles, local_tiles, conts, live, base, q, k, v, bias, out, norm):
+def tile_lanes():
     first_half = lax.broadcasted_iota(jnp.int32, (T, 2 * HEAD), 1) < HEAD
     place = lax.broadcasted_iota(jnp.int32, (T, T), 1)
-
-    def tile(i, is_cont):
-        rows = pl.ds(pl.multiple_of(i * T, T), T)
-        queries = q[rows, :]
-        query_tile = tiles if is_cont else base[0] + i
-        cont = i - local_tiles
-        cont_keys = pl.ds(pl.multiple_of((tiles + cont) * T, T), T)
-        mixed = []
-        for h in range(2):
-            mine = first_half if h == 0 else ~first_half
-            masked = jnp.where(mine, queries, jnp.zeros_like(queries))
-            scores = nt(masked, k[0 : tiles * T, :])
-            parts = []
-            for j in range(tiles):
-                band = band_of(lax.rem(base[1] + j, tiles), query_tile)
-                parts.append(scores[:, j * T : (j + 1) * T] + bias[h, band])
-            if is_cont:
-                own = nt(masked, k[cont_keys, :]) + bias[h, 2]
-                parts.append(jnp.where(place < live[0, cont], own, NEGATIVE))
-            top = jnp.max(functools.reduce(jnp.maximum, parts), axis=1, keepdims=True)
-            weights = [jnp.exp(part - top) for part in parts]
-            total = jnp.sum(functools.reduce(jnp.add, weights), axis=1, keepdims=True)
-            inverse = 1.0 / total
-            probs = [(weight * inverse).astype(BF) for weight in weights]
-            result = nn(jnp.concatenate(probs[:tiles], axis=1), v[0 : tiles * T, :])
-            if is_cont:
-                result = result + nn(probs[tiles], v[cont_keys, :])
-            mixed.append(result)
-            norm[h, rows, :] = top + jnp.log(total)
-        out[rows, :] = jnp.where(first_half, mixed[0], mixed[1]).astype(BF)
-
-    def prompt_tile(i, carry):
-        tile(i, False)
+    return first_half, place
+
+
+def tile_rows(i):
+    return pl.ds(pl.multiple_of(i * T, T), T)
+
+
+def attend_tile(shape, i, is_cont, live, base, q, k, v, bias, out, norm):
+    first_half, place = tile_lanes()
+    rows = tile_rows(i)
+    queries = q[rows, :]
+    query_tile = shape.tiles if is_cont else base + i
+    mixed = []
+    for h in range(2):
+        mine = first_half if h == 0 else ~first_half
+        masked = jnp.where(mine, queries, jnp.zeros_like(queries))
+        logits = []
+        for start, js in shape.parts:
+            scores = nt(masked, k[start : start + len(js) * T, :])
+            for at, j in enumerate(js):
+                band = band_of(lax.rem(base + j, shape.tiles), query_tile)
+                logits.append(scores[:, at * T : (at + 1) * T] + bias[h, band])
+        if is_cont:
+            own = nt(masked, k[rows, :]) + bias[h, 2]
+            logits.append(jnp.where(place < live[0, i - shape.local_tiles], own, NEGATIVE))
+        top = jnp.max(functools.reduce(jnp.maximum, logits), axis=1, keepdims=True)
+        weights = [jnp.exp(part - top) for part in logits]
+        total = jnp.sum(functools.reduce(jnp.add, weights), axis=1, keepdims=True)
+        inverse = 1.0 / total
+        probs = [(weight * inverse).astype(BF) for weight in weights]
+        result = None
+        for start, js in shape.parts:
+            left = jnp.concatenate([probs[j] for j in js], axis=1)
+            term = nn(left, v[start : start + len(js) * T, :])
+            result = term if result is None else result + term
+        if is_cont:
+            result = result + nn(probs[shape.tiles], v[rows, :])
+        mixed.append(result)
+        norm[h, rows, :] = top + jnp.log(total)
+    out[rows, :] = jnp.where(first_half, mixed[0], mixed[1]).astype(BF)
+
+
+def for_tiles(shape, conts, action):
+    first, last = (shape.local_tiles, shape.local_tiles + shape.conts) if conts else (0, shape.local_tiles)
+
+    def one(i, carry):
+        action(i, conts)
         return carry
 
-    def cont_tile(i, carry):
-        tile(i, True)
-        return carry
-
-    lax.fori_loop(0, local_tiles, prompt_tile, 0)
-    lax.fori_loop(local_tiles, local_tiles + conts, cont_tile, 0)
-
-
-def attend(q, k, v, bias, live, base, tiles, local_tiles, conts):
+    lax.fori_loop(first, last, one, 0)
+
+
+def attend_kernel(shape, live, base, q, k, v, bias, out, norm):
+    for conts in (False, True):
+        for_tiles(
+            shape,
+            conts,
+            lambda i, c: attend_tile(shape, i, c, live, base[0], q, k, v, bias, out, norm),
+        )
+
+
+def pair_block(n):
+    return pl.BlockSpec((n, 2 * HEAD), lambda h, *_: (0, h))
+
+
+def attend(q, k, v, bias, live, base, shape):
     rows, width = q.shape
-    keys = k.shape[0]
     pairs = width // (2 * HEAD)
-    block = lambda n: pl.BlockSpec((n, 2 * HEAD), lambda h, *_: (0, h))
     return pl.pallas_call(
-        functools.partial(attend_kernel, tiles, local_tiles, conts),
+        functools.partial(attend_kernel, shape),
         grid_spec=pltpu.PrefetchScalarGridSpec(
             num_scalar_prefetch=2,
             grid=(pairs,),
             in_specs=[
-                block(rows),
-                block(keys),
-                block(keys),
+                pair_block(rows),
+                pair_block(shape.keys),
+                pair_block(shape.keys),
                 pl.BlockSpec((2, BANDS, T, T), lambda h, *_: (h, 0, 0, 0)),
             ],
-            out_specs=[block(rows), pl.BlockSpec((2, rows, 1), lambda h, *_: (h, 0, 0))],
+            out_specs=[pair_block(rows), pl.BlockSpec((2, rows, 1), lambda h, *_: (h, 0, 0))],
         ),
         out_shape=[
             jax.ShapeDtypeStruct((rows, width), BF),
@@ -455,110 +485,87 @@
     )(live, base, q, k, v, bias)
 
 
+def attend_back_tile(
+    shape, i, is_cont, live, base, q, k, v, bias, grad, out, norm, d_q, d_bias, k_sum, v_sum
+):
+    first_half, place = tile_lanes()
+    rows = tile_rows(i)
+    queries = q[rows, :]
+    grads = grad[rows, :]
+    query_tile = shape.tiles if is_cont else base + i
+    overlap = grads.astype(F32) * out[rows, :].astype(F32)
+    mixed = []
+    for h in range(2):
+        mine = first_half if h == 0 else ~first_half
+        masked = jnp.where(mine, queries, jnp.zeros_like(queries))
+        masked_grad = jnp.where(mine, grads, jnp.zeros_like(grads))
+        inner = jnp.sum(jnp.where(mine, overlap, 0.0), axis=1, keepdims=True)
+        log_norm = norm[h, rows, :]
+
+        def piece(keys, bands, allowed):
+            scores = nt(masked, k[keys, :])
+            d_probs = nt(masked_grad, v[keys, :])
+            probs_low, scores_low = [], []
+            for at, band in enumerate(bands):
+                cols = slice(at * T, (at + 1) * T)
+                logits = scores[:, cols] + bias[h, band]
+                if allowed is not None:
+                    logits = jnp.where(allowed, logits, NEGATIVE)
+                probs = jnp.exp(logits - log_norm)
+                d_scores = probs * (d_probs[:, cols] - inner)
+                d_bias[h, band] += d_scores
+                probs_low.append(probs.astype(BF))
+                scores_low.append(d_scores.astype(BF))
+            probs_low = jnp.concatenate(probs_low, axis=1)
+            scores_low = jnp.concatenate(scores_low, axis=1)
+            v_sum[keys, :] += tn(probs_low, masked_grad)
+            k_sum[keys, :] += tn(scores_low, masked)
+            return nn(scores_low, k[keys, :])
+
+        result = None
+        for start, js in shape.parts:
+            bands = [band_of(lax.rem(base + j, shape.tiles), query_tile) for j in js]
+            term = piece(pl.ds(start, len(js) * T), bands, None)
+            result = term if result is None else result + term
+        if is_cont:
+            result = result + piece(rows, [2], place < live[0, i - shape.local_tiles])
+        mixed.append(result)
+    d_q[rows, :] = jnp.where(first_half, mixed[0], mixed[1]).astype(BF)
+
+
 def attend_back_kernel(
-    tiles,
-    local_tiles,
-    conts,
-    live,
-    base,
-    q,
-    k,
-    v,
-    bias,
-    grad,
-    out,
-    norm,
-    d_q,
-    d_k,
-    d_v,
-    d_bias,
-    k_sum,
-    v_sum,
+    shape, live, base, q, k, v, bias, grad, out, norm, d_q, d_k, d_v, d_bias, k_sum, v_sum
 ):
-    first_half = lax.broadcasted_iota(jnp.int32, (T, 2 * HEAD), 1) < HEAD
-    place = lax.broadcasted_iota(jnp.int32, (T, T), 1)
     k_sum[...] = jnp.zeros_like(k_sum)
     v_sum[...] = jnp.zeros_like(v_sum)
     d_bias[...] = jnp.zeros_like(d_bias)
-
-    def tile(i, is_cont):
-        rows = pl.ds(pl.multiple_of(i * T, T), T)
-        queries = q[rows, :]
-        grads = grad[rows, :]
-        query_tile = tiles if is_cont else base[0] + i
-        overlap = grads.astype(F32) * out[rows, :].astype(F32)
-        mixed = []
-        for h in range(2):
-            mine = first_half if h == 0 else ~first_half
-            masked = jnp.where(mine, queries, jnp.zeros_like(queries))
-            masked_grad = jnp.where(mine, grads, jnp.zeros_like(grads))
-            inner = jnp.sum(jnp.where(mine, overlap, 0.0), axis=1, keepdims=True)
-            log_norm = norm[h, rows, :]
-
-            def piece(keys, bands, allowed):
-                scores = nt(masked, k[keys, :])
-                d_probs = nt(masked_grad, v[keys, :])
-                probs_low, scores_low = [], []
-                for j, band in enumerate(bands):
-                    cols = slice(j * T, (j + 1) * T)
-                    logits = scores[:, cols] + bias[h, band]
-                    if allowed is not None:
-                        logits = jnp.where(allowed, logits, NEGATIVE)
-                    probs = jnp.exp(logits - log_norm)
-                    d_scores = probs * (d_probs[:, cols] - inner)
-                    d_bias[h, band] += d_scores
-                    probs_low.append(probs.astype(BF))
-                    scores_low.append(d_scores.astype(BF))
-                probs_low = jnp.concatenate(probs_low, axis=1)
-                scores_low = jnp.concatenate(scores_low, axis=1)
-                v_sum[keys, :] += tn(probs_low, masked_grad)
-                k_sum[keys, :] += tn(scores_low, masked)
-                return nn(scores_low, k[keys, :])
-
-            bands = [band_of(lax.rem(base[1] + j, tiles), query_tile) for j in range(tiles)]
-            result = piece(pl.ds(0, tiles * T), bands, None)
-            if is_cont:
-                cont = i - local_tiles
-                cont_keys = pl.ds(pl.multiple_of((tiles + cont) * T, T), T)
-                result = result + piece(cont_keys, [2], place < live[0, cont])
-            mixed.append(result)
-        d_q[rows, :] = jnp.where(first_half, mixed[0], mixed[1]).astype(BF)
-
-    def prompt_tile(i, carry):
-        tile(i, False)
-        return carry
-
-    def cont_tile(i, carry):
-        tile(i, True)
-        return carry
-
-    lax.fori_loop(0, local_tiles, prompt_tile, 0)
-    lax.fori_loop(local_tiles, local_tiles + conts, cont_tile, 0)
+    refs = (q, k, v, bias, grad, out, norm, d_q, d_bias, k_sum, v_sum)
+    for conts in (False, True):
+        for_tiles(shape, conts, lambda i, c: attend_back_tile(shape, i, c, live, base[0], *refs))
     d_k[...] = k_sum[...].astype(BF)
     d_v[...] = v_sum[...].astype(BF)
 
 
-def attend_back(q, k, v, bias, grad, out, norm, live, base, tiles, local_tiles, conts):
+def attend_back(q, k, v, bias, grad, out, norm, live, base, shape):
     rows, width = q.shape
-    keys = k.shape[0]
     pairs = width // (2 * HEAD)
-    block = lambda n: pl.BlockSpec((n, 2 * HEAD), lambda h, *_: (0, h))
+    keys = shape.keys
     bands = pl.BlockSpec((2, BANDS, T, T), lambda h, *_: (h, 0, 0, 0))
     return pl.pallas_call(
-        functools.partial(attend_back_kernel, tiles, local_tiles, conts),
+        functools.partial(attend_back_kernel, shape),
         grid_spec=pltpu.PrefetchScalarGridSpec(
             num_scalar_prefetch=2,
             grid=(pairs,),
             in_specs=[
-                block(rows),
-                block(keys),
-                block(keys),
+                pair_block(rows),
+                pair_block(keys),
+                pair_block(keys),
                 bands,
-                block(rows),
-                block(rows),
+                pair_block(rows),
+                pair_block(rows),
                 pl.BlockSpec((2, rows, 1), lambda h, *_: (h, 0, 0)),
             ],
-            out_specs=[block(rows), block(keys), block(keys), bands],
+            out_specs=[pair_block(rows), pair_block(keys), pair_block(keys), bands],
             scratch_shapes=[pltpu.VMEM((keys, 2 * HEAD), F32), pltpu.VMEM((keys, 2 * HEAD), F32)],
         ),
         out_shape=[
@@ -569,6 +576,358 @@
         ],
         compiler_params=pltpu.CompilerParams(vmem_limit_bytes=VMEM_LIMIT),
     )(live, base, q, k, v, bias, grad, out, norm)
+
+
+SPAN = 4 * T
+VECTOR_ROWS = 8
+
+
+def turned(tile):
+    row = lax.broadcasted_iota(jnp.int32, tile.shape, 0)
+    for bit in range(7):
+        moved = pltpu.roll(tile, SPAN - (1 << bit), 1)
+        tile = jnp.where((row >> bit) & 1 == 1, moved, tile)
+    return tile
+
+
+def band_sums(d_bias, h):
+    near = jnp.concatenate([d_bias[h, 1], d_bias[h, 2], d_bias[h, 3]], axis=1)
+    near = jnp.concatenate([near, jnp.zeros((T, T), F32)], axis=1)
+    diagonal = jnp.sum(turned(near), axis=0, keepdims=True)
+    rows = [diagonal[:, i * T : (i + 1) * T] for i in range(4)]
+    rows += [jnp.sum(d_bias[h, band], axis=0, keepdims=True) for band in (0, 4)]
+    return jnp.concatenate(rows + [jnp.zeros((2, T), F32)], axis=0)
+
+
+def rows_of(vector):
+    return [vector[:, i * T : (i + 1) * T] for i in range(vector.shape[1] // T)]
+
+
+class Combine:
+    def __init__(self, place, total, arrived, send, recv):
+        self.p, self.total, self.arrived, self.send, self.recv = place, total, arrived, send, recv
+
+    def partners(self):
+        p = self.p
+        found = [p.device(c=1 - p.c), p.device(x=1 - p.x), p.device(y=1 - p.y)]
+        bit = 1
+        while bit < p.zs:
+            found.append(p.device(z=p.z + bit - 2 * bit * ((p.z // bit) % 2)))
+            bit *= 2
+        return found
+
+    def copy(self, i):
+        return remote(
+            self.total.at[i],
+            self.arrived.at[i],
+            self.send.at[i],
+            self.recv.at[i],
+            self.partners()[i],
+        )
+
+    def start(self, i):
+        self.copy(i).start()
+
+    def finish(self, i):
+        self.copy(i).wait_recv()
+        self.copy(i).wait_send()
+        self.total[i + 1] = self.total[i] + self.arrived[i]
+
+
+def back_kernel(zs, xs, shape, width, kept, live, *refs):
+    q, k, v, bias, grad, out, norm, attended, branch_hbm, normed_hbm, parts, weights_hbm = refs[:12]
+    d_middle, x_low, gain, d_gain_two = refs[12:16]
+    d_x, sums, vector_out = refs[16:19]
+    (stage, turn_buf, d_q, d_kv, back_kv, k_sum, v_sum, d_bias) = refs[19:27]
+    (w_buf, held, vector, total, arrived, gain_sum) = refs[27:33]
+    (local, loads, kv_sems, both_sems) = refs[33:37]
+    bufs, scatter_sems = refs[37:44], refs[44:46]
+    place = Place(zs, xs)
+    step = pl.program_id(0)
+    rows, keys = shape.rows, shape.keys
+    prompt = shape.local_tiles * T
+    pairs = d_q.shape[0]
+    last = 2 * pairs
+    turns = rows // T
+    first_kept, end_kept = kept
+    fed = parts.shape[0] - (end_kept - first_kept)
+    group_two = last - 1
+    count = fed + 4
+    blocks = rows // d_x.shape[0]
+
+    def stage_load(source):
+        return pltpu.make_async_copy(source, stage, local.at[0])
+
+    def weights_load(i):
+        return pltpu.make_async_copy(weights_hbm.at[i], w_buf.at[i], local.at[1 + i])
+
+    def turn():
+        def one(i, carry):
+            part = tile_rows(i)
+            turn_buf[:, part] = stage[part, :].T
+            return carry
+
+        lax.fori_loop(0, turns, one, 0)
+
+    @pl.when(step == 0)
+    def _():
+        stage_load(branch_hbm).start()
+        place.barrier()
+        for i in range(3):
+            weights_load(i).start()
+        stage_load(branch_hbm).wait()
+        turn()
+        stage_load(normed_hbm).start()
+
+    engine = Scatter(place, bufs, *scatter_sems, sums)
+
+    def due(offset, action):
+        at = step - offset
+        chunk = jnp.where(at < group_two, at, at - group_two + fed)
+        early = (at >= 0) & (at < fed)
+        late = (at >= group_two) & (at < group_two + 4)
+
+        @pl.when(early | late)
+        def _():
+            action(chunk)
+
+    def part_load(c):
+        j = jnp.where(c < first_kept, c, c + end_kept - first_kept)
+        return pltpu.make_async_copy(parts.at[j], held.at[c % 3], loads.at[c % 3])
+
+    def first(c):
+        @pl.when(c < fed)
+        def _():
+            part_load(c).wait()
+
+        engine.start_first(c, held.at[c % 3])
+
+    due(5, engine.finish)
+    due(4, engine.start_fourth)
+    due(3, engine.start_third)
+    due(2, lambda c: engine.start_second(c, held.at[c % 3]))
+    due(1, first)
+
+    @pl.when(step < fed)
+    def _():
+        part_load(step).start()
+
+    def kv_send(p):
+        src = d_kv.at[p, :, pl.ds(rows, keys - rows)]
+        peer = place.device(x=1 - place.x)
+        return remote(src, back_kv.at[p], kv_sems.at[0, p], kv_sems.at[1, p], peer)
+
+    @pl.when((step >= 2) & (step <= last) & (step % 2 == 0))
+    def _():
+        kv_send(step // 2 - 1).start()
+
+    @pl.when(step < last)
+    def _():
+        p = step // 2
+        half = step % 2
+
+        @pl.when(half == 0)
+        def _():
+            k_sum[...] = jnp.zeros_like(k_sum)
+            v_sum[...] = jnp.zeros_like(v_sum)
+            d_bias[...] = jnp.zeros_like(d_bias)
+
+        inputs = (q, k, v, bias, grad, out, norm, d_q.at[p], d_bias, k_sum, v_sum)
+        base = place.x * shape.local_tiles
+        action = lambda i, c: attend_back_tile(shape, i, c, live, base, *inputs)
+
+        @pl.when(half == 0)
+        def _():
+            for_tiles(shape, False, action)
+
+        @pl.when(half == 1)
+        def _():
+            for_tiles(shape, True, action)
+            d_kv[p, 0] = k_sum[...].astype(BF)
+            d_kv[p, 1] = v_sum[...].astype(BF)
+            for h in range(2):
+                vector[2 * p + h] = band_sums(d_bias, h)
+
+    def produce(c, right):
+        slot = c % 3
+        for m in range(3):
+            operand = right(m)
+
+            def one(z, carry, m=m, operand=operand):
+                block = turn_buf.shape[0] // zs
+                part = pl.ds(pl.multiple_of(z * block, block), block)
+                result = nn(turn_buf[part, :], operand).astype(BF)
+                for side in range(2):
+                    index = 2 * m + side
+                    value = result[:, side * T : (side + 1) * T]
+                    held[slot, index // 3, index % 3, z] = value.reshape(held.shape[4:])
+                return carry
+
+            lax.fori_loop(0, zs, one, 0)
+
+    @pl.when(step == last - 1)
+    def _():
+        produce(fed, lambda m: attended[:, 2 * m * T : 2 * (m + 1) * T])
+
+    @pl.when(step == last)
+    def _():
+        stage_load(normed_hbm).wait()
+        turn()
+        produce(fed + 1, lambda m: jnp.concatenate([d_q[2 * m], d_q[2 * m + 1]], axis=1))
+
+        def join(p, carry):
+            kv_send(p).wait_recv()
+            kv_send(p).wait_send()
+            for side in range(2):
+                own = d_kv[p, side, 0:prompt, :].astype(F32)
+                d_kv[p, side, 0:prompt, :] = (own + back_kv[p, side].astype(F32)).astype(BF)
+            return carry
+
+        lax.fori_loop(0, pairs, join, 0)
+        for i in range(3):
+            weights_load(i).wait()
+        gain_sum[...] = jnp.zeros_like(gain_sum)
+
+    for side in range(2):
+
+        @pl.when(step == last + 1 + side)
+        def _(side=side):
+            pick = lambda p: d_kv[p, side, 0:rows, :]
+            produce(fed + 2 + side, lambda m: jnp.concatenate([pick(2 * m), pick(2 * m + 1)], axis=1))
+
+    @pl.when((step >= last) & (step < last + blocks))
+    def _():
+        size = d_x.shape[0]
+        part = pl.ds(pl.multiple_of((step - last) * size, size), size)
+        d_normed = None
+        for i in range(3):
+            for m in range(pairs // 2):
+                if i == 0:
+                    left = [d_q[2 * m + e, part, :] for e in range(2)]
+                else:
+                    left = [d_kv[2 * m + e, i - 1, part, :] for e in range(2)]
+                pieces = [2 * m, 2 * m + 1]
+                right = [w_buf[i, j // 3, j % 3].reshape(width, T) for j in pieces]
+                term = nt(jnp.concatenate(left, axis=1), jnp.concatenate(right, axis=1))
+                d_normed = term if d_normed is None else d_normed + term
+        x = x_low[...].astype(F32)
+        scale = lax.rsqrt(jnp.mean(x * x, axis=-1, keepdims=True) + EPS)
+        unit = x * scale
+        gain_sum[...] += jnp.sum(d_normed * unit, axis=0, keepdims=True)
+        d_unit = d_normed * gain[...]
+        inner = jnp.mean(d_unit * unit, axis=-1, keepdims=True)
+        d_x[...] = (d_middle[...] + scale * (d_unit - unit * inner)).astype(BF)
+
+    mix = Combine(place, total, arrived, both_sems.at[0], both_sems.at[1])
+    start = last + blocks
+    stages = total.shape[0] - 1
+    tiles = 2 * pairs
+
+    @pl.when(step == start)
+    def _():
+        total[0, 0:tiles] = vector[...]
+        both = rows_of(gain_sum[...]) + rows_of(d_gain_two[...])
+        for i in range(len(both) // VECTOR_ROWS):
+            group = both[i * VECTOR_ROWS : (i + 1) * VECTOR_ROWS]
+            total[0, tiles + i] = jnp.concatenate(group, axis=0)
+
+    for i in range(stages + 1):
+
+        @pl.when(step == start + 1 + i)
+        def _(i=i):
+            if i > 0:
+                mix.finish(i - 1)
+            if i < stages:
+                mix.start(i)
+            else:
+                vector_out[...] = total[stages]
+
+
+def back(q, k, v, bias, grad, out, norm, branch, normed, parts, weights, d_middle, x_low, gain,
+         d_gain_two, live, shape, sizes, kept, collective_id):
+    grp, seq = sizes
+    rows, width = x_low.shape
+    inner = q.shape[1]
+    pairs = inner // (2 * HEAD)
+    zs = grp // (Y * C)
+    keys = shape.keys
+    chunks, _, n, _, _, _, shard, lanes = parts.shape
+    count = chunks - (kept[1] - kept[0]) + 4
+    assert chunks - (kept[1] - kept[0]) <= 2 * pairs - 1
+    assert (pairs, n) == (6, 3) and 2 * width // T % VECTOR_ROWS == 0
+    last = 2 * pairs
+    size = min(rows, 256)
+    blocks = rows // size
+    tile = (2, n, zs, Y, C * seq, shard, lanes)
+    stages = 3 + (zs - 1).bit_length()
+    steps = last + blocks + stages + 2
+    vector = (2 * pairs + 2 * width // T // VECTOR_ROWS, VECTOR_ROWS, T)
+    pair = lambda s: jnp.minimum(s // 2, pairs - 1)
+    by_pair = lambda rows_: pl.BlockSpec((rows_, 2 * HEAD), lambda s, *_: (0, pair(s)))
+    row_block = lambda s: jnp.clip(s - last, 0, blocks - 1)
+    by_rows = pl.BlockSpec((size, width), lambda s, *_: (row_block(s), 0))
+    full = lambda *dims: pl.BlockSpec(
+        dims, lambda s, *_: (0,) * len(dims), pipeline_mode=pl.Buffered(1)
+    )
+    anywhere = pl.BlockSpec(memory_space=pl.ANY)
+    sems = lambda *dims: pltpu.SemaphoreType.DMA(dims)
+    return pl.pallas_call(
+        functools.partial(back_kernel, zs, seq, shape, width, kept),
+        grid_spec=pltpu.PrefetchScalarGridSpec(
+            num_scalar_prefetch=1,
+            grid=(steps,),
+            in_specs=[
+                by_pair(rows),
+                by_pair(keys),
+                by_pair(keys),
+                pl.BlockSpec((2, BANDS, T, T), lambda s, *_: (pair(s), 0, 0, 0)),
+                by_pair(rows),
+                by_pair(rows),
+                pl.BlockSpec((2, rows, 1), lambda s, *_: (pair(s), 0, 0)),
+                full(rows, inner),
+                anywhere,
+                anywhere,
+                anywhere,
+                anywhere,
+                by_rows,
+                by_rows,
+                full(1, width),
+                full(1, width),
+            ],
+            out_specs=[by_rows, full(count, 2, n, shard, lanes), full(*vector)],
+            scratch_shapes=[
+                pltpu.VMEM((rows, width), BF),
+                pltpu.VMEM((width, rows), BF),
+                pltpu.VMEM((pairs, rows, 2 * HEAD), BF),
+                pltpu.VMEM((pairs, 2, keys, 2 * HEAD), BF),
+                pltpu.VMEM((pairs, 2, keys - rows, 2 * HEAD), BF),
+                pltpu.VMEM((keys, 2 * HEAD), F32),
+                pltpu.VMEM((keys, 2 * HEAD), F32),
+                pltpu.VMEM((2, BANDS, T, T), F32),
+                pltpu.VMEM((3, *tile), BF),
+                pltpu.VMEM((3, *tile), BF),
+                pltpu.VMEM((2 * pairs, VECTOR_ROWS, T), F32),
+                pltpu.VMEM((stages + 1, *vector), F32),
+                pltpu.VMEM((stages, *vector), F32),
+                pltpu.VMEM((1, width), F32),
+                sems(4),
+                sems(3),
+                sems(2, pairs),
+                sems(2, stages),
+            ]
+            + scatter_buffers(n, zs, seq, shard, lanes)
+            + [sems(2, 2, zs + 2), sems(2, 2, zs + 2)],
+        ),
+        out_shape=[
+            jax.ShapeDtypeStruct((rows, width), BF),
+            jax.ShapeDtypeStruct((count, 2, n, shard, lanes), F32),
+            jax.ShapeDtypeStruct(vector, F32),
+        ],
+        compiler_params=pltpu.CompilerParams(
+            collective_id=collective_id, has_side_effects=True, vmem_limit_bytes=VMEM_LIMIT
+        ),
+    )(live, q, k, v, bias, grad, out, norm, out, branch, normed, parts, weights, d_middle,
+      x_low, gain, d_gain_two)
 
 
 GELU_SCALE = 0.7978845608028654
@@ -920,21 +1279,18 @@
     queries = nn(normed_one, q_full).astype(BF)
     prompt_kv = kv[:local_prompt]
     if seq == 2:
-        other = lax.ppermute(prompt_kv, "seq", [(0, 1), (1, 0)])
-        every = jnp.concatenate([kv[:local_prompt], other, kv[local_prompt:]], axis=0)
-        first_tile = seq_index * local_tiles
+        others = lax.ppermute(prompt_kv, "seq", [(0, 1), (1, 0)])
     else:
         gathered = lax.all_gather(prompt_kv, "seq", axis=0, tiled=True)
-        every = jnp.concatenate([gathered, kv[local_prompt:]], axis=0)
-        first_tile = jnp.zeros((), jnp.int32)
+        others = jnp.roll(gathered, -seq_index * local_prompt, axis=0)[local_prompt:]
+    every = jnp.concatenate([kv, others], axis=0)
     keys, values = every[:, :inner], every[:, inner:]
-    base = jnp.stack([seq_index * local_tiles, first_tile]).astype(jnp.int32)
+    base = (seq_index * local_tiles).reshape(1).astype(jnp.int32)
 
     one_hot = band_one_hot(num_buckets)
     bias = jnp.einsum("cqkb,bh->hcqk", one_hot, bucket_table, precision=lax.Precision.HIGHEST)
-    attended, log_norm = attend(
-        queries, keys, values, bias, cont_len, base, tiles, local_tiles, conts
-    )
+    shape = Shape(tiles, local_tiles, conts)
+    attended, log_norm = attend(queries, keys, values, bias, cont_len, base, shape)
     middle = x + nt(attended, o_full)
     scale_two = rms_scale(middle)
     unit_two = middle * scale_two
@@ -942,8 +1298,8 @@
 
     moving = can_move(sizes, shard)
     if moving:
-        kept = (0, own_feed.shape[0])
-        out_sum, d_normed_two, _, _, feed_sums = feed_moving(
+        kept = (6, 13)
+        out_sum, d_normed_two, _, feed_parts, kept_sums = feed_moving(
             normed_two, dy_low, own_feed, own_feed, sizes, 0, kept, 1
         )
     else:
@@ -956,51 +1312,53 @@
     d_middle = dy + norm_back(d_normed_two, unit_two, scale_two, gain_two)
     d_branch = d_middle.astype(BF)
     d_attended = nn(d_branch, o_full).astype(BF)
-    d_o = tn(d_branch, attended)
-
-    d_queries, d_keys, d_values, d_bias = attend_back(
-        queries,
-        keys,
-        values,
-        bias,
-        d_attended,
-        attended,
-        log_norm,
-        cont_len,
-        base,
-        tiles,
-        local_tiles,
-        conts,
-    )
-    d_table = jnp.einsum("hcqk,cqkb->bh", d_bias, one_hot, precision=lax.Precision.HIGHEST)
-    d_kv = jnp.concatenate([d_keys, d_values], axis=1)
-    prompt_rows = local_prompt * seq
-    if seq == 2:
-        back = lax.ppermute(d_kv[local_prompt:prompt_rows], "seq", [(0, 1), (1, 0)])
-        d_prompt = (d_kv[:local_prompt].astype(F32) + back.astype(F32)).astype(BF)
+    if moving:
+        d_x, sums, vector = back(
+            queries, keys, values, bias, d_attended, attended, log_norm, d_branch, normed_one,
+            feed_parts, attention_whole.reshape(-1, *feed_parts.shape[1:]), d_middle, x_low,
+            gain_one[None], d_gain_two[None], cont_len, shape, sizes, kept, 2,
+        )
+        fed = sums.shape[0] - 4
+        feed_sums = jnp.concatenate([sums[: kept[0]], kept_sums, sums[kept[0] : fed]], axis=0)
+        attention_sums = jnp.concatenate([sums[fed + 1 :], sums[fed : fed + 1]], axis=0)
+        attention_sums = attention_sums.reshape(-1, shard, T)
+        near = vector[:heads, :4].reshape(heads, SPAN)
+        far = jnp.sum(vector[:heads, 4:6], axis=-1)
+        relative = (jnp.arange(SPAN) + T) % SPAN - 2 * T
+        ids = jnp.concatenate([bucket_ids(relative), bucket_ids(jnp.array([-T, T]))])
+        hot = (ids[:, None] == jnp.arange(num_buckets)).astype(F32)
+        both = jnp.concatenate([near, far], axis=1)
+        table_grad = jnp.einsum("hr,rb->bh", both, hot, precision=lax.Precision.HIGHEST)
+        gain_grads = vector[heads:].reshape(2, sizes[0] * seq, shard)
+        me = lax.axis_index("grp") * seq + seq_index
+        norm1_grad, norm2_grad = lax.dynamic_index_in_dim(gain_grads, me, 1, keepdims=False)
     else:
-        d_prompt = lax.psum_scatter(
-            d_kv[:prompt_rows], "seq", scatter_dimension=0, tiled=True
+        d_o = tn(d_branch, attended)
+        d_queries, d_keys, d_values, d_bias = attend_back(
+            queries, keys, values, bias, d_attended, attended, log_norm, cont_len, base, shape
         )
-    d_kv = jnp.concatenate([d_prompt, d_kv[prompt_rows:]], axis=0)
-    d_normed_one = nt(d_queries, q_full) + nt(d_kv, jnp.concatenate([k_full, v_full], axis=1))
-    d_q = tn(normed_one, d_queries)
-    d_kv_weight = tn(normed_one, d_kv)
-    d_gain_one = jnp.sum(d_normed_one * unit_one, axis=0)
-    d_x = d_middle + norm_back(d_normed_one, unit_one, scale_one, gain_one)
-    d_x = d_x.astype(BF)
-
-    attention_parts = attention_chunks([d_q, d_kv_weight, d_o]).astype(BF)
-    attention_sums = scatter(attention_parts, sizes, shard, 2).reshape(-1, shard, T)
-    feed_sums = feed_sums.reshape(-1, 3, shard, T)
-    feed_sums = feed_sums[: hidden_width // T]
+        d_table = jnp.einsum("hcqk,cqkb->bh", d_bias, one_hot, precision=lax.Precision.HIGHEST)
+        d_kv = jnp.concatenate([d_keys, d_values], axis=1)
+        prompt_parts = jnp.concatenate([d_kv[:local_prompt], d_kv[shape.rows :]], axis=0)
+        prompt_parts = jnp.roll(prompt_parts, seq_index * local_prompt, axis=0)
+        d_prompt = lax.psum_scatter(prompt_parts, "seq", scatter_dimension=0, tiled=True)
+        d_kv = jnp.concatenate([d_prompt, d_kv[local_prompt : shape.rows]], axis=0)
+        d_normed_one = nt(d_queries, q_full) + nt(d_kv, jnp.concatenate([k_full, v_full], axis=1))
+        d_q = tn(normed_one, d_queries)
+        d_kv_weight = tn(normed_one, d_kv)
+        d_gain_one = jnp.sum(d_normed_one * unit_one, axis=0)
+        d_x = d_middle + norm_back(d_normed_one, unit_one, scale_one, gain_one)
+        d_x = d_x.astype(BF)
+        attention_parts = attention_chunks([d_q, d_kv_weight, d_o]).astype(BF)
+        attention_sums = scatter(attention_parts, sizes, shard, 2).reshape(-1, shard, T)
+        norm1_grad = lax.psum_scatter(d_gain_one, ("grp", "seq"), scatter_dimension=0, tiled=True)
+        norm2_grad = lax.psum_scatter(d_gain_two, ("grp", "seq"), scatter_dimension=0, tiled=True)
+        table_grad = lax.psum(d_table, ("grp", "seq"))
+    feed_sums = feed_sums.reshape(-1, 3, shard, T)[: hidden_width // T]
     gate_grad, up_grad, down_grad = [joined(feed_sums[:, i]) for i in range(3)]
     q_grad, k_grad, v_grad, o_grad = [
         joined(attention_sums[i * count : (i + 1) * count]) for i in range(4)
     ]
-    norm1_grad = lax.psum_scatter(d_gain_one, ("grp", "seq"), scatter_dimension=0, tiled=True)
-    norm2_grad = lax.psum_scatter(d_gain_two, ("grp", "seq"), scatter_dimension=0, tiled=True)
-    table_grad = lax.psum(d_table, ("grp", "seq"))
     split = lambda rows: (
         rows[:local_prompt][None],
         rows[local_prompt:].reshape(1, conts, cont_rows, width),

time: 881 us -> 768 us (0.87)
  matrix products: 73.4 us -> 28.1 us
  blocking collectives: 39.6 us -> 0 us
  local copies, waits for them, and re-layouts: 92.5 us -> 65.4 us
  Pallas kernels: 615 us -> 627 us
    pallas_call x3 -> x2, Pallas kernels: 193 us -> 275 us  [the longest x1 218 us: back(): pl.pallas_call(functools.partial(back_kernel, zs, seq, shape, width, kept...]
    pallas_call x1, Pallas kernels: 351 us -> 281 us  [feed_moving(): pl.pallas_call(functools.partial(feed_moving_kernel, zs, seq, early, kept...]
    unnamed x1 -> x0, blocking collectives: 39.6 us -> none
    dot_general x4 -> x1, matrix products: 23.2 us -> 0.9 us  [body(): jnp.einsum('hr,rb->bh', both, hot, precision=lax.Precision.HIGHEST)]
    dot_general x3 -> x1, matrix products: 24.1 us -> 5.8 us  [nt(): lax.dot_general(left, right, (((1,), (1,)), ((), ())), preferred_element_...]
    reshape x10 -> x7, local copies, waits for them, and re-layouts: 17.3 us -> 1.93 us  [pieces_of(): return jnp.swapaxes(matrix.reshape(rows, columns // T, T), 0, 1)]
    unnamed x87 -> x86, local copies, waits for them, and re-layouts: 18.2 us -> 12.1 us
  transfers between devices with their start and end apart: 2 -> 1, of which waited for: 0 -> 1; matrix products, arithmetic and copies ran while one was open for 8% -> 4% of each run, Pallas kernels for 0% -> 0%
where the time goes in v3:
time: 768 us; the launch traced here: 763 us
  Pallas kernels  627 us (82%)
  local copies, waits for them, and re-layouts  65.4 us (9%)
  other arithmetic  38.1 us (5%)
  matrix products  28.1 us (4%)
    pallas_call x1, Pallas kernels, feed_moving(): pl.pallas_call(functools.partial(feed_moving_kernel, zs, seq, early, kept...  281 us
    pallas_call x1, Pallas kernels, back(): pl.pallas_call(functools.partial(back_kernel, zs, seq, shape, width, kept...  218 us
    pallas_call x1, Pallas kernels, gather(): pl.pallas_call(functools.partial(gather_kernel, zs, seq), grid=(chunks +...  70.9 us
    pallas_call x1, Pallas kernels, attend(): pl.pallas_call(functools.partial(attend_kernel, shape), grid_spec=pltpu.P...  56.2 us
    slice x5, local copies, waits for them, and re-layouts, body(): flat[i * count:(i + 1) * count]  18.6 us
    dot_general x3, matrix products, nn(): return jnp.dot(left, right, preferred_element_type=F32)  16.5 us
  transfers between devices with their start and end apart: 1, of which 1 were waited for; matrix products, arithmetic and copies ran while one was open for 4% of the time, Pallas kernels for 0%

profile of v3, /device:TPU:0, one launch (start us, length us, event | category | flops | bytes accessed | tf_op | source)
XLA Modules:
  0.0 762.9 jit_solution(1414206081531745229)
XLA Ops:
  0.7 2.7 fusion.1
  6.3 70.9 %shard_map.263.refs_11_ = bf16[5,2,3,4,2,4,48,128]{7,6,5,4,3,2,1,0:T(8,128)(2,1)} custom-call(bf16[5,2,3,48,128]{4,3,2,1,0:T(8,128)(2,1)} %bitcast.150), custom_call_target="tpu_custom_call" | custom-call | tf_op jit(solution)/shard_map/pallas_call | solution.py:198
  77.2 6.6 fusion.37
  83.8 2.1 fusion.36
  86.1 2.5 copy.71
  88.6 4.4 copy.72
  93.0 4.4 fusion.3.refs_9_
  97.4 6.2 fusion.9
  112.1 4.9 fusion
  118.8 2.7 copy.70
  121.5 5.7 copy.108
  127.3 2.5 copy.74
  137.3 3.7 convolution_convert_fusion.1.q.refs_0_
  142.3 3.6 pad_maximum_fusion.2
  145.8 56.2 %shard_map.264 = (bf16[1024,768]{1,0:T(8,128)(2,1)}, f32[12,1024,1]{2,1,0:T(8,128)}) custom-call(s32[1,4]{1,0:T(1,128)} %live.3, s32[1]{0:T(128)} %bitcast.2.base, bf16[1024,768]{1,0:T(8,128)(2,1)} %convolution_convert_fusion.1.q.refs_0_, bf16[1536,768]{1,0:T(8,128)(2,1)} %get-tuple-element.44.k.refs_1_, bf16[1536,768]{1,0:T(8,128)(2,1)} %get-tuple-element.43.v.refs_2_, ...), custom_call_target="tpu_custom_call" | custom-call | tf_op jit(solution)/shard_map/pallas_call | solution.py:467
  202.1 5.8 multiply_reduce_fusion.2
  207.9 2.6 multiply_convert_fusion.refs_0_
  211.5 281.0 %shard_map.265 = (f32[1024,1536]{1,0:T(8,128)}, f32[1024,1536]{1,0:T(8,128)}, bf16[16,2,3,4,2,4,48,128]{7,6,5,4,3,2,1,0:T(8,128)(2,1)}, bf16[16,2,3,4,2,4,48,128...) custom-call(bf16[1024,1536]{1,0:T(8,128)(2,1)} %multiply_convert_fusion.refs_0_, ...), custom_call_target="tpu_custom_call" | custom-call | tf_op jit(solution)/shard_map/pallas_call | solution.py:1164
  492.5 5.9 multiply_reduce_fusion
  500.8 9.9 %fusion.35 = (bf16[1024,1536]{1,0:T(8,128)(2,1)S(1)}, f32[1024,1536]{1,0:T(8,128)}, bf16[1024,1536]{1,0:T(8,128)(2,1)}) fusion(f32[1024]{0:T(1024)S(1)} %broadcast_multiply_fusion, f32[1024,1536]{1,0:T(8,128)S(1)} %bitcast.115, f32[1024,1536]{1,0:T(8,128)S(1)} %copy-done.3, f32[1536]{0:T(1024)S(1)} %convert_reduce_fusion, f32[1024]{0:T(1024)S(1)} %add_rsqrt_fusion, ...), kind=kLoop, calls=%fused_computation.88 | loop fusion | flops 20447232 | bytes 34617344 | tf_op jit(solution)/shard_map/convert_element_type | solution.py:1313
  510.7 6.6 convolution_convert_fusion.refs_4_
  517.9 218.5 %shard_map.266 = (bf16[1024,1536]{1,0:T(8,128)(2,1)}, f32[13,2,3,48,128]{4,3,2,1,0:T(8,128)}, f32[15,8,128]{2,1,0:T(8,128)}) custom-call(s32[1,4]{1,0:T(1,128)} %live.3, bf16[1024,768]{1,0:T(8,128)(2,1)} %convolution_convert_fusion.1.q.refs_0_, bf16[1536,768]{1,0:T(8,128)(2,1)} %get-tuple-element.44.k.refs_1_, ...), custom_call_target="tpu_custom_call" | custom-call | tf_op jit(solution)/shard_map/pallas_call | solution.py:874
  750.7 3.6 copy_bitcast_fusion.1
  755.9 4.7 fusion.38
  (147 shorter events, 43.8 us)
Async XLA Ops:
  0.6 111.5 %copy-start = (f32[32,12]{0,1:T(8,128)S(1)}, f32[32,12]{0,1:T(8,128)}, u32[]{:S(2)}) copy-start(f32[32,12]{0,1:T(8,128)} %param.26) | copy-start | bytes 4612
  88.6 4.4 copy-start.4
  88.6 4.4 copy-start.5
  93.0 4.4 copy-start.17
  93.0 4.4 copy-start.18
  97.4 6.2 copy-start.6
  103.6 5.3 copy-start.12
  105.0 37.3 %collective-permute-start = (bf16[512,1536]{1,0:T(8,128)(2,1)}, bf16[512,1536]{1,0:T(8,128)(2,1)}, u32[]{:S(2)}, u32[]{:S(2)}) collective-permute-start(bf16[512,1536]{1,0:T(8,128)(2,1)} %slice.147), channel_id=1, source_target_pairs={{0,1},{1,0},{2,3},{3,2},{4,5},{5,4},{6,7},{7,6},{8,9},{9,8},{10,11... | collective-permute-start | bytes 4718600 | tf_op jit(solution)/shard_map/ppermute | solution.py:1282
  112.1 4.9 copy-start.19
  112.1 6.1 copy-start.33
  112.1 6.7 copy-start.11
  121.5 5.8 copy-start.10
  129.8 3.8 copy-start.15
  137.3 4.9 copy-start.13
  492.5 6.0 slice-start
  492.5 6.5 slice-start.1
  492.5 8.3 %copy-start.3 = (f32[1024,1536]{1,0:T(8,128)S(1)}, f32[1024,1536]{1,0:T(8,128)}, u32[]{:S(2)}) copy-start(f32[1024,1536]{1,0:T(8,128)} %get-tuple-element.25) | copy-start | bytes 18874372
  510.7 6.6 copy-start.8
  736.4 6.5 copy-start.21
  747.1 8.7 %copy-start.9 = (bf16[1024,1536]{1,0:T(8,128)(2,1)S(1)}, bf16[1024,1536]{1,0:T(8,128)(2,1)}, u32[]{:S(2)}) copy-start(bf16[1024,1536]{1,0:T(8,128)(2,1)} %get-tuple-element.42) | copy-start | bytes 9437188
  750.7 4.4 copy-start.23
  755.8 4.7 copy-start.30
  755.8 4.7 copy-start.32
  755.8 6.8 copy-start.1
  (15 other events, 46.2 us)

commit v4 on v3

--- a/solution.py
+++ b/solution.py
@@ -459,6 +459,85 @@
 
 def pair_block(n):
     return pl.BlockSpec((n, 2 * HEAD), lambda h, *_: (0, h))
+
+
+def attend_moving_kernel(zs, xs, shape, early, live, q, k, v, bias, own, out, norm, ready, *scratch):
+    held, local, send, recv = scratch
+    place = Place(zs, xs)
+    step = pl.program_id(0)
+
+    @pl.when(step == 0)
+    def _():
+        place.barrier()
+
+    Gather(place, own, ready, send, recv).tick(step, 0, early)
+
+    @pl.when(step == 0)
+    def _():
+        load = pltpu.make_async_copy(own.at[0:early], held, local.at[0])
+        load.start()
+        load.wait()
+        mine = ready.at[:, :, :, place.z, place.y, place.c * place.xs + place.x]
+        store = pltpu.make_async_copy(held, mine, local.at[1])
+        store.start()
+        store.wait()
+
+    base = place.x * shape.local_tiles
+    for part in range(2):
+
+        @pl.when(step % 2 == part)
+        def _(part=part):
+            for_tiles(
+                shape,
+                part == 1,
+                lambda i, c: attend_tile(shape, i, c, live, base, q, k, v, bias, out, norm),
+            )
+
+
+def attend_moving(q, k, v, bias, live, own, shape, sizes, early, collective_id):
+    grp, seq = sizes
+    rows, width = q.shape
+    pairs = width // (2 * HEAD)
+    _, _, n, shard, lanes = own.shape
+    zs = grp // (Y * C)
+    tile = (2, n, zs, Y, C * seq, shard, lanes)
+    block = lambda count: pl.BlockSpec((count, 2 * HEAD), lambda s, *_: (0, s // 2))
+    anywhere = pl.BlockSpec(memory_space=pl.ANY)
+    sems = lambda *dims: pltpu.SemaphoreType.DMA(dims)
+    assert early + 4 <= 2 * pairs
+    return pl.pallas_call(
+        functools.partial(attend_moving_kernel, zs, seq, shape, early),
+        grid_spec=pltpu.PrefetchScalarGridSpec(
+            num_scalar_prefetch=1,
+            grid=(2 * pairs,),
+            in_specs=[
+                block(rows),
+                block(shape.keys),
+                block(shape.keys),
+                pl.BlockSpec((2, BANDS, T, T), lambda s, *_: (s // 2, 0, 0, 0)),
+                anywhere,
+            ],
+            out_specs=[
+                block(rows),
+                pl.BlockSpec((2, rows, 1), lambda s, *_: (s // 2, 0, 0)),
+                anywhere,
+            ],
+            scratch_shapes=[
+                pltpu.VMEM((early, *own.shape[1:]), BF),
+                sems(2),
+                sems(early, 2, zs + 2),
+                sems(early, 2, zs + 2),
+            ],
+        ),
+        out_shape=[
+            jax.ShapeDtypeStruct((rows, width), BF),
+            jax.ShapeDtypeStruct((2 * pairs, rows, 1), F32),
+            jax.ShapeDtypeStruct((early, *tile), BF),
+        ],
+        compiler_params=pltpu.CompilerParams(
+            collective_id=collective_id, has_side_effects=True, vmem_limit_bytes=VMEM_LIMIT
+        ),
+    )(live, q, k, v, bias, own)
 
 
 def attend(q, k, v, bias, live, base, shape):
@@ -1290,22 +1369,27 @@
     one_hot = band_one_hot(num_buckets)
     bias = jnp.einsum("cqkb,bh->hcqk", one_hot, bucket_table, precision=lax.Precision.HIGHEST)
     shape = Shape(tiles, local_tiles, conts)
-    attended, log_norm = attend(queries, keys, values, bias, cont_len, base, shape)
+    moving = can_move(sizes, shard)
+    early, kept = 5, (8, 14)
+    if moving:
+        attended, log_norm, ready = attend_moving(
+            queries, keys, values, bias, cont_len, own_feed, shape, sizes, early, 3
+        )
+    else:
+        attended, log_norm = attend(queries, keys, values, bias, cont_len, base, shape)
     middle = x + nt(attended, o_full)
     scale_two = rms_scale(middle)
     unit_two = middle * scale_two
     normed_two = (unit_two * gain_two).astype(BF)
 
-    moving = can_move(sizes, shard)
     if moving:
-        kept = (6, 13)
         out_sum, d_normed_two, _, feed_parts, kept_sums = feed_moving(
-            normed_two, dy_low, own_feed, own_feed, sizes, 0, kept, 1
+            normed_two, dy_low, own_feed, ready, sizes, early, kept, 1
         )
     else:
         feed_whole = gather(own_feed, sizes, 1)
         out_sum, d_normed_two, feed_grads = feed(normed_two, dy_low, feed_whole)
-        feed_sums = scatter(feed_grads, sizes, shard, 3)
+        feed_sums = scatter(feed_grads, sizes, shard, 4)
     final = (middle + out_sum).astype(BF)
 
     d_gain_two = jnp.sum(d_normed_two * unit_two, axis=0)

time: 768 us -> 755 us (0.983)
  Pallas kernels: 627 us -> 614 us
    pallas_call x1, Pallas kernels: 281 us -> 228 us  [feed_moving(): pl.pallas_call(functools.partial(feed_moving_kernel, zs, seq, early, kept...]
    pallas_call x1, Pallas kernels: 56.2 us -> 89.8 us  [attend_moving(): pl.pallas_call(functools.partial(attend_moving_kernel, zs, seq, shape, ea...]
where the time goes in v4:
time: 755 us; the launch traced here: 750 us
  Pallas kernels  614 us (81%)
  local copies, waits for them, and re-layouts  63.9 us (8%)
  other arithmetic  39.9 us (5%)
  matrix products  28.1 us (4%)
    pallas_call x1, Pallas kernels, feed_moving(): pl.pallas_call(functools.partial(feed_moving_kernel, zs, seq, early, kept...  228 us
    pallas_call x1, Pallas kernels, back(): pl.pallas_call(functools.partial(back_kernel, zs, seq, shape, width, kept...  225 us
    pallas_call x1, Pallas kernels, attend_moving(): pl.pallas_call(functools.partial(attend_moving_kernel, zs, seq, shape, ea...  89.8 us
    pallas_call x1, Pallas kernels, gather(): pl.pallas_call(functools.partial(gather_kernel, zs, seq), grid=(chunks +...  70.9 us
    slice x5, local copies, waits for them, and re-layouts, body(): flat[i * count:(i + 1) * count]  18.6 us
    dot_general x3, matrix products, nn(): return jnp.dot(left, right, preferred_element_type=F32)  16.5 us
  transfers between devices with their start and end apart: 1, of which 1 were waited for; matrix products, arithmetic and copies ran while one was open for 4% of the time, Pallas kernels for 0%

profile of v4, /device:TPU:0, one launch (start us, length us, event | category | flops | bytes accessed | tf_op | source)
XLA Modules:
  0.0 750.1 jit_solution(10259829486419120386)
XLA Ops:
  0.7 2.7 fusion.1
  6.3 70.9 %shard_map.263.refs_11_ = bf16[5,2,3,4,2,4,48,128]{7,6,5,4,3,2,1,0:T(8,128)(2,1)} custom-call(bf16[5,2,3,48,128]{4,3,2,1,0:T(8,128)(2,1)} %bitcast.149), custom_call_target="tpu_custom_call" | custom-call | tf_op jit(solution)/shard_map/pallas_call | solution.py:198
  77.2 6.6 fusion.37
  86.1 2.5 copy.71
  88.6 4.4 copy.72
  93.0 4.4 fusion.3.refs_9_
  97.4 6.2 fusion.9
  114.2 4.9 fusion
  119.9 2.7 copy.70
  122.6 5.7 copy.108
  130.3 2.5 copy.75
  133.0 3.9 pad_maximum_fusion.1.refs_1_
  137.5 3.7 convolution_convert_fusion.1.q.refs_0_
  142.3 3.6 pad_maximum_fusion.2
  145.9 89.8 %shard_map.264 = (bf16[1024,768]{1,0:T(8,128)(2,1)}, f32[12,1024,1]{2,1,0:T(8,128)}, bf16[5,2,3,4,2,4,48,128]{7,6,5,4,3,2,1,0:T(8,128)(2,1)}) custom-call(s32[1,4]{1,0:T(1,128)} %live.3, bf16[1024,768]{1,0:T(8,128)(2,1)} %convolution_convert_fusion.1.q.refs_0_, bf16[1536,768]{1,0:T(8,128)(2,1)} %get-tuple-element.46.k.refs_1_, ...), custom_call_target="tpu_custom_call" | custom-call | tf_op jit(solution)/shard_map/pallas_call | solution.py:508
  235.7 5.8 multiply_reduce_fusion.2
  241.5 2.6 multiply_convert_fusion.refs_0_
  245.1 228.0 %shard_map.265 = (f32[1024,1536]{1,0:T(8,128)}, f32[1024,1536]{1,0:T(8,128)}, bf16[16,2,3,4,2,4,48,128]{7,6,5,4,3,2,1,0:T(8,128)(2,1)}, bf16[16,2,3,4,2,4,48,128...) custom-call(bf16[1024,1536]{1,0:T(8,128)(2,1)} %multiply_convert_fusion.refs_0_, ...), custom_call_target="tpu_custom_call" | custom-call | tf_op jit(solution)/shard_map/pallas_call | solution.py:1243
  473.2 6.0 multiply_reduce_fusion
  481.5 9.9 %fusion.35 = (bf16[1024,1536]{1,0:T(8,128)(2,1)S(1)}, f32[1024,1536]{1,0:T(8,128)}, bf16[1024,1536]{1,0:T(8,128)(2,1)}) fusion(f32[1024]{0:T(1024)S(1)} %broadcast_multiply_fusion, f32[1024,1536]{1,0:T(8,128)S(1)} %bitcast.114, f32[1024,1536]{1,0:T(8,128)S(1)} %copy-done.3, f32[1536]{0:T(1024)S(1)} %convert_reduce_fusion, f32[1024]{0:T(1024)S(1)} %add_rsqrt_fusion, ...), kind=kLoop, calls=%fused_computation.88 | loop fusion | flops 20447232 | bytes 34617344 | tf_op jit(solution)/shard_map/convert_element_type | solution.py:1397
  491.4 6.6 convolution_convert_fusion.refs_4_
  498.6 225.0 %shard_map.266 = (bf16[1024,1536]{1,0:T(8,128)(2,1)}, f32[14,2,3,48,128]{4,3,2,1,0:T(8,128)}, f32[15,8,128]{2,1,0:T(8,128)}) custom-call(s32[1,4]{1,0:T(1,128)} %live.3, bf16[1024,768]{1,0:T(8,128)(2,1)} %convolution_convert_fusion.1.q.refs_0_, bf16[1536,768]{1,0:T(8,128)(2,1)} %get-tuple-element.46.k.refs_1_, ...), custom_call_target="tpu_custom_call" | custom-call | tf_op jit(solution)/shard_map/pallas_call | solution.py:953
  737.9 3.6 copy_bitcast_fusion.1
  743.1 4.7 fusion.38
  (147 shorter events, 42.0 us)
Async XLA Ops:
  0.6 113.5 %copy-start = (f32[32,12]{0,1:T(8,128)S(1)}, f32[32,12]{0,1:T(8,128)}, u32[]{:S(2)}) copy-start(f32[32,12]{0,1:T(8,128)} %param.26) | copy-start | bytes 4612
  88.6 4.4 copy-start.4
  88.6 4.4 copy-start.5
  97.4 6.2 copy-start.6
  103.6 5.3 copy-start.12
  105.0 37.3 %collective-permute-start = (bf16[512,1536]{1,0:T(8,128)(2,1)}, bf16[512,1536]{1,0:T(8,128)(2,1)}, u32[]{:S(2)}, u32[]{:S(2)}) collective-permute-start(bf16[512,1536]{1,0:T(8,128)(2,1)} %slice.147), channel_id=1, source_target_pairs={{0,1},{1,0},{2,3},{3,2},{4,5},{5,4},{6,7},{7,6},{8,9},{9,8},{10,11... | collective-permute-start | bytes 4718600 | tf_op jit(solution)/shard_map/ppermute | solution.py:1361
  114.2 4.9 copy-start.17
  114.2 4.9 copy-start.18
  114.2 4.9 copy-start.19
  114.2 5.1 copy-start.31
  114.2 5.1 copy-start.33
  114.2 5.7 copy-start.11
  133.0 4.5 copy-start.7
  133.0 4.5 copy-start.14
  137.5 4.8 copy-start.13
  473.2 6.1 slice-start
  473.2 6.5 slice-start.1
  473.2 8.3 %copy-start.3 = (f32[1024,1536]{1,0:T(8,128)S(1)}, f32[1024,1536]{1,0:T(8,128)}, u32[]{:S(2)}) copy-start(f32[1024,1536]{1,0:T(8,128)} %get-tuple-element.27) | copy-start | bytes 18874372
  491.4 6.6 copy-start.8
  723.6 6.6 copy-start.21
  734.3 8.7 %copy-start.9 = (bf16[1024,1536]{1,0:T(8,128)(2,1)S(1)}, bf16[1024,1536]{1,0:T(8,128)(2,1)}, u32[]{:S(2)}) copy-start(bf16[1024,1536]{1,0:T(8,128)(2,1)} %get-tuple-element.44) | copy-start | bytes 9437188
  743.1 4.7 copy-start.30
  743.1 4.7 copy-start.32
  743.1 6.8 copy-start.1
  (15 other events, 51.9 us)

commit v5 on v3

--- a/solution.py
+++ b/solution.py
@@ -169,47 +169,8 @@
             staged(step, offset, end - first, lambda k, action=action: action(first + k))
 
 
-def gather_kernel(zs, xs, own, whole, held, local, send, recv):
-    place = Place(zs, xs)
-    step = pl.program_id(0)
-
-    @pl.when(step == 0)
-    def _():
-        place.barrier()
-        load = pltpu.make_async_copy(own, held, local.at[0])
-        load.start()
-        load.wait()
-        mine = whole.at[:, :, :, place.z, place.y, place.c * place.xs + place.x]
-        store = pltpu.make_async_copy(held, mine, local.at[1])
-        store.start()
-        store.wait()
-
-    Gather(place, held, whole, send, recv).tick(step, 0, own.shape[0])
-
-
-def gather(own, sizes, collective_id):
-    grp, seq = sizes
-    chunks, halves, n, rows, lanes = own.shape
-    if not can_move(sizes, rows):
-        whole = lax.all_gather(own, ("grp", "seq"), axis=3, tiled=True)
-        return whole
-    zs = grp // (Y * C)
-    slots = (chunks, 2, zs + 2)
-    whole = pl.pallas_call(
-        functools.partial(gather_kernel, zs, seq),
-        grid=(chunks + 4,),
-        out_shape=jax.ShapeDtypeStruct((chunks, 2, n, zs, Y, C * seq, rows, lanes), own.dtype),
-        in_specs=[pl.BlockSpec(memory_space=pl.ANY)],
-        out_specs=pl.BlockSpec(memory_space=pl.ANY),
-        scratch_shapes=[
-            pltpu.VMEM(own.shape, own.dtype),
-            pltpu.SemaphoreType.DMA((2,)),
-            pltpu.SemaphoreType.DMA(slots),
-            pltpu.SemaphoreType.DMA(slots),
-        ],
-        compiler_params=pltpu.CompilerParams(collective_id=collective_id, has_side_effects=True),
-    )(own)
-    return whole.reshape(chunks, 2, n, grp * seq * rows, lanes)
+def gather(own, sizes):
+    return lax.all_gather(own, ("grp", "seq"), axis=3, tiled=True)
 
 
 class Scatter:
@@ -329,55 +290,8 @@
     return [pltpu.VMEM(shape, BF) for shape in shapes]
 
 
-def scatter_kernel(zs, xs, chunks, parts, out, held, local, *rest):
-    bufs, (send, recv) = rest[:7], rest[7:]
-    place = Place(zs, xs)
-    step = pl.program_id(0)
-    engine = Scatter(place, bufs, send, recv, out)
-
-    @pl.when(step == 0)
-    def _():
-        place.barrier()
-
-    def load(k):
-        return pltpu.make_async_copy(parts.at[k], held.at[k % 3], local.at[k % 3])
-
-    def first(k):
-        load(k).wait()
-        engine.start_first(k, held.at[k % 3])
-
-    staged(step, 5, chunks, engine.finish)
-    staged(step, 4, chunks, engine.start_fourth)
-    staged(step, 3, chunks, engine.start_third)
-    staged(step, 2, chunks, lambda k: engine.start_second(k, held.at[k % 3]))
-    staged(step, 1, chunks, first)
-    staged(step, 0, chunks, lambda k: load(k).start())
-
-
-def scatter(parts, sizes, rows, collective_id):
-    grp, seq = sizes
-    chunks, halves, n, _, lanes = parts.shape
-    if not can_move(sizes, rows):
-        return lax.psum_scatter(parts, ("grp", "seq"), scatter_dimension=3, tiled=True).astype(F32)
-    zs = grp // (Y * C)
-    view = parts.reshape(chunks, 2, n, zs, Y, C * seq, rows, lanes)
-    sems = (2, 2, zs + 2)
-    return pl.pallas_call(
-        functools.partial(scatter_kernel, zs, seq, chunks),
-        grid=(chunks + 5,),
-        out_shape=jax.ShapeDtypeStruct((chunks, 2, n, rows, lanes), F32),
-        in_specs=[pl.BlockSpec(memory_space=pl.ANY)],
-        out_specs=pl.BlockSpec((chunks, 2, n, rows, lanes), lambda step: (0, 0, 0, 0, 0)),
-        scratch_shapes=[
-            pltpu.VMEM((3, 2, n, zs, Y, C * seq, rows, lanes), BF),
-            pltpu.SemaphoreType.DMA((3,)),
-        ]
-        + scatter_buffers(n, zs, seq, rows, lanes)
-        + [pltpu.SemaphoreType.DMA(sems), pltpu.SemaphoreType.DMA(sems)],
-        compiler_params=pltpu.CompilerParams(
-            collective_id=collective_id, has_side_effects=True, vmem_limit_bytes=VMEM_LIMIT
-        ),
-    )(view)
+def scatter(parts):
+    return lax.psum_scatter(parts, ("grp", "seq"), scatter_dimension=3, tiled=True).astype(F32)
 
 
 class Shape:
@@ -578,6 +492,277 @@
     )(live, base, q, k, v, bias, grad, out, norm)
 
 
+ORDER = (1, 2, 0, 3)
+FIRST_PAIR = 8
+
+
+def joined_pieces(w_buf, slot, m):
+    pieces = [w_buf[slot, j // 3, j % 3] for j in (2 * m, 2 * m + 1)]
+    return jnp.concatenate([piece.reshape(-1, T) for piece in pieces], axis=1)
+
+
+def front_kernel(zs, xs, shape, early, live, *refs):
+    (prompt_x, cont_x, own_gain, *weights) = refs[:10]
+    table = refs[10]
+    (whole, own_out, x_out, normed_out, kv_out, bias_out) = refs[11:17]
+    (q, attended, norm, middle, normed_two, gains) = refs[17:23]
+    (x, normed, kv, bias, held, w_buf, gain_whole) = refs[23:30]
+    (local, kv_sems, send, recv, gain_send, gain_recv) = refs[30:36]
+    place = Place(zs, xs)
+    step = pl.program_id(0)
+    rows, width = x.shape
+    prompt = shape.local_tiles * T
+    pairs = q.shape[0]
+    size = middle.shape[0]
+    blocks = rows // size
+    last = FIRST_PAIR + pairs
+    count = 4 + early
+    feed_weights = weights[4:]
+    columns = feed_weights[0].shape[1] // T
+
+    def x_load(i):
+        source, part = ((prompt_x, pl.ds(0, prompt)), (cont_x, pl.ds(prompt, rows - prompt)))[i]
+        return pltpu.make_async_copy(source, x.at[part], local.at[i])
+
+    def mine_store():
+        mine = whole.at[:, :, :, place.z, place.y, place.c * place.xs + place.x]
+        return pltpu.make_async_copy(held.at[pl.ds(0, count)], mine, local.at[2])
+
+    feed_own = held.at[pl.ds(4, held.shape[0] - 4)]
+    kept = ((feed_own, own_out), (x, x_out), (normed, normed_out), (bias, bias_out), (kv, kv_out))
+
+    def result(i):
+        return pltpu.make_async_copy(*kept[i], local.at[3 + i])
+
+    def weight_load(k):
+        return pltpu.make_async_copy(whole.at[k], w_buf.at[k % 2], local.at[8 + k])
+
+    @pl.when(step == 0)
+    def _():
+        place.barrier()
+        x_load(0).start()
+        x_load(1).start()
+        for c, matrix in enumerate(ORDER):
+            for j in range(6):
+                held[c, j // 3, j % 3] = weights[matrix][:, j * T : (j + 1) * T].astype(BF)
+        gain_whole[0, :, :, place.z, place.y, place.c * place.xs + place.x] = own_gain[0]
+
+    Gather(place, own_gain, gain_whole, gain_send, gain_recv).tick(step, 0, 1)
+    Gather(place, held, whole, send, recv).tick(step, 0, count)
+
+    @pl.when(step == 0)
+    def _():
+        def convert(j, carry):
+            part = pl.ds(pl.multiple_of(j * T, T), T)
+            for i in range(3):
+                held[4 + j // 2, j % 2, i] = feed_weights[i][:, part].astype(BF)
+            return carry
+
+        lax.fori_loop(0, columns, convert, 0)
+        if columns % 2:
+            held[4 + columns // 2, 1] = jnp.zeros(held.shape[2:], BF)
+        mine_store().start()
+        mine_store().wait()
+        result(0).start()
+        x_load(0).wait()
+        x_load(1).wait()
+        result(1).start()
+
+    @pl.when(step == 1)
+    def _():
+        query = lax.broadcasted_iota(jnp.int32, (T, T), 0)
+        key = lax.broadcasted_iota(jnp.int32, (T, T), 1)
+        half = table.shape[0] // 2
+        ids = [bucket_ids(band * T + key - query) for band in (-1, 0, 1)]
+        found = (range(1, half), [*range(half), *range(half + 1, 2 * half)], range(half + 1, 2 * half))
+
+        def one(h, carry):
+            bias[h, 0] = jnp.full((T, T), table[half - 1, h])
+            bias[h, 4] = jnp.full((T, T), table[2 * half - 1, h])
+            for band in range(3):
+                value = jnp.zeros((T, T), F32)
+                for bucket in found[band]:
+                    value = jnp.where(ids[band] == bucket, table[bucket, h], value)
+                bias[h, 1 + band] = value
+            return carry
+
+        lax.fori_loop(0, bias.shape[0], one, 0)
+
+    for k in range(4):
+
+        @pl.when(step == 4 + k)
+        def _(k=k):
+            weight_load(k).start()
+
+    def by_rows(action):
+        def one(i, carry):
+            action(pl.ds(pl.multiple_of(i * size, size), size))
+            return carry
+
+        lax.fori_loop(0, blocks, one, 0)
+
+    @pl.when(step == 4)
+    def _():
+        result(3).start()
+        eye = lax.broadcasted_iota(jnp.int32, (T, T), 0) == lax.broadcasted_iota(jnp.int32, (T, T), 1)
+        for g in range(2):
+            column = gain_whole[0, g, 0].reshape(width, T).astype(F32)
+            for i in range(width // T):
+                cols = slice(i * T, (i + 1) * T)
+                gains[g, :, cols] = jnp.sum(jnp.where(eye, column[cols], 0.0), axis=0, keepdims=True)
+
+        def norm_rows(part):
+            values = x[part, :].astype(F32)
+            scale = lax.rsqrt(jnp.mean(values * values, axis=-1, keepdims=True) + EPS)
+            normed[part, :] = (values * scale * gains[0]).astype(BF)
+
+        by_rows(norm_rows)
+        result(2).start()
+
+    def project(slot, target):
+        for m in range(pairs // 2):
+            right = joined_pieces(w_buf, slot, m)
+
+            def rows_of_product(part, m=m, right=right):
+                product = nn(normed[part, :], right).astype(BF)
+                target[2 * m, part, :] = product[:, :T]
+                target[2 * m + 1, part, :] = product[:, T:]
+
+            by_rows(rows_of_product)
+
+    def kv_send(side, p):
+        src = kv.at[side, p, pl.ds(0, prompt)]
+        dst = kv.at[side, p, pl.ds(rows, prompt)]
+        peer = place.device(x=1 - place.x)
+        return remote(src, dst, kv_sems.at[0, side, p], kv_sems.at[1, side, p], peer)
+
+    for k in range(3):
+
+        @pl.when(step == 5 + k)
+        def _(k=k):
+            weight_load(k).wait()
+            project(k % 2, kv.at[k] if k < 2 else q)
+            if k < 2:
+                for p in range(pairs):
+                    kv_send(k, p).start()
+
+    @pl.when(step == FIRST_PAIR)
+    def _():
+        weight_load(3).wait()
+
+    @pl.when((step >= FIRST_PAIR) & (step < last))
+    def _():
+        p = step - FIRST_PAIR
+        for side in range(2):
+            kv_send(side, p).wait_recv()
+            kv_send(side, p).wait_send()
+        base = place.x * shape.local_tiles
+        inputs = (q.at[p], kv.at[0, p], kv.at[1, p], bias.at[pl.ds(2 * p, 2)], attended.at[p], norm)
+        for conts in (False, True):
+            for_tiles(shape, conts, lambda i, c: attend_tile(shape, i, c, live, base, *inputs))
+
+    @pl.when(step == last)
+    def _():
+        result(4).start()
+
+    @pl.when(step >= last)
+    def _():
+        part = pl.ds(pl.multiple_of((step - last) * size, size), size)
+        branch = None
+        for m in range(pairs // 2):
+            left = jnp.concatenate([attended[2 * m + e, part, :] for e in range(2)], axis=1)
+            term = nt(left, joined_pieces(w_buf, 1, m))
+            branch = term if branch is None else branch + term
+        total = x[part, :].astype(F32) + branch
+        middle[...] = total
+        scale = lax.rsqrt(jnp.mean(total * total, axis=-1, keepdims=True) + EPS)
+        normed_two[...] = (total * scale * gains[1]).astype(BF)
+
+    @pl.when(step == last + blocks - 1)
+    def _():
+        for i in range(len(kept)):
+            result(i).wait()
+
+
+def front(prompt_x, cont_x, own_gain, weights, table, live, shape, sizes, early, collective_id):
+    grp, seq = sizes
+    rows, width = shape.rows, prompt_x.shape[1]
+    shard, inner = weights[0].shape
+    feed_columns = weights[4].shape[1] // T
+    pairs, keys, heads = inner // (2 * HEAD), shape.keys, table.shape[1]
+    assert pairs == 6 and table.shape[0] == 32 and keys - rows == prompt_x.shape[0]
+    zs = grp // (Y * C)
+    chunks = 4 + (feed_columns + 1) // 2
+    count = 4 + early
+    own = (2, 3, shard, T)
+    tile = (2, 3, zs, Y, C * seq, shard, T)
+    size = min(rows, 256)
+    blocks = rows // size
+    last = FIRST_PAIR + pairs
+    steps = last + blocks
+    assert count + 4 <= steps and count <= chunks
+    full = lambda *dims: pl.BlockSpec(
+        dims, lambda s, *_: (0,) * len(dims), pipeline_mode=pl.Buffered(1)
+    )
+    by_rows = pl.BlockSpec((size, width), lambda s, *_: (jnp.clip(s - last, 0, blocks - 1), 0))
+    anywhere = pl.BlockSpec(memory_space=pl.ANY)
+    sems = lambda *dims: pltpu.SemaphoreType.DMA(dims)
+    out = jax.ShapeDtypeStruct
+    return pl.pallas_call(
+        functools.partial(front_kernel, zs, seq, shape, early),
+        grid_spec=pltpu.PrefetchScalarGridSpec(
+            num_scalar_prefetch=1,
+            grid=(steps,),
+            in_specs=[anywhere, anywhere, full(*own_gain.shape)]
+            + [full(*w.shape) for w in weights]
+            + [pl.BlockSpec(memory_space=pltpu.SMEM)],
+            out_specs=[anywhere] * 6
+            + [
+                full(pairs, rows, 2 * HEAD),
+                full(pairs, rows, 2 * HEAD),
+                pl.BlockSpec(
+                    (2, rows, 1), lambda s, *_: (jnp.clip(s - FIRST_PAIR, 0, pairs - 1), 0, 0)
+                ),
+                by_rows,
+                by_rows,
+                full(2, 1, width),
+            ],
+            scratch_shapes=[
+                pltpu.VMEM((rows, width), BF),
+                pltpu.VMEM((rows, width), BF),
+                pltpu.VMEM((2, pairs, keys, 2 * HEAD), BF),
+                pltpu.VMEM((heads, BANDS, T, T), F32),
+                pltpu.VMEM((chunks, *own), BF),
+                pltpu.VMEM((2, *tile), BF),
+                pltpu.VMEM((1, 2, 1, zs, Y, C * seq, shard, T), BF),
+                sems(12),
+                sems(2, 2, pairs),
+                sems(count, 2, zs + 2),
+                sems(count, 2, zs + 2),
+                sems(1, 2, zs + 2),
+                sems(1, 2, zs + 2),
+            ],
+        ),
+        out_shape=[
+            out((count, *tile), BF),
+            out((chunks - 4, *own), BF),
+            out((rows, width), BF),
+            out((rows, width), BF),
+            out((2, pairs, keys, 2 * HEAD), BF),
+            out((heads, BANDS, T, T), F32),
+            out((pairs, rows, 2 * HEAD), BF),
+            out((pairs, rows, 2 * HEAD), BF),
+            out((2 * pairs, rows, 1), F32),
+            out((rows, width), F32),
+            out((rows, width), BF),
+            out((2, 1, width), F32),
+        ],
+        compiler_params=pltpu.CompilerParams(
+            collective_id=collective_id, has_side_effects=True, vmem_limit_bytes=VMEM_LIMIT
+        ),
+    )(live, prompt_x, cont_x, own_gain, *weights, table)
+
+
 SPAN = 4 * T
 VECTOR_ROWS = 8
 
@@ -659,7 +844,7 @@
         return pltpu.make_async_copy(source, stage, local.at[0])
 
     def weights_load(i):
-        return pltpu.make_async_copy(weights_hbm.at[i], w_buf.at[i], local.at[1 + i])
+        return pltpu.make_async_copy(weights_hbm.at[(2, 0, 1)[i]], w_buf.at[i], local.at[1 + i])
 
     def turn():
         def one(i, carry):
@@ -767,7 +952,7 @@
 
     @pl.when(step == last - 1)
     def _():
-        produce(fed, lambda m: attended[:, 2 * m * T : 2 * (m + 1) * T])
+        produce(fed, lambda m: jnp.concatenate([attended[2 * m], attended[2 * m + 1]], axis=1))
 
     @pl.when(step == last)
     def _():
@@ -843,12 +1028,11 @@
                 vector_out[...] = total[stages]
 
 
-def back(q, k, v, bias, grad, out, norm, branch, normed, parts, weights, d_middle, x_low, gain,
+def back(q, kv, bias, grad, out, norm, branch, normed, parts, weights, d_middle, x_low, gain,
          d_gain_two, live, shape, sizes, kept, collective_id):
     grp, seq = sizes
     rows, width = x_low.shape
-    inner = q.shape[1]
-    pairs = inner // (2 * HEAD)
+    pairs = q.shape[0]
     zs = grp // (Y * C)
     keys = shape.keys
     chunks, _, n, _, _, _, shard, lanes = parts.shape
@@ -864,6 +1048,10 @@
     vector = (2 * pairs + 2 * width // T // VECTOR_ROWS, VECTOR_ROWS, T)
     pair = lambda s: jnp.minimum(s // 2, pairs - 1)
     by_pair = lambda rows_: pl.BlockSpec((rows_, 2 * HEAD), lambda s, *_: (0, pair(s)))
+    in_pair = pl.BlockSpec((None, rows, 2 * HEAD), lambda s, *_: (pair(s), 0, 0))
+    of_keys = lambda side: pl.BlockSpec(
+        (None, None, keys, 2 * HEAD), lambda s, *_: (side, pair(s), 0, 0)
+    )
     row_block = lambda s: jnp.clip(s - last, 0, blocks - 1)
     by_rows = pl.BlockSpec((size, width), lambda s, *_: (row_block(s), 0))
     full = lambda *dims: pl.BlockSpec(
@@ -877,14 +1065,14 @@
             num_scalar_prefetch=1,
             grid=(steps,),
             in_specs=[
-                by_pair(rows),
-                by_pair(keys),
-                by_pair(keys),
+                in_pair,
+                of_keys(0),
+                of_keys(1),
                 pl.BlockSpec((2, BANDS, T, T), lambda s, *_: (pair(s), 0, 0, 0)),
                 by_pair(rows),
-                by_pair(rows),
+                in_pair,
                 pl.BlockSpec((2, rows, 1), lambda s, *_: (pair(s), 0, 0)),
-                full(rows, inner),
+                full(pairs, rows, 2 * HEAD),
                 anywhere,
                 anywhere,
                 anywhere,
@@ -926,7 +1114,7 @@
         compiler_params=pltpu.CompilerParams(
             collective_id=collective_id, has_side_effects=True, vmem_limit_bytes=VMEM_LIMIT
         ),
-    )(live, q, k, v, bias, grad, out, norm, out, branch, normed, parts, weights, d_middle,
+    )(live, q, kv, kv, bias, grad, out, norm, out, branch, normed, parts, weights, d_middle,
       x_low, gain, d_gain_two)
 
 
@@ -944,13 +1132,17 @@
     return a * half, slope
 
 
-def feed_load(x_hbm, dy_hbm, x, x_t, dy, dy_t, sem):
-    load_x = pltpu.make_async_copy(x_hbm, x, sem.at[0])
-    load_dy = pltpu.make_async_copy(dy_hbm, dy, sem.at[1])
-    load_x.start()
-    load_dy.start()
-    load_x.wait()
-    load_dy.wait()
+def feed_load(x_hbm, dy_parts, x, x_t, dy, dy_t, sem):
+    loads = [pltpu.make_async_copy(x_hbm, x, sem.at[0])]
+    start = 0
+    for i, part in enumerate(dy_parts):
+        target = dy.at[pl.ds(start, part.shape[0])]
+        loads.append(pltpu.make_async_copy(part, target, sem.at[1 + i]))
+        start += part.shape[0]
+    for load in loads:
+        load.start()
+    for load in loads:
+        load.wait()
 
     def turn(i, carry):
         part = pl.ds(pl.multiple_of(i * T, T), T)
@@ -1003,7 +1195,7 @@
 
     @pl.when(pl.program_id(0) == 0)
     def _():
-        feed_load(x_hbm, dy_hbm, x, x_t, dy, dy_t, sem)
+        feed_load(x_hbm, [dy_hbm], x, x_t, dy, dy_t, sem)
         out[...] = jnp.zeros_like(out)
         d_x[...] = jnp.zeros_like(d_x)
 
@@ -1025,7 +1217,7 @@
         pltpu.VMEM((rows, 2 * T), BF),
         pltpu.VMEM((rows, 2 * T), BF),
         pltpu.VMEM((rows, 2 * T), BF),
-        pltpu.SemaphoreType.DMA((2,)),
+        pltpu.SemaphoreType.DMA((3,)),
     ]
 
 
@@ -1050,10 +1242,10 @@
 
 
 def feed_moving_kernel(zs, xs, early, kept, *refs):
-    x_hbm, dy_hbm, own, ready, out, d_x, whole, parts, sums = refs[:9]
-    x, x_t, dy, dy_t, hidden, d_gate, d_up, sem = refs[9:17]
-    held, w_buf, g_buf, local = refs[17:21]
-    gather_sems, bufs, scatter_sems = refs[21:23], refs[23:30], refs[30:32]
+    x_hbm, dy_one, dy_two, own, ready, out, d_x, whole, parts, sums = refs[:10]
+    x, x_t, dy, dy_t, hidden, d_gate, d_up, sem = refs[10:18]
+    held, w_buf, g_buf, local = refs[18:22]
+    gather_sems, bufs, scatter_sems = refs[22:24], refs[24:31], refs[31:33]
     chunks = own.shape[0]
     place = Place(zs, xs)
     step = pl.program_id(0)
@@ -1077,19 +1269,21 @@
         store = pltpu.make_async_copy(held, mine, local.at[1])
         store.start()
         store.wait()
-        feed_load(x_hbm, dy_hbm, x, x_t, dy, dy_t, sem)
+        feed_load(x_hbm, [dy_one, dy_two], x, x_t, dy, dy_t, sem)
         out[...] = jnp.zeros_like(out)
         d_x[...] = jnp.zeros_like(d_x)
 
-    def weight_load(j, source):
-        return pltpu.make_async_copy(source.at[j], w_buf.at[j % 2], local.at[2 + j % 2])
+    skipped = ready.shape[0] - early
+
+    def weight_load(j, source, first=0):
+        return pltpu.make_async_copy(source.at[first + j], w_buf.at[j % 2], local.at[2 + j % 2])
 
     def start_load(j):
         if early > 0:
 
             @pl.when(j < early)
             def _():
-                weight_load(j, ready).start()
+                weight_load(j, ready, skipped).start()
 
         @pl.when(j >= early)
         def _():
@@ -1146,7 +1340,7 @@
             part_store(chunk).start()
 
 
-def feed_moving(x, dy, own, ready, sizes, early, kept, collective_id):
+def feed_moving(x, dy_one, dy_two, own, ready, sizes, early, kept, collective_id):
     grp, seq = sizes
     rows, width = x.shape
     chunks, _, n, shard, lanes = own.shape
@@ -1164,7 +1358,7 @@
     return pl.pallas_call(
         functools.partial(feed_moving_kernel, zs, seq, early, kept),
         grid=(steps,),
-        in_specs=[anywhere] * 4,
+        in_specs=[anywhere] * 5,
         out_specs=[whole, whole, anywhere, anywhere, sums],
         out_shape=[
             jax.ShapeDtypeStruct((rows, width), F32),
@@ -1187,7 +1381,7 @@
         compiler_params=pltpu.CompilerParams(
             collective_id=collective_id, has_side_effects=True, vmem_limit_bytes=VMEM_LIMIT
         ),
-    )(x, dy, own, ready)
+    )(x, dy_one, dy_two, own, ready)
 
 
 def rms_scale(values):
@@ -1254,69 +1448,39 @@
     tiles = local_tiles * seq
     seq_index = lax.axis_index("seq")
 
-    x_low = jnp.concatenate([prompt_x[0], cont_x[0].reshape(-1, width)], axis=0)
-    dy_low = jnp.concatenate([prompt_cot[0], cont_cot[0].reshape(-1, width)], axis=0)
-    x = x_low.astype(F32)
-    dy = dy_low.astype(F32)
-
-    lanes = jnp.zeros((shard, T - 2), F32)
-    gains = jnp.concatenate([norm1_gain[:, None], norm2_gain[:, None], lanes], axis=1)
-    own_attention = attention_chunks([q_weight, k_weight, v_weight, o_weight, gains]).astype(BF)
-    own_feed = feed_chunks([gate_weight, up_weight, down_weight]).astype(BF)
-    attention_whole = gather(own_attention, sizes, 0)
+    split = lambda rows: (
+        rows[:local_prompt][None],
+        rows[local_prompt:].reshape(1, conts, cont_rows, width),
+    )
+    shape = Shape(tiles, local_tiles, conts)
     count = inner // T
-    flat = attention_whole.reshape(-1, width, T)
-    q_full, k_full, v_full, o_full = [
-        joined(flat[i * count : (i + 1) * count]) for i in range(4)
-    ]
-    gain_one = flat[4 * count, :, 0].astype(F32)
-    gain_two = flat[4 * count, :, 1].astype(F32)
-
-    scale_one = rms_scale(x)
-    unit_one = x * scale_one
-    normed_one = (unit_one * gain_one).astype(BF)
-    kv = nn(normed_one, jnp.concatenate([k_full, v_full], axis=1)).astype(BF)
-    queries = nn(normed_one, q_full).astype(BF)
-    prompt_kv = kv[:local_prompt]
-    if seq == 2:
-        others = lax.ppermute(prompt_kv, "seq", [(0, 1), (1, 0)])
-    else:
-        gathered = lax.all_gather(prompt_kv, "seq", axis=0, tiled=True)
-        others = jnp.roll(gathered, -seq_index * local_prompt, axis=0)[local_prompt:]
-    every = jnp.concatenate([kv, others], axis=0)
-    keys, values = every[:, :inner], every[:, inner:]
-    base = (seq_index * local_tiles).reshape(1).astype(jnp.int32)
-
-    one_hot = band_one_hot(num_buckets)
-    bias = jnp.einsum("cqkb,bh->hcqk", one_hot, bucket_table, precision=lax.Precision.HIGHEST)
-    shape = Shape(tiles, local_tiles, conts)
-    attended, log_norm = attend(queries, keys, values, bias, cont_len, base, shape)
-    middle = x + nt(attended, o_full)
-    scale_two = rms_scale(middle)
-    unit_two = middle * scale_two
-    normed_two = (unit_two * gain_two).astype(BF)
-
-    moving = can_move(sizes, shard)
-    if moving:
-        kept = (6, 13)
+    if can_move(sizes, shard):
+        early, kept = 7, (9, 15)
+        own_gain = jnp.stack([norm1_gain, norm2_gain])[None, :, None, :, None]
+        own_gain = jnp.broadcast_to(own_gain, (1, 2, 1, shard, T)).astype(BF)
+        cont_dy = cont_cot[0].reshape(-1, width)
+        matrices = (q_weight, k_weight, v_weight, o_weight, gate_weight, up_weight, down_weight)
+        (whole, own_feed, x_low, normed_one, kv, bias, queries, attended, log_norm, middle,
+         normed_two, gains) = front(
+            prompt_x[0], cont_x[0].reshape(-1, width), own_gain, matrices, bucket_table, cont_len,
+            shape, sizes, early, 0,
+        )
+        gain_one, gain_two = gains[0], gains[1]
+        scale_two = rms_scale(middle)
+        unit_two = middle * scale_two
         out_sum, d_normed_two, _, feed_parts, kept_sums = feed_moving(
-            normed_two, dy_low, own_feed, own_feed, sizes, 0, kept, 1
+            normed_two, prompt_cot[0], cont_dy, own_feed, whole, sizes, early, kept, 1
         )
-    else:
-        feed_whole = gather(own_feed, sizes, 1)
-        out_sum, d_normed_two, feed_grads = feed(normed_two, dy_low, feed_whole)
-        feed_sums = scatter(feed_grads, sizes, shard, 3)
-    final = (middle + out_sum).astype(BF)
-
-    d_gain_two = jnp.sum(d_normed_two * unit_two, axis=0)
-    d_middle = dy + norm_back(d_normed_two, unit_two, scale_two, gain_two)
-    d_branch = d_middle.astype(BF)
-    d_attended = nn(d_branch, o_full).astype(BF)
-    if moving:
+        final = (middle + out_sum).astype(BF)
+        dy = jnp.concatenate([prompt_cot[0], cont_dy], axis=0).astype(F32)
+        d_gain_two = jnp.sum(d_normed_two * unit_two, axis=0)
+        d_middle = dy + norm_back(d_normed_two, unit_two, scale_two, gain_two)
+        d_branch = d_middle.astype(BF)
+        o_full = joined(whole[3].reshape(-1, width, T))
+        d_attended = nn(d_branch, o_full).astype(BF)
         d_x, sums, vector = back(
-            queries, keys, values, bias, d_attended, attended, log_norm, d_branch, normed_one,
-            feed_parts, attention_whole.reshape(-1, *feed_parts.shape[1:]), d_middle, x_low,
-            gain_one[None], d_gain_two[None], cont_len, shape, sizes, kept, 2,
+            queries, kv, bias, d_attended, attended, log_norm, d_branch, normed_one, feed_parts,
+            whole, d_middle, x_low, gain_one, d_gain_two[None], cont_len, shape, sizes, kept, 2,
         )
         fed = sums.shape[0] - 4
         feed_sums = jnp.concatenate([sums[: kept[0]], kept_sums, sums[kept[0] : fed]], axis=0)
@@ -1333,6 +1497,45 @@
         me = lax.axis_index("grp") * seq + seq_index
         norm1_grad, norm2_grad = lax.dynamic_index_in_dim(gain_grads, me, 1, keepdims=False)
     else:
+        x_low = jnp.concatenate([prompt_x[0], cont_x[0].reshape(-1, width)], axis=0)
+        dy_low = jnp.concatenate([prompt_cot[0], cont_cot[0].reshape(-1, width)], axis=0)
+        x = x_low.astype(F32)
+        dy = dy_low.astype(F32)
+        lanes = jnp.zeros((shard, T - 2), F32)
+        gains = jnp.concatenate([norm1_gain[:, None], norm2_gain[:, None], lanes], axis=1)
+        own_attention = attention_chunks([q_weight, k_weight, v_weight, o_weight, gains]).astype(BF)
+        own_feed = feed_chunks([gate_weight, up_weight, down_weight]).astype(BF)
+        attention_whole = gather(own_attention, sizes)
+        flat = attention_whole.reshape(-1, width, T)
+        q_full, k_full, v_full, o_full = [
+            joined(flat[i * count : (i + 1) * count]) for i in range(4)
+        ]
+        gain_one = flat[4 * count, :, 0].astype(F32)
+        gain_two = flat[4 * count, :, 1].astype(F32)
+        scale_one = rms_scale(x)
+        unit_one = x * scale_one
+        normed_one = (unit_one * gain_one).astype(BF)
+        kv = nn(normed_one, jnp.concatenate([k_full, v_full], axis=1)).astype(BF)
+        queries = nn(normed_one, q_full).astype(BF)
+        gathered = lax.all_gather(kv[:local_prompt], "seq", axis=0, tiled=True)
+        others = jnp.roll(gathered, -seq_index * local_prompt, axis=0)[local_prompt:]
+        every = jnp.concatenate([kv, others], axis=0)
+        keys, values = every[:, :inner], every[:, inner:]
+        base = (seq_index * local_tiles).reshape(1).astype(jnp.int32)
+        one_hot = band_one_hot(num_buckets)
+        bias = jnp.einsum("cqkb,bh->hcqk", one_hot, bucket_table, precision=lax.Precision.HIGHEST)
+        attended, log_norm = attend(queries, keys, values, bias, cont_len, base, shape)
+        middle = x + nt(attended, o_full)
+        scale_two = rms_scale(middle)
+        unit_two = middle * scale_two
+        normed_two = (unit_two * gain_two).astype(BF)
+        out_sum, d_normed_two, feed_grads = feed(normed_two, dy_low, gather(own_feed, sizes))
+        feed_sums = scatter(feed_grads)
+        final = (middle + out_sum).astype(BF)
+        d_gain_two = jnp.sum(d_normed_two * unit_two, axis=0)
+        d_middle = dy + norm_back(d_normed_two, unit_two, scale_two, gain_two)
+        d_branch = d_middle.astype(BF)
+        d_attended = nn(d_branch, o_full).astype(BF)
         d_o = tn(d_branch, attended)
         d_queries, d_keys, d_values, d_bias = attend_back(
             queries, keys, values, bias, d_attended, attended, log_norm, cont_len, base, shape
@@ -1350,7 +1553,7 @@
         d_x = d_middle + norm_back(d_normed_one, unit_one, scale_one, gain_one)
         d_x = d_x.astype(BF)
         attention_parts = attention_chunks([d_q, d_kv_weight, d_o]).astype(BF)
-        attention_sums = scatter(attention_parts, sizes, shard, 2).reshape(-1, shard, T)
+        attention_sums = scatter(attention_parts).reshape(-1, shard, T)
         norm1_grad = lax.psum_scatter(d_gain_one, ("grp", "seq"), scatter_dimension=0, tiled=True)
         norm2_grad = lax.psum_scatter(d_gain_two, ("grp", "seq"), scatter_dimension=0, tiled=True)
         table_grad = lax.psum(d_table, ("grp", "seq"))
@@ -1359,10 +1562,6 @@
     q_grad, k_grad, v_grad, o_grad = [
         joined(attention_sums[i * count : (i + 1) * count]) for i in range(4)
     ]
-    split = lambda rows: (
-        rows[:local_prompt][None],
-        rows[local_prompt:].reshape(1, conts, cont_rows, width),
-    )
     return (
         *split(final),
         *split(d_x),

time: 768 us -> 661 us (0.86)
  local copies, waits for them, and re-layouts: 65.4 us -> 27.9 us
  matrix products: 28.1 us -> 6.28 us
  Pallas kernels: 627 us -> 607 us
  other arithmetic: 38.1 us -> 18.1 us
    pallas_call x1, Pallas kernels: 281 us -> 200 us  [feed_moving(): pl.pallas_call(functools.partial(feed_moving_kernel, zs, seq, early, kept...]
    pallas_call x2 -> x1, Pallas kernels: 127 us -> 188 us  [front(): pl.pallas_call(functools.partial(front_kernel, zs, seq, shape, early), gr...]
    slice x8 -> x1, local copies, waits for them, and re-layouts: 23.2 us -> 4.78 us  [body(): o_full = joined(whole[3].reshape(-1, width, T))]
    dot_general x3 -> x1, matrix products: 16.5 us -> 5.38 us  [nn(): return jnp.dot(left, right, preferred_element_type=F32)]
    dot_general x2 -> x0, matrix products: 10.7 us -> none  [the longest x1 5.8 us: nt(): lax.dot_general(left, right, (((1,), (1,)), ((), ())), preferred_element_...]
  transfers between devices with their start and end apart: 1 -> 0, of which waited for: 1 -> 0; matrix products, arithmetic and copies ran while one was open for 4% -> 0% of each run, Pallas kernels for 0% -> 0%
where the time goes in v5:
time: 661 us; the launch traced here: 660 us
  Pallas kernels  607 us (92%)
  local copies, waits for them, and re-layouts  27.9 us (4%)
  other arithmetic  18.1 us (3%)
    pallas_call x1, Pallas kernels, back(): pl.pallas_call(functools.partial(back_kernel, zs, seq, shape, width, kept...  219 us
    pallas_call x1, Pallas kernels, feed_moving(): pl.pallas_call(functools.partial(feed_moving_kernel, zs, seq, early, kept...  200 us
    pallas_call x1, Pallas kernels, front(): pl.pallas_call(functools.partial(front_kernel, zs, seq, shape, early), gr...  188 us

profile of v5, /device:TPU:0, one launch (start us, length us, event | category | flops | bytes accessed | tf_op | source)
XLA Modules:
  0.0 660.5 jit_solution(7437829647133341313)
XLA Ops:
  0.6 0.7 convert_bitcast_fusion
  1.3 0.7 broadcast_in_dim.8.refs_2_
  2.0 1.4 copy.38.refs_10_
  3.4 188.2 %shard_map.263 = (bf16[11,2,3,4,2,4,48,128]{7,6,5,4,3,2,1,0:T(8,128)(2,1)}, bf16[16,2,3,48,128]{4,3,2,1,0:T(8,128)(2,1)}, bf16[1024,1536]{1,0:T(8,128)(2,1)}, bf...) custom-call(s32[1,4]{1,0:T(1,128)} %live.3, ...), custom_call_target="tpu_custom_call" | custom-call | tf_op jit(solution)/shard_map/pallas_call | solution.py:711
  191.6 200.4 %shard_map.264 = (f32[1024,1536]{1,0:T(8,128)}, f32[1024,1536]{1,0:T(8,128)}, bf16[16,2,3,4,2,4,48,128]{7,6,5,4,3,2,1,0:T(8,128)(2,1)}, bf16[16,2,3,4,2,4,48,128...) custom-call(bf16[1024,1536]{1,0:T(8,128)(2,1)} %get-tuple-element.34.refs_0_, bf16[512,1536]{1,0:T(8,128)(2,1)} %bitcast.79, ...), custom_call_target="tpu_custom_call" | custom-call | tf_op jit(solution)/shard_map/pallas_call | solution.py:1358
  392.0 3.4 multiply_reduce_fusion.2
  396.6 4.5 multiply_reduce_fusion
  401.2 9.2 %fusion.9 = (bf16[1024,1536]{1,0:T(8,128)(2,1)S(1)}, f32[1024,1536]{1,0:T(8,128)}, bf16[1024,1536]{1,0:T(8,128)(2,1)}) fusion(f32[1024]{0:T(1024)S(1)} %broadcast_multiply_fusion, f32[1024,1536]{1,0:T(8,128)S(1)} %bitcast.76, f32[1024,1536]{1,0:T(8,128)S(1)} %copy-done, f32[1536]{0:T(1024)S(1)} %get-tuple-element.72, f32[1024]{0:T(1024)S(1)} %add_rsqrt_fusion, ...), kind=kLoop, calls=%fused_computation.45 | loop fusion | flops 20447232 | bytes 34617344 | tf_op jit(solution)/shard_map/convert_element_type | solution.py:1478
  410.4 4.8 slice.86
  415.1 4.3 copy.39
  419.5 5.4 convolution_convert_fusion.refs_4_
  425.4 218.8 %shard_map.265 = (bf16[1024,1536]{1,0:T(8,128)(2,1)}, f32[14,2,3,48,128]{4,3,2,1,0:T(8,128)}, f32[15,8,128]{2,1,0:T(8,128)}) custom-call(s32[1,4]{1,0:T(1,128)} %live.3, bf16[6,1024,128]{2,1,0:T(8,128)(2,1)} %get-tuple-element.38.refs_0_, bf16[2,6,1536,128]{3,2,1,0:T(8,128)(2,1)} %get-tuple-element.39.refs_1_.refs_2_, ...), custom_call_target="tpu_custom_call" | custom-call | tf_op jit(solution)/shard_map/pallas_call | solution.py:1062
  644.3 1.5 slice.101
  645.8 1.3 fusion.13
  647.7 1.3 copy.65
  649.2 1.3 copy.66
  650.8 1.3 copy.67
  652.3 0.9 fusion
  653.2 1.9 fusion.10
  655.1 0.7 copy.68
  655.9 0.7 copy.69
  656.6 0.7 copy.70
  657.3 0.7 copy.71
  658.6 1.9 fusion.11
  (46 shorter events, 3.9 us)
Async XLA Ops:
  392.0 3.5 copy-start.7
  392.0 4.6 copy-start
  396.0 5.1 slice-start
  396.6 4.5 slice-start.1
  396.6 4.6 copy-start.3
  410.4 9.1 %copy-start.1 = (bf16[1024,1536]{1,0:T(8,128)(2,1)}, bf16[1024,1536]{1,0:T(8,128)(2,1)S(1)}, u32[]{:S(2)}) copy-start(bf16[1024,1536]{1,0:T(8,128)(2,1)S(1)} %get-tuple-element.54.refs_8_) | copy-start | bytes 9437188
  644.3 2.8 copy-start.5
  649.0 3.2 copy-start.6
  649.0 3.3 copy-start.8
  649.0 4.2 copy-start.4
  653.2 5.4 copy-start.2

commit v6 on v5

--- a/solution.py
+++ b/solution.py
@@ -108,16 +108,23 @@
     def copy(self, k, half, index, src, dst, device):
         return remote(src, dst, self.send.at[k, half, index], self.recv.at[k, half, index], device)
 
-    def along_z(self, k, half, d):
+    def alone(self, k, half):
         p = self.p
         dst = self.whole.at[k, half, :, p.z, p.y, p.c * p.xs + p.x]
-        return self.copy(k, half, d - 1, self.own.at[k, half], dst, p.device(z=(p.z + d) % p.zs))
+        src = self.own.at[k, half]
+        if half == 0:
+            return [self.copy(k, half, 0, src, dst, p.device(x=1 - p.x))]
+        peers = [p.device(z=(p.z + d) % p.zs) for d in range(1, p.zs)]
+        return [self.copy(k, half, i, src, dst, peer) for i, peer in enumerate(peers)]
 
     def second(self, k, half):
         p = self.p
+        if half == 0:
+            view = self.whole.at[k, half, :, p.z, p.y, pl.ds(p.c * p.xs, p.xs)]
+            peers = [p.device(z=(p.z + d) % p.zs) for d in range(1, p.zs)]
+            return [self.copy(k, half, 1 + i, view, view, peer) for i, peer in enumerate(peers)]
         view = self.whole.at[k, half, :, :, p.y, p.c * p.xs + p.x]
-        peer = p.device(x=1 - p.x) if half == 0 else p.device(y=1 - p.y)
-        return self.copy(k, half, p.zs - 1, view, view, peer)
+        return [self.copy(k, half, p.zs - 1, view, view, p.device(y=1 - p.y))]
 
     def third(self, k, half):
         p = self.p
@@ -127,46 +134,31 @@
         else:
             view = self.whole.at[k, half, :, :, :, p.c * p.xs + p.x]
             peer = p.device(x=1 - p.x)
-        return self.copy(k, half, p.zs, view, view, peer)
+        return [self.copy(k, half, p.zs, view, view, peer)]
 
     def fourth(self, k, half):
         p = self.p
         view = self.whole.at[k, half, :, :, :, pl.ds(p.c * p.xs, p.xs)]
-        return self.copy(k, half, p.zs + 1, view, view, p.device(c=1 - p.c))
+        return [self.copy(k, half, p.zs + 1, view, view, p.device(c=1 - p.c))]
 
     def tick(self, step, first, end):
-        def start_z(k):
+        stages = (self.alone, self.second, self.third, self.fourth)
+
+        def advance(offset, k):
             for half in (0, 1):
-                for d in range(1, self.p.zs):
-                    self.along_z(k, half, d).start()
-
-        def start_second(k):
-            for half in (0, 1):
-                for d in range(1, self.p.zs):
-                    self.along_z(k, half, d).wait_recv()
-                self.second(k, half).start()
-
-        def start_third(k):
-            for half in (0, 1):
-                self.second(k, half).wait_recv()
-                self.third(k, half).start()
-
-        def start_fourth(k):
-            for half in (0, 1):
-                self.third(k, half).wait_recv()
-                self.fourth(k, half).start()
-
-        def finish(k):
-            for half in (0, 1):
-                self.fourth(k, half).wait_recv()
-                for d in range(1, self.p.zs):
-                    self.along_z(k, half, d).wait_send()
-                self.second(k, half).wait_send()
-                self.third(k, half).wait_send()
-                self.fourth(k, half).wait_send()
-
-        for offset, action in enumerate((start_z, start_second, start_third, start_fourth, finish)):
-            staged(step, offset, end - first, lambda k, action=action: action(first + k))
+                if offset > 0:
+                    for copy in stages[offset - 1](k, half):
+                        copy.wait_recv()
+                if offset < 4:
+                    for copy in stages[offset](k, half):
+                        copy.start()
+                else:
+                    for stage in stages:
+                        for copy in stage(k, half):
+                            copy.wait_send()
+
+        for offset in range(5):
+            staged(step, offset, end - first, lambda k, offset=offset: advance(offset, first + k))
 
 
 def gather(own, sizes):
@@ -176,7 +168,8 @@
 class Scatter:
     def __init__(self, place, bufs, send, recv, out):
         self.p, self.send, self.recv, self.out = place, send, recv, out
-        (self.in1, self.in2, self.in3, self.in4, self.sum1, self.sum2, self.sum3) = bufs
+        (self.in1, self.in2, self.sum1, self.sum2) = bufs[:4]
+        self.in3, self.in4, self.sum3 = bufs[4:6], bufs[6:8], bufs[8:10]
 
     def copy(self, k, half, index, src, dst, device):
         slot = k % 2
@@ -198,49 +191,61 @@
         return self.copy(k, half, 1, src, self.in2.at[k % 2, half], peer)
 
     def third(self, k, half):
-        p = self.p
-        other = 1 - p.x if half == 0 else 1 - p.y
-        peer = p.device(x=1 - p.x) if half == 0 else p.device(y=1 - p.y)
-        src = self.sum2.at[k % 2, half, :, :, other]
-        return self.copy(k, half, 2, src, self.in3.at[k % 2, half], peer)
-
-    def fourth(self, k, half, d):
-        p = self.p
-        target = (p.z + d) % p.zs
-        src = self.sum3.at[k % 2, half, :, target]
-        dst = self.in4.at[k % 2, half, d - 1]
-        return self.copy(k, half, 2 + d, src, dst, p.device(z=target))
+        p, slot = self.p, k % 2
+        if half == 1:
+            src = self.sum2.at[slot, half, :, :, 1 - p.y]
+            return [self.copy(k, half, 2, src, self.in3[1].at[slot], p.device(y=1 - p.y))]
+        copies = []
+        for d in range(1, p.zs):
+            target = (p.z + d) % p.zs
+            src = self.sum2.at[slot, half, :, target]
+            dst = self.in3[0].at[slot, d - 1]
+            copies.append(self.copy(k, half, 1 + d, src, dst, p.device(z=target)))
+        return copies
+
+    def fourth(self, k, half):
+        p, slot = self.p, k % 2
+        if half == 0:
+            src = self.sum3[0].at[slot, :, 1 - p.x]
+            return [self.copy(k, half, p.zs + 1, src, self.in4[0].at[slot, 0], p.device(x=1 - p.x))]
+        copies = []
+        for d in range(1, p.zs):
+            target = (p.z + d) % p.zs
+            src = self.sum3[1].at[slot, :, target]
+            dst = self.in4[1].at[slot, d - 1]
+            copies.append(self.copy(k, half, 2 + d, src, dst, p.device(z=target)))
+        return copies
 
     def finish(self, k):
-        p = self.p
-        slot = k % 2
+        p, slot = self.p, k % 2
         for half in (0, 1):
-            total = self.sum3[slot, half, :, p.z].astype(F32)
-            for d in range(1, p.zs):
-                copy = self.fourth(k, half, d)
+            total = self.sum3[half][slot, :, p.x if half == 0 else p.z].astype(F32)
+            for i, copy in enumerate(self.fourth(k, half)):
                 copy.wait_recv()
                 copy.wait_send()
-                total = total + self.in4[slot, half, d - 1].astype(F32)
+                total = total + self.in4[half][slot, i].astype(F32)
             self.out[k, half] = total
 
     def start_fourth(self, k):
-        p = self.p
-        slot = k % 2
+        p, slot = self.p, k % 2
         for half in (0, 1):
-            copy = self.third(k, half)
-            copy.wait_recv()
-            copy.wait_send()
-            keep = p.x if half == 0 else p.y
-            for i in range(self.sum3.shape[2]):
-                total = self.sum2[slot, half, i, :, keep].astype(F32)
-                total = total + self.in3[slot, half, i].astype(F32)
-                self.sum3[slot, half, i] = total.astype(BF)
-            for d in range(1, p.zs):
-                self.fourth(k, half, d).start()
+            for copy in self.third(k, half):
+                copy.wait_recv()
+                copy.wait_send()
+            for i in range(self.sum2.shape[2]):
+                if half == 0:
+                    total = self.sum2[slot, half, i, p.z].astype(F32)
+                    for d in range(1, p.zs):
+                        total = total + self.in3[0][slot, d - 1, i].astype(F32)
+                else:
+                    total = self.sum2[slot, half, i, :, p.y].astype(F32)
+                    total = total + self.in3[1][slot, i].astype(F32)
+                self.sum3[half][slot, i] = total.astype(BF)
+            for copy in self.fourth(k, half):
+                copy.start()
 
     def start_third(self, k):
-        p = self.p
-        slot = k % 2
+        p, slot = self.p, k % 2
         for half in (0, 1):
             copy = self.second(k, half)
             copy.wait_recv()
@@ -252,11 +257,11 @@
                     mine = self.sum1[slot, half, i, :, :, p.x]
                 total = mine.astype(F32) + self.in2[slot, half, i].astype(F32)
                 self.sum2[slot, half, i] = total.astype(BF)
-            self.third(k, half).start()
+            for copy in self.third(k, half):
+                copy.start()
 
     def start_second(self, k, part):
-        p = self.p
-        slot = k % 2
+        p, slot = self.p, k % 2
         for half in (0, 1):
             copy = self.first(k, half, part)
             copy.wait_recv()
@@ -277,15 +282,22 @@
             self.first(k, half, part).start()
 
 
+BUFFERS = 10
+
+
 def scatter_buffers(n, zs, xs, rows, lanes):
+    block = (rows, lanes)
     shapes = [
-        (2, 2, n, zs, Y, xs, rows, lanes),
-        (2, 2, n, zs, 2, rows, lanes),
-        (2, 2, n, zs, rows, lanes),
-        (2, 2, zs - 1, n, rows, lanes),
-        (2, 2, n, zs, Y, xs, rows, lanes),
-        (2, 2, n, zs, 2, rows, lanes),
-        (2, 2, n, zs, rows, lanes),
+        (2, 2, n, zs, Y, xs, *block),
+        (2, 2, n, zs, 2, *block),
+        (2, 2, n, zs, Y, xs, *block),
+        (2, 2, n, zs, 2, *block),
+        (2, zs - 1, n, 2, *block),
+        (2, n, zs, *block),
+        (2, 1, n, *block),
+        (2, zs - 1, n, *block),
+        (2, n, 2, *block),
+        (2, n, zs, *block),
     ]
     return [pltpu.VMEM(shape, BF) for shape in shapes]
 
@@ -784,6 +796,22 @@
     return jnp.concatenate(rows + [jnp.zeros((2, T), F32)], axis=0)
 
 
+def put(i, first_blocks, targets, value):
+    @pl.when(i < first_blocks)
+    def _():
+        targets[0][...] = value
+
+    @pl.when(i >= first_blocks)
+    def _():
+        targets[1][...] = value
+
+
+def two_parts(size, width, first_blocks, blocks, first_step):
+    one = lambda s, *_: (jnp.clip(s - first_step, 0, first_blocks - 1), 0)
+    two = lambda s, *_: (jnp.clip(s - first_step - first_blocks, 0, blocks - first_blocks - 1), 0)
+    return [pl.BlockSpec((size, width), one), pl.BlockSpec((size, width), two)]
+
+
 def rows_of(vector):
     return [vector[:, i * T : (i + 1) * T] for i in range(vector.shape[1] // T)]
 
@@ -822,11 +850,11 @@
 def back_kernel(zs, xs, shape, width, kept, live, *refs):
     q, k, v, bias, grad, out, norm, attended, branch_hbm, normed_hbm, parts, weights_hbm = refs[:12]
     d_middle, x_low, gain, d_gain_two = refs[12:16]
-    d_x, sums, vector_out = refs[16:19]
-    (stage, turn_buf, d_q, d_kv, back_kv, k_sum, v_sum, d_bias) = refs[19:27]
-    (w_buf, held, vector, total, arrived, gain_sum) = refs[27:33]
-    (local, loads, kv_sems, both_sems) = refs[33:37]
-    bufs, scatter_sems = refs[37:44], refs[44:46]
+    d_x, (sums, vector_out) = refs[16:18], refs[18:20]
+    (stage, turn_buf, d_q, d_kv, back_kv, k_sum, v_sum, d_bias) = refs[20:28]
+    (w_buf, held, vector, total, arrived, gain_sum) = refs[28:34]
+    (local, loads, kv_sems, both_sems) = refs[34:38]
+    bufs, scatter_sems = refs[38 : 38 + BUFFERS], refs[38 + BUFFERS :]
     place = Place(zs, xs)
     step = pl.program_id(0)
     rows, keys = shape.rows, shape.keys
@@ -836,9 +864,8 @@
     turns = rows // T
     first_kept, end_kept = kept
     fed = parts.shape[0] - (end_kept - first_kept)
-    group_two = last - 1
-    count = fed + 4
-    blocks = rows // d_x.shape[0]
+    size = d_x[0].shape[0]
+    blocks = rows // size
 
     def stage_load(source):
         return pltpu.make_async_copy(source, stage, local.at[0])
@@ -854,31 +881,29 @@
 
         lax.fori_loop(0, turns, one, 0)
 
+    def part_load(c):
+        j = jnp.where(c < first_kept, c, c + end_kept - first_kept)
+        return pltpu.make_async_copy(parts.at[j], held.at[c % 3], loads.at[c % 3])
+
     @pl.when(step == 0)
     def _():
+        part_load(step).start()
         stage_load(branch_hbm).start()
         place.barrier()
         for i in range(3):
             weights_load(i).start()
-        stage_load(branch_hbm).wait()
-        turn()
-        stage_load(normed_hbm).start()
 
     engine = Scatter(place, bufs, *scatter_sems, sums)
 
     def due(offset, action):
         at = step - offset
-        chunk = jnp.where(at < group_two, at, at - group_two + fed)
+        chunk = jnp.where(at < last, at, at - last + fed)
         early = (at >= 0) & (at < fed)
-        late = (at >= group_two) & (at < group_two + 4)
+        late = (at >= last) & (at < last + 4)
 
         @pl.when(early | late)
         def _():
             action(chunk)
-
-    def part_load(c):
-        j = jnp.where(c < first_kept, c, c + end_kept - first_kept)
-        return pltpu.make_async_copy(parts.at[j], held.at[c % 3], loads.at[c % 3])
 
     def first(c):
         @pl.when(c < fed)
@@ -887,15 +912,21 @@
 
         engine.start_first(c, held.at[c % 3])
 
-    due(5, engine.finish)
-    due(4, engine.start_fourth)
-    due(3, engine.start_third)
-    due(2, lambda c: engine.start_second(c, held.at[c % 3]))
-    due(1, first)
-
-    @pl.when(step < fed)
-    def _():
-        part_load(step).start()
+    due(4, engine.finish)
+    due(3, engine.start_fourth)
+    due(2, engine.start_third)
+    due(1, lambda c: engine.start_second(c, held.at[c % 3]))
+    due(0, first)
+
+    @pl.when(step + 1 < fed)
+    def _():
+        part_load(step + 1).start()
+
+    @pl.when(step == 0)
+    def _():
+        stage_load(branch_hbm).wait()
+        turn()
+        stage_load(normed_hbm).start()
 
     def kv_send(p):
         src = d_kv.at[p, :, pl.ds(rows, keys - rows)]
@@ -982,7 +1013,6 @@
 
     @pl.when((step >= last) & (step < last + blocks))
     def _():
-        size = d_x.shape[0]
         part = pl.ds(pl.multiple_of((step - last) * size, size), size)
         d_normed = None
         for i in range(3):
@@ -1001,7 +1031,8 @@
         gain_sum[...] += jnp.sum(d_normed * unit, axis=0, keepdims=True)
         d_unit = d_normed * gain[...]
         inner = jnp.mean(d_unit * unit, axis=-1, keepdims=True)
-        d_x[...] = (d_middle[...] + scale * (d_unit - unit * inner)).astype(BF)
+        value = (d_middle[...] + scale * (d_unit - unit * inner)).astype(BF)
+        put(step - last, prompt // size, d_x, value)
 
     mix = Combine(place, total, arrived, both_sems.at[0], both_sems.at[1])
     start = last + blocks
@@ -1037,11 +1068,13 @@
     keys = shape.keys
     chunks, _, n, _, _, _, shard, lanes = parts.shape
     count = chunks - (kept[1] - kept[0]) + 4
-    assert chunks - (kept[1] - kept[0]) <= 2 * pairs - 1
+    assert chunks - (kept[1] - kept[0]) <= 2 * pairs
     assert (pairs, n) == (6, 3) and 2 * width // T % VECTOR_ROWS == 0
     last = 2 * pairs
     size = min(rows, 256)
     blocks = rows // size
+    prompt = shape.local_tiles * T
+    assert prompt % size == 0
     tile = (2, n, zs, Y, C * seq, shard, lanes)
     stages = 3 + (zs - 1).bit_length()
     steps = last + blocks + stages + 2
@@ -1082,7 +1115,8 @@
                 full(1, width),
                 full(1, width),
             ],
-            out_specs=[by_rows, full(count, 2, n, shard, lanes), full(*vector)],
+            out_specs=two_parts(size, width, prompt // size, blocks, last)
+            + [full(count, 2, n, shard, lanes), full(*vector)],
             scratch_shapes=[
                 pltpu.VMEM((rows, width), BF),
                 pltpu.VMEM((width, rows), BF),
@@ -1107,7 +1141,8 @@
             + [sems(2, 2, zs + 2), sems(2, 2, zs + 2)],
         ),
         out_shape=[
-            jax.ShapeDtypeStruct((rows, width), BF),
+            jax.ShapeDtypeStruct((prompt, width), BF),
+            jax.ShapeDtypeStruct((rows - prompt, width), BF),
             jax.ShapeDtypeStruct((count, 2, n, shard, lanes), F32),
             jax.ShapeDtypeStruct(vector, F32),
         ],
@@ -1242,10 +1277,12 @@
 
 
 def feed_moving_kernel(zs, xs, early, kept, *refs):
-    x_hbm, dy_one, dy_two, own, ready, out, d_x, whole, parts, sums = refs[:10]
-    x, x_t, dy, dy_t, hidden, d_gate, d_up, sem = refs[10:18]
-    held, w_buf, g_buf, local = refs[18:22]
-    gather_sems, bufs, scatter_sems = refs[22:24], refs[24:31], refs[31:33]
+    x_hbm, dy_one, dy_two, own, ready, middle, gain, whole, parts, sums = refs[:10]
+    final, (d_middle, d_branch, d_attended, d_gain) = refs[10:12], refs[12:16]
+    x, x_t, dy, dy_t, hidden, d_gate, d_up, sem = refs[16:24]
+    out, d_x, held, w_buf, g_buf, local = refs[24:30]
+    gather_sems, bufs = refs[30:32], refs[32 : 32 + BUFFERS]
+    scatter_sems = refs[32 + BUFFERS :]
     chunks = own.shape[0]
     place = Place(zs, xs)
     step = pl.program_id(0)
@@ -1339,40 +1376,90 @@
         def _():
             part_store(chunk).start()
 
-
-def feed_moving(x, dy_one, dy_two, own, ready, sizes, early, kept, collective_id):
+    spare = chunks % 2
+    rows, size = x.shape[0], middle.shape[0]
+    blocks = rows // size
+
+    def o_load():
+        return pltpu.make_async_copy(ready.at[skipped - 1], w_buf.at[spare], local.at[6])
+
+    @pl.when(chunk == chunks - 1)
+    def _():
+        o_load().start()
+        d_gain[...] = jnp.zeros_like(d_gain)
+
+    @pl.when(chunk == chunks)
+    def _():
+        o_load().wait()
+
+    @pl.when((chunk >= chunks) & (chunk < chunks + blocks))
+    def _():
+        i = chunk - chunks
+        part = pl.ds(pl.multiple_of(i * size, size), size)
+        values = middle[...]
+        put(i, dy_one.shape[0] // size, final, (values + out[part, :]).astype(BF))
+        scale = rms_scale(values)
+        unit = values * scale
+        d_normed = d_x[part, :]
+        d_gain[...] += jnp.sum(d_normed * unit, axis=0, keepdims=True)
+        total = dy[part, :].astype(F32) + norm_back(d_normed, unit, scale, gain[...])
+        d_middle[...] = total
+        low = total.astype(BF)
+        d_branch[...] = low
+        for m in range(d_attended.shape[1] // (2 * T)):
+            right = joined_pieces(w_buf, spare, m)
+            d_attended[:, 2 * m * T : 2 * (m + 1) * T] = nn(low, right).astype(BF)
+
+
+def feed_moving(x, dy_one, dy_two, own, ready, middle, gain, inner, sizes, early, kept, collective_id):
     grp, seq = sizes
     rows, width = x.shape
     chunks, _, n, shard, lanes = own.shape
     zs = grp // (Y * C)
     tile = (2, n, zs, Y, C * seq, shard, lanes)
-    whole = pl.BlockSpec((rows, width), lambda j: (0, 0), pipeline_mode=pl.Buffered(1))
+    one = pl.BlockSpec((1, width), lambda j: (0, 0), pipeline_mode=pl.Buffered(1))
     number = kept[1] - kept[0]
     sums = pl.BlockSpec(
         (number, 2, n, shard, lanes), lambda j: (0,) * 5, pipeline_mode=pl.Buffered(1)
     )
     lag = max(0, 5 - early)
-    steps = lag + max(chunks + 2, kept[1] + 5)
+    size = min(rows, 256)
+    blocks = rows // size
+    assert dy_one.shape[0] % size == 0
+    steps = lag + max(chunks + max(2, blocks), kept[1] + 5)
+    tail = lag + chunks
+    by_rows = lambda columns: pl.BlockSpec(
+        (size, columns), lambda j: (jnp.clip(j - tail, 0, blocks - 1), 0)
+    )
+    out = jax.ShapeDtypeStruct
     anywhere = pl.BlockSpec(memory_space=pl.ANY)
     sems = lambda *shape: pltpu.SemaphoreType.DMA(shape)
     return pl.pallas_call(
         functools.partial(feed_moving_kernel, zs, seq, early, kept),
         grid=(steps,),
-        in_specs=[anywhere] * 5,
-        out_specs=[whole, whole, anywhere, anywhere, sums],
+        in_specs=[anywhere] * 5 + [by_rows(width), one],
+        out_specs=[anywhere, anywhere, sums]
+        + two_parts(size, width, dy_one.shape[0] // size, blocks, tail)
+        + [by_rows(width), by_rows(width), by_rows(inner), one],
         out_shape=[
-            jax.ShapeDtypeStruct((rows, width), F32),
-            jax.ShapeDtypeStruct((rows, width), F32),
-            jax.ShapeDtypeStruct((chunks, *tile), BF),
-            jax.ShapeDtypeStruct((chunks, *tile), BF),
-            jax.ShapeDtypeStruct((number, 2, n, shard, lanes), F32),
+            out((chunks, *tile), BF),
+            out((chunks, *tile), BF),
+            out((number, 2, n, shard, lanes), F32),
+            out(dy_one.shape, BF),
+            out(dy_two.shape, BF),
+            out((rows, width), F32),
+            out((rows, width), BF),
+            out((rows, inner), BF),
+            out((1, width), F32),
         ],
         scratch_shapes=feed_scratch(rows, width)
         + [
+            pltpu.VMEM((rows, width), F32),
+            pltpu.VMEM((rows, width), F32),
             pltpu.VMEM(own.shape, BF),
             pltpu.VMEM((2, *tile), BF),
             pltpu.VMEM((2, *tile), BF),
-            sems(6),
+            sems(7),
             sems(chunks, 2, zs + 2),
             sems(chunks, 2, zs + 2),
         ]
@@ -1381,7 +1468,7 @@
         compiler_params=pltpu.CompilerParams(
             collective_id=collective_id, has_side_effects=True, vmem_limit_bytes=VMEM_LIMIT
         ),
-    )(x, dy_one, dy_two, own, ready)
+    )(x, dy_one, dy_two, own, ready, middle, gain)
 
 
 def rms_scale(values):
@@ -1448,10 +1535,8 @@
     tiles = local_tiles * seq
     seq_index = lax.axis_index("seq")
 
-    split = lambda rows: (
-        rows[:local_prompt][None],
-        rows[local_prompt:].reshape(1, conts, cont_rows, width),
-    )
+    split = lambda parts: (parts[0][None], parts[1].reshape(1, conts, cont_rows, width))
+    cut = lambda values: (values[:local_prompt], values[local_prompt:])
     shape = Shape(tiles, local_tiles, conts)
     count = inner // T
     if can_move(sizes, shard):
@@ -1465,22 +1550,13 @@
             prompt_x[0], cont_x[0].reshape(-1, width), own_gain, matrices, bucket_table, cont_len,
             shape, sizes, early, 0,
         )
-        gain_one, gain_two = gains[0], gains[1]
-        scale_two = rms_scale(middle)
-        unit_two = middle * scale_two
-        out_sum, d_normed_two, _, feed_parts, kept_sums = feed_moving(
-            normed_two, prompt_cot[0], cont_dy, own_feed, whole, sizes, early, kept, 1
+        _, feed_parts, kept_sums, *final, d_middle, d_branch, d_attended, d_gain_two = feed_moving(
+            normed_two, prompt_cot[0], cont_dy, own_feed, whole, middle, gains[1], inner, sizes,
+            early, kept, 1,
         )
-        final = (middle + out_sum).astype(BF)
-        dy = jnp.concatenate([prompt_cot[0], cont_dy], axis=0).astype(F32)
-        d_gain_two = jnp.sum(d_normed_two * unit_two, axis=0)
-        d_middle = dy + norm_back(d_normed_two, unit_two, scale_two, gain_two)
-        d_branch = d_middle.astype(BF)
-        o_full = joined(whole[3].reshape(-1, width, T))
-        d_attended = nn(d_branch, o_full).astype(BF)
-        d_x, sums, vector = back(
+        *d_x, sums, vector = back(
             queries, kv, bias, d_attended, attended, log_norm, d_branch, normed_one, feed_parts,
-            whole, d_middle, x_low, gain_one, d_gain_two[None], cont_len, shape, sizes, kept, 2,
+            whole, d_middle, x_low, gains[0], d_gain_two, cont_len, shape, sizes, kept, 2,
         )
         fed = sums.shape[0] - 4
         feed_sums = jnp.concatenate([sums[: kept[0]], kept_sums, sums[kept[0] : fed]], axis=0)
@@ -1531,7 +1607,7 @@
         normed_two = (unit_two * gain_two).astype(BF)
         out_sum, d_normed_two, feed_grads = feed(normed_two, dy_low, gather(own_feed, sizes))
         feed_sums = scatter(feed_grads)
-        final = (middle + out_sum).astype(BF)
+        final = cut((middle + out_sum).astype(BF))
         d_gain_two = jnp.sum(d_normed_two * unit_two, axis=0)
         d_middle = dy + norm_back(d_normed_two, unit_two, scale_two, gain_two)
         d_branch = d_middle.astype(BF)
@@ -1551,7 +1627,7 @@
         d_kv_weight = tn(normed_one, d_kv)
         d_gain_one = jnp.sum(d_normed_one * unit_one, axis=0)
         d_x = d_middle + norm_back(d_normed_one, unit_one, scale_one, gain_one)
-        d_x = d_x.astype(BF)
+        d_x = cut(d_x.astype(BF))
         attention_parts = attention_chunks([d_q, d_kv_weight, d_o]).astype(BF)
         attention_sums = scatter(attention_parts).reshape(-1, shard, T)
         norm1_grad = lax.psum_scatter(d_gain_one, ("grp", "seq"), scatter_dimension=0, tiled=True)

time: 661 us -> 626 us (0.947)
  other arithmetic: 18.1 us -> 0.96 us
  local copies, waits for them, and re-layouts: 27.9 us -> 20.8 us
    convert_element_type x1 -> x0, other arithmetic: 9.18 us -> none  [body(): d_branch = d_middle.astype(BF)]
    pallas_call x1, Pallas kernels: 188 us -> 180 us  [front(): pl.pallas_call(functools.partial(front_kernel, zs, seq, shape, early), gr...]
    slice x3 -> x0, local copies, waits for them, and re-layouts: 8.51 us -> none  [the longest x1 4.78 us: body(): o_full = joined(whole[3].reshape(-1, width, T))]
    reduce_sum x2 -> x0, other arithmetic: 7.91 us -> none  [the longest x1 4.5 us: body(): d_gain_two = jnp.sum(d_normed_two * unit_two, axis=0)]
    unnamed x35 -> x31, local copies, waits for them, and re-layouts: 9.52 us -> 15.1 us
where the time goes in v6:
time: 626 us
  Pallas kernels  602 us (96%)
  local copies, waits for them, and re-layouts  20.8 us (3%)
    pallas_call x1, Pallas kernels, back(): pl.pallas_call(functools.partial(back_kernel, zs, seq, shape, width, kept...  216 us
    pallas_call x1, Pallas kernels, feed_moving(): pl.pallas_call(functools.partial(feed_moving_kernel, zs, seq, early, kept...  207 us
    pallas_call x1, Pallas kernels, front(): pl.pallas_call(functools.partial(front_kernel, zs, seq, shape, early), gr...  180 us
    unnamed x31, local copies, waits for them, and re-layouts  15.1 us

profile of v6, /device:TPU:0, one launch (start us, length us, event | category | flops | bytes accessed | tf_op | source)
XLA Modules:
  0.0 625.7 jit_solution(4761347465944213277)
XLA Ops:
  0.6 0.7 convert_bitcast_fusion
  1.3 0.7 broadcast_in_dim.6.refs_2_
  2.0 1.4 copy.38.refs_10_
  3.4 179.5 %shard_map.263 = (bf16[11,2,3,4,2,4,48,128]{7,6,5,4,3,2,1,0:T(8,128)(2,1)}, bf16[16,2,3,48,128]{4,3,2,1,0:T(8,128)(2,1)}, bf16[1024,1536]{1,0:T(8,128)(2,1)}, bf...) custom-call(s32[1,4]{1,0:T(1,128)} %live.3, ...), custom_call_target="tpu_custom_call" | custom-call | tf_op jit(solution)/shard_map/pallas_call | solution.py:723
  182.9 1.3 slice_bitcast_fusion
  184.3 206.6 %shard_map.264 = (bf16[16,2,3,4,2,4,48,128]{7,6,5,4,3,2,1,0:T(8,128)(2,1)}, bf16[16,2,3,4,2,4,48,128]{7,6,5,4,3,2,1,0:T(8,128)(2,1)}, f32[6,2,3,48,128]{4,3,2,1,...) custom-call(bf16[1024,1536]{1,0:T(8,128)(2,1)} %get-tuple-element.38, ...), custom_call_target="tpu_custom_call" | custom-call | tf_op jit(solution)/shard_map/pallas_call | solution.py:1437
  390.9 216.1 %shard_map.265 = (bf16[512,1536]{1,0:T(8,128)(2,1)}, bf16[512,1536]{1,0:T(8,128)(2,1)}, f32[14,2,3,48,128]{4,3,2,1,0:T(8,128)}, f32[15,8,128]{2,1,0:T(8,128)}) custom-call(s32[1,4]{1,0:T(1,128)} %live.3, bf16[6,1024,128]{2,1,0:T(8,128)(2,1)} %get-tuple-element.45.refs_0_, bf16[2,6,1536,128]{3,2,1,0:T(8,128)(2,1)} %get-tuple-element.46.refs_1_.refs_2_, ...), custom_call_target="tpu_custom_call" | custom-call | tf_op jit(solution)/shard_map/pallas_call | solution.py:1095
  607.0 1.5 slice.81
  608.5 1.3 fusion.10
  610.3 1.3 copy.64
  611.9 1.3 copy.65
  613.5 1.3 copy.66
  615.0 0.9 fusion
  616.0 0.7 copy.67
  616.7 0.7 copy.68
  617.4 0.7 copy.69
  618.2 0.7 copy.70
  619.0 0.5 dynamic-slice_bitcast_fusion
  619.5 1.1 copy.75
  620.6 1.1 copy.76
  621.8 0.8 copy-done.3
  622.6 1.1 copy.77
  623.8 0.8 copy-done.2
  624.6 1.1 copy.78
  (30 shorter events, 1.5 us)
Async XLA Ops:
  607.0 2.8 copy-start.4
  611.9 2.9 copy-start.5
  611.9 3.1 copy-start.6
  613.5 6.0 copy-start.1
  617.4 3.2 copy-start
  620.6 2.0 copy-start.3
  622.6 2.0 copy-start.2

commit v7 on v6

--- a/solution.py
+++ b/solution.py
@@ -224,7 +224,7 @@
                 copy.wait_recv()
                 copy.wait_send()
                 total = total + self.in4[half][slot, i].astype(F32)
-            self.out[k, half] = total
+            self.out(k, half, total)
 
     def start_fourth(self, k):
         p, slot = self.p, k % 2
@@ -817,40 +817,44 @@
 
 
 class Combine:
+    STAGES = 4
+
     def __init__(self, place, total, arrived, send, recv):
         self.p, self.total, self.arrived, self.send, self.recv = place, total, arrived, send, recv
 
-    def partners(self):
+    def copies(self, i):
         p = self.p
-        found = [p.device(c=1 - p.c), p.device(x=1 - p.x), p.device(y=1 - p.y)]
-        bit = 1
-        while bit < p.zs:
-            found.append(p.device(z=p.z + bit - 2 * bit * ((p.z // bit) % 2)))
-            bit *= 2
-        return found
-
-    def copy(self, i):
-        return remote(
-            self.total.at[i],
-            self.arrived.at[i],
-            self.send.at[i],
-            self.recv.at[i],
-            self.partners()[i],
-        )
+        if i < 3:
+            peers = [(i, (p.device(c=1 - p.c), p.device(x=1 - p.x), p.device(y=1 - p.y))[i])]
+        else:
+            peers = [(3 + d, p.device(z=(p.z + d) % p.zs)) for d in range(1, p.zs)]
+        return [
+            remote(self.total.at[i], self.arrived.at[at], self.send.at[at], self.recv.at[at], peer)
+            for at, peer in peers
+        ]
 
     def start(self, i):
-        self.copy(i).start()
+        for copy in self.copies(i):
+            copy.start()
 
     def finish(self, i):
-        self.copy(i).wait_recv()
-        self.copy(i).wait_send()
-        self.total[i + 1] = self.total[i] + self.arrived[i]
+        p = self.p
+        for copy in self.copies(i):
+            copy.wait_recv()
+            copy.wait_send()
+        if i < 3:
+            self.total[i + 1] = self.total[i] + self.arrived[i]
+        else:
+            self.arrived[3] = self.total[i]
+            terms = [self.arrived[3 + (p.z - z + p.zs) % p.zs] for z in range(p.zs)]
+            self.total[i + 1] = functools.reduce(jnp.add, terms)
 
 
 def back_kernel(zs, xs, shape, width, kept, live, *refs):
     q, k, v, bias, grad, out, norm, attended, branch_hbm, normed_hbm, parts, weights_hbm = refs[:12]
-    d_middle, x_low, gain, d_gain_two = refs[12:16]
-    d_x, (sums, vector_out) = refs[16:18], refs[18:20]
+    d_middle, x_low, gain, d_gain_two, kept_sums = refs[12:17]
+    d_x, feed_out, attention_out, vector_out = refs[17:19], refs[19:22], refs[22:26], refs[26]
+    refs = refs[7:]
     (stage, turn_buf, d_q, d_kv, back_kv, k_sum, v_sum, d_bias) = refs[20:28]
     (w_buf, held, vector, total, arrived, gain_sum) = refs[28:34]
     (local, loads, kv_sems, both_sems) = refs[34:38]
@@ -893,7 +897,38 @@
         for i in range(3):
             weights_load(i).start()
 
-    engine = Scatter(place, bufs, *scatter_sems, sums)
+    def feed_store(j, half, total):
+        piece = 2 * j + half
+
+        @pl.when(piece < feed_out[0].shape[1] // T)
+        def _():
+            part = pl.ds(pl.multiple_of(piece * T, T), T)
+            for i in range(3):
+                feed_out[i][:, part] = total[i]
+
+    def keep(c, half, total):
+        @pl.when(c < fed)
+        def _():
+            feed_store(jnp.where(c < first_kept, c, c + end_kept - first_kept), half, total)
+
+        for m, matrix in enumerate((3, 0, 1, 2)):
+
+            @pl.when(c == fed + m)
+            def _(matrix=matrix):
+                for i in range(3):
+                    piece = 3 * half + i
+                    attention_out[matrix][:, piece * T : (piece + 1) * T] = total[i]
+
+    @pl.when(step == 1)
+    def _():
+        def one(k, carry):
+            for half in range(2):
+                feed_store(k + first_kept, half, kept_sums[k, half])
+            return carry
+
+        lax.fori_loop(0, end_kept - first_kept, one, 0)
+
+    engine = Scatter(place, bufs, *scatter_sems, keep)
 
     def due(offset, action):
         at = step - offset
@@ -933,10 +968,6 @@
         peer = place.device(x=1 - place.x)
         return remote(src, back_kv.at[p], kv_sems.at[0, p], kv_sems.at[1, p], peer)
 
-    @pl.when((step >= 2) & (step <= last) & (step % 2 == 0))
-    def _():
-        kv_send(step // 2 - 1).start()
-
     @pl.when(step < last)
     def _():
         p = step // 2
@@ -961,6 +992,7 @@
             for_tiles(shape, True, action)
             d_kv[p, 0] = k_sum[...].astype(BF)
             d_kv[p, 1] = v_sum[...].astype(BF)
+            kv_send(p).start()
             for h in range(2):
                 vector[2 * p + h] = band_sums(d_bias, h)
 
@@ -1036,38 +1068,36 @@
 
     mix = Combine(place, total, arrived, both_sems.at[0], both_sems.at[1])
     start = last + blocks
-    stages = total.shape[0] - 1
     tiles = 2 * pairs
 
-    @pl.when(step == start)
+    @pl.when(step == start - 1)
     def _():
         total[0, 0:tiles] = vector[...]
         both = rows_of(gain_sum[...]) + rows_of(d_gain_two[...])
         for i in range(len(both) // VECTOR_ROWS):
             group = both[i * VECTOR_ROWS : (i + 1) * VECTOR_ROWS]
             total[0, tiles + i] = jnp.concatenate(group, axis=0)
-
-    for i in range(stages + 1):
-
-        @pl.when(step == start + 1 + i)
+        mix.start(0)
+
+    for i in range(mix.STAGES):
+
+        @pl.when(step == start + i)
         def _(i=i):
-            if i > 0:
-                mix.finish(i - 1)
-            if i < stages:
-                mix.start(i)
+            mix.finish(i)
+            if i + 1 < mix.STAGES:
+                mix.start(i + 1)
             else:
-                vector_out[...] = total[stages]
+                vector_out[...] = total[mix.STAGES]
 
 
 def back(q, kv, bias, grad, out, norm, branch, normed, parts, weights, d_middle, x_low, gain,
-         d_gain_two, live, shape, sizes, kept, collective_id):
+         d_gain_two, kept_sums, hidden, live, shape, sizes, kept, collective_id):
     grp, seq = sizes
     rows, width = x_low.shape
     pairs = q.shape[0]
     zs = grp // (Y * C)
     keys = shape.keys
     chunks, _, n, _, _, _, shard, lanes = parts.shape
-    count = chunks - (kept[1] - kept[0]) + 4
     assert chunks - (kept[1] - kept[0]) <= 2 * pairs
     assert (pairs, n) == (6, 3) and 2 * width // T % VECTOR_ROWS == 0
     last = 2 * pairs
@@ -1076,8 +1106,9 @@
     prompt = shape.local_tiles * T
     assert prompt % size == 0
     tile = (2, n, zs, Y, C * seq, shard, lanes)
-    stages = 3 + (zs - 1).bit_length()
-    steps = last + blocks + stages + 2
+    stages = Combine.STAGES
+    steps = max(last + blocks + stages, last + 8)
+    inner = pairs * 2 * HEAD
     vector = (2 * pairs + 2 * width // T // VECTOR_ROWS, VECTOR_ROWS, T)
     pair = lambda s: jnp.minimum(s // 2, pairs - 1)
     by_pair = lambda rows_: pl.BlockSpec((rows_, 2 * HEAD), lambda s, *_: (0, pair(s)))
@@ -1114,9 +1145,12 @@
                 by_rows,
                 full(1, width),
                 full(1, width),
+                full(*kept_sums.shape),
             ],
             out_specs=two_parts(size, width, prompt // size, blocks, last)
-            + [full(count, 2, n, shard, lanes), full(*vector)],
+            + [full(shard, hidden)] * 3
+            + [full(shard, inner)] * 4
+            + [full(*vector)],
             scratch_shapes=[
                 pltpu.VMEM((rows, width), BF),
                 pltpu.VMEM((width, rows), BF),
@@ -1130,12 +1164,12 @@
                 pltpu.VMEM((3, *tile), BF),
                 pltpu.VMEM((2 * pairs, VECTOR_ROWS, T), F32),
                 pltpu.VMEM((stages + 1, *vector), F32),
-                pltpu.VMEM((stages, *vector), F32),
+                pltpu.VMEM((3 + zs, *vector), F32),
                 pltpu.VMEM((1, width), F32),
                 sems(4),
                 sems(3),
                 sems(2, pairs),
-                sems(2, stages),
+                sems(2, 3 + zs),
             ]
             + scatter_buffers(n, zs, seq, shard, lanes)
             + [sems(2, 2, zs + 2), sems(2, 2, zs + 2)],
@@ -1143,14 +1177,17 @@
         out_shape=[
             jax.ShapeDtypeStruct((prompt, width), BF),
             jax.ShapeDtypeStruct((rows - prompt, width), BF),
-            jax.ShapeDtypeStruct((count, 2, n, shard, lanes), F32),
+        ]
+        + [jax.ShapeDtypeStruct((shard, hidden), F32)] * 3
+        + [jax.ShapeDtypeStruct((shard, inner), F32)] * 4
+        + [
             jax.ShapeDtypeStruct(vector, F32),
         ],
         compiler_params=pltpu.CompilerParams(
             collective_id=collective_id, has_side_effects=True, vmem_limit_bytes=VMEM_LIMIT
         ),
     )(live, q, kv, kv, bias, grad, out, norm, out, branch, normed, parts, weights, d_middle,
-      x_low, gain, d_gain_two)
+      x_low, gain, d_gain_two, kept_sums)
 
 
 GELU_SCALE = 0.7978845608028654
@@ -1332,7 +1369,10 @@
     def is_kept(j):
         return (j >= first_kept) & (j < end_kept)
 
-    engine = Scatter(place, bufs, *scatter_sems, sums)
+    def keep(k, half, total):
+        sums[k, half] = total
+
+    engine = Scatter(place, bufs, *scatter_sems, keep)
     due = lag + first_kept
     number = end_kept - first_kept
     grads_of = lambda k: g_buf.at[(k + first_kept) % 2]
@@ -1471,6 +1511,34 @@
     )(x, dy_one, dy_two, own, ready, middle, gain)
 
 
+def settle_kernel(*refs):
+    *refs, sem = refs
+    count = len(refs) // 3
+    sources, targets, held = refs[:count], refs[count : 2 * count], refs[2 * count :]
+    loads = [pltpu.make_async_copy(sources[i], held[i], sem.at[i]) for i in range(count)]
+    stores = [pltpu.make_async_copy(held[i], targets[i], sem.at[count + i]) for i in range(count)]
+    for load in loads:
+        load.start()
+    for load, store in zip(loads, stores):
+        load.wait()
+        store.start()
+    for store in stores:
+        store.wait()
+
+
+def settle(*arrays):
+    anywhere = pl.BlockSpec(memory_space=pl.ANY)
+    return pl.pallas_call(
+        settle_kernel,
+        in_specs=[anywhere] * len(arrays),
+        out_specs=[anywhere] * len(arrays),
+        out_shape=[jax.ShapeDtypeStruct(a.shape, a.dtype) for a in arrays],
+        scratch_shapes=[pltpu.VMEM(a.shape, a.dtype) for a in arrays]
+        + [pltpu.SemaphoreType.DMA((2 * len(arrays),))],
+        compiler_params=pltpu.CompilerParams(vmem_limit_bytes=VMEM_LIMIT),
+    )(*arrays)
+
+
 def rms_scale(values):
     return lax.rsqrt(jnp.mean(values * values, axis=-1, keepdims=True) + EPS)
 
@@ -1554,14 +1622,16 @@
             normed_two, prompt_cot[0], cont_dy, own_feed, whole, middle, gains[1], inner, sizes,
             early, kept, 1,
         )
-        *d_x, sums, vector = back(
+        (*d_x, gate_grad, up_grad, down_grad, q_grad, k_grad, v_grad, o_grad, vector) = back(
             queries, kv, bias, d_attended, attended, log_norm, d_branch, normed_one, feed_parts,
-            whole, d_middle, x_low, gains[0], d_gain_two, cont_len, shape, sizes, kept, 2,
+            whole, d_middle, x_low, gains[0], d_gain_two, kept_sums, hidden_width, cont_len, shape,
+            sizes, kept, 2,
         )
-        fed = sums.shape[0] - 4
-        feed_sums = jnp.concatenate([sums[: kept[0]], kept_sums, sums[kept[0] : fed]], axis=0)
-        attention_sums = jnp.concatenate([sums[fed + 1 :], sums[fed : fed + 1]], axis=0)
-        attention_sums = attention_sums.reshape(-1, shard, T)
+        settled = settle(
+            *final, *d_x, gate_grad, up_grad, down_grad, q_grad, k_grad, v_grad, o_grad
+        )
+        final, d_x = settled[:2], settled[2:4]
+        gate_grad, up_grad, down_grad, q_grad, k_grad, v_grad, o_grad = settled[4:]
         near = vector[:heads, :4].reshape(heads, SPAN)
         far = jnp.sum(vector[:heads, 4:6], axis=-1)
         relative = (jnp.arange(SPAN) + T) % SPAN - 2 * T
@@ -1633,11 +1703,11 @@
         norm1_grad = lax.psum_scatter(d_gain_one, ("grp", "seq"), scatter_dimension=0, tiled=True)
         norm2_grad = lax.psum_scatter(d_gain_two, ("grp", "seq"), scatter_dimension=0, tiled=True)
         table_grad = lax.psum(d_table, ("grp", "seq"))
-    feed_sums = feed_sums.reshape(-1, 3, shard, T)[: hidden_width // T]
-    gate_grad, up_grad, down_grad = [joined(feed_sums[:, i]) for i in range(3)]
-    q_grad, k_grad, v_grad, o_grad = [
-        joined(attention_sums[i * count : (i + 1) * count]) for i in range(4)
-    ]
+        feed_sums = feed_sums.reshape(-1, 3, shard, T)[: hidden_width // T]
+        gate_grad, up_grad, down_grad = [joined(feed_sums[:, i]) for i in range(3)]
+        q_grad, k_grad, v_grad, o_grad = [
+            joined(attention_sums[i * count : (i + 1) * count]) for i in range(4)
+        ]
     return (
         *split(final),
         *split(d_x),

time: 626 us -> 616 us (0.984)
  local copies, waits for them, and re-layouts: 20.8 us -> 5.51 us
    unnamed x31 -> x5, local copies, waits for them, and re-layouts: 15.1 us -> 1.4 us
    pallas_call x0 -> x1, Pallas kernels: none -> 7.18 us  [settle(): pl.pallas_call(settle_kernel, in_specs=[anywhere] * len(arrays), out_spec...]
where the time goes in v7:
time: 616 us; the launch traced here: 615 us
  Pallas kernels  606 us (98%)
    pallas_call x1, Pallas kernels, back(): pl.pallas_call(functools.partial(back_kernel, zs, seq, shape, width, kept...  213 us
    pallas_call x1, Pallas kernels, feed_moving(): pl.pallas_call(functools.partial(feed_moving_kernel, zs, seq, early, kept...  207 us
    pallas_call x1, Pallas kernels, front(): pl.pallas_call(functools.partial(front_kernel, zs, seq, shape, early), gr...  180 us

profile of v7, /device:TPU:0, one launch (start us, length us, event | category | flops | bytes accessed | tf_op | source)
XLA Modules:
  0.0 615.2 jit_solution(1776921230938860606)
XLA Ops:
  0.6 0.7 convert_bitcast_fusion
  1.3 0.7 broadcast_in_dim.6.refs_2_
  2.0 1.4 copy.30.refs_10_
  3.4 179.6 %shard_map.263 = (bf16[11,2,3,4,2,4,48,128]{7,6,5,4,3,2,1,0:T(8,128)(2,1)}, bf16[16,2,3,48,128]{4,3,2,1,0:T(8,128)(2,1)}, bf16[1024,1536]{1,0:T(8,128)(2,1)}, bf...) custom-call(s32[1,4]{1,0:T(1,128)} %live.3, ...), custom_call_target="tpu_custom_call" | custom-call | tf_op jit(solution)/shard_map/pallas_call | solution.py:723
  183.0 1.3 slice_bitcast_fusion
  184.3 206.8 %shard_map.264 = (bf16[16,2,3,4,2,4,48,128]{7,6,5,4,3,2,1,0:T(8,128)(2,1)}, bf16[16,2,3,4,2,4,48,128]{7,6,5,4,3,2,1,0:T(8,128)(2,1)}, f32[6,2,3,48,128]{4,3,2,1,...) custom-call(bf16[1024,1536]{1,0:T(8,128)(2,1)} %get-tuple-element.55, ...), custom_call_target="tpu_custom_call" | custom-call | tf_op jit(solution)/shard_map/pallas_call | solution.py:1477
  391.1 0.0 copy-start
  391.1 212.9 %shard_map.265 = (bf16[512,1536]{1,0:T(8,128)(2,1)}, bf16[512,1536]{1,0:T(8,128)(2,1)}, f32[48,3968]{1,0:T(8,128)}, f32[48,3968]{1,0:T(8,128)}, f32[48,3968]{1,0...) custom-call(s32[1,4]{1,0:T(1,128)} %live.3, ...), custom_call_target="tpu_custom_call" | custom-call | tf_op jit(solution)/shard_map/pallas_call | solution.py:1126
  604.0 0.8 slice.20
  604.9 0.9 slice_reduce_fusion
  605.8 0.0 copy-done
  605.8 0.9 fusion
  606.7 7.2 %shard_map.266 = (bf16[512,1536]{1,0:T(8,128)(2,1)}, bf16[512,1536]{1,0:T(8,128)(2,1)}, bf16[512,1536]{1,0:T(8,128)(2,1)}, bf16[512,1536]{1,0:T(8,128)(2,1)}, f3...) custom-call(bf16[512,1536]{1,0:T(8,128)(2,1)} %get-tuple-element.60., ...), custom_call_target="tpu_custom_call" | custom-call | tf_op jit(solution)/shard_map/pallas_call | solution.py:1531
  613.9 0.7 slice.19
  614.6 0.1 reshape.63
  614.7 0.5 dynamic-slice_bitcast_fusion
  (5 shorter events, 0.0 us)
Async XLA Ops:
  391.1 214.7 %copy-start = (s32[2]{0:T(128)S(1)}, s32[2]{0:T(128)}, u32[]{:S(2)}) copy-start(s32[2]{0:T(128)} %constant.113) | copy-start | bytes 28

commit v8 on v7

--- a/solution.py
+++ b/solution.py
@@ -517,9 +517,9 @@
     (prompt_x, cont_x, own_gain, *weights) = refs[:10]
     table = refs[10]
     (whole, own_out, x_out, normed_out, kv_out, bias_out) = refs[11:17]
-    (q, attended, norm, middle, normed_two, gains) = refs[17:23]
-    (x, normed, kv, bias, held, w_buf, gain_whole) = refs[23:30]
-    (local, kv_sems, send, recv, gain_send, gain_recv) = refs[30:36]
+    (q, attended, norm, middle, normed_two, *gains) = refs[17:24]
+    (x, normed, kv, bias, held, w_buf, gain_whole) = refs[24:31]
+    (local, kv_sems, send, recv, gain_send, gain_recv) = refs[31:37]
     place = Place(zs, xs)
     step = pl.program_id(0)
     rows, width = x.shape
@@ -584,17 +584,17 @@
     def _():
         query = lax.broadcasted_iota(jnp.int32, (T, T), 0)
         key = lax.broadcasted_iota(jnp.int32, (T, T), 1)
-        half = table.shape[0] // 2
+        half = table.shape[1] // 2
         ids = [bucket_ids(band * T + key - query) for band in (-1, 0, 1)]
         found = (range(1, half), [*range(half), *range(half + 1, 2 * half)], range(half + 1, 2 * half))
 
         def one(h, carry):
-            bias[h, 0] = jnp.full((T, T), table[half - 1, h])
-            bias[h, 4] = jnp.full((T, T), table[2 * half - 1, h])
+            bias[h, 0] = jnp.full((T, T), table[h, half - 1])
+            bias[h, 4] = jnp.full((T, T), table[h, 2 * half - 1])
             for band in range(3):
                 value = jnp.zeros((T, T), F32)
                 for bucket in found[band]:
-                    value = jnp.where(ids[band] == bucket, table[bucket, h], value)
+                    value = jnp.where(ids[band] == bucket, table[h, bucket], value)
                 bias[h, 1 + band] = value
             return carry
 
@@ -621,12 +621,12 @@
             column = gain_whole[0, g, 0].reshape(width, T).astype(F32)
             for i in range(width // T):
                 cols = slice(i * T, (i + 1) * T)
-                gains[g, :, cols] = jnp.sum(jnp.where(eye, column[cols], 0.0), axis=0, keepdims=True)
+                gains[g][:, cols] = jnp.sum(jnp.where(eye, column[cols], 0.0), axis=0, keepdims=True)
 
         def norm_rows(part):
             values = x[part, :].astype(F32)
             scale = lax.rsqrt(jnp.mean(values * values, axis=-1, keepdims=True) + EPS)
-            normed[part, :] = (values * scale * gains[0]).astype(BF)
+            normed[part, :] = (values * scale * gains[0][...]).astype(BF)
 
         by_rows(norm_rows)
         result(2).start()
@@ -688,7 +688,7 @@
         total = x[part, :].astype(F32) + branch
         middle[...] = total
         scale = lax.rsqrt(jnp.mean(total * total, axis=-1, keepdims=True) + EPS)
-        normed_two[...] = (total * scale * gains[1]).astype(BF)
+        normed_two[...] = (total * scale * gains[1][...]).astype(BF)
 
     @pl.when(step == last + blocks - 1)
     def _():
@@ -701,8 +701,8 @@
     rows, width = shape.rows, prompt_x.shape[1]
     shard, inner = weights[0].shape
     feed_columns = weights[4].shape[1] // T
-    pairs, keys, heads = inner // (2 * HEAD), shape.keys, table.shape[1]
-    assert pairs == 6 and table.shape[0] == 32 and keys - rows == prompt_x.shape[0]
+    pairs, keys, heads = inner // (2 * HEAD), shape.keys, table.shape[0]
+    assert pairs == 6 and table.shape[1] == 32 and keys - rows == prompt_x.shape[0]
     zs = grp // (Y * C)
     chunks = 4 + (feed_columns + 1) // 2
     count = 4 + early
@@ -737,7 +737,8 @@
                 ),
                 by_rows,
                 by_rows,
-                full(2, 1, width),
+                full(1, width),
+                full(1, width),
             ],
             scratch_shapes=[
                 pltpu.VMEM((rows, width), BF),
@@ -767,7 +768,8 @@
             out((2 * pairs, rows, 1), F32),
             out((rows, width), F32),
             out((rows, width), BF),
-            out((2, 1, width), F32),
+            out((1, width), F32),
+            out((1, width), F32),
         ],
         compiler_params=pltpu.CompilerParams(
             collective_id=collective_id, has_side_effects=True, vmem_limit_bytes=VMEM_LIMIT
@@ -932,9 +934,9 @@
 
     def due(offset, action):
         at = step - offset
-        chunk = jnp.where(at < last, at, at - last + fed)
-        early = (at >= 0) & (at < fed)
-        late = (at >= last) & (at < last + 4)
+        chunk = jnp.where(at <= fed, at, at - last + fed)
+        early = (at >= 0) & (at <= fed)
+        late = (at > last) & (at < last + 4)
 
         @pl.when(early | late)
         def _():
@@ -1013,7 +1015,7 @@
 
             lax.fori_loop(0, zs, one, 0)
 
-    @pl.when(step == last - 1)
+    @pl.when(step == fed - 1)
     def _():
         produce(fed, lambda m: jnp.concatenate([attended[2 * m], attended[2 * m + 1]], axis=1))
 
@@ -1098,7 +1100,7 @@
     zs = grp // (Y * C)
     keys = shape.keys
     chunks, _, n, _, _, _, shard, lanes = parts.shape
-    assert chunks - (kept[1] - kept[0]) <= 2 * pairs
+    assert 0 < chunks - (kept[1] - kept[0]) <= 2 * pairs
     assert (pairs, n) == (6, 3) and 2 * width // T % VECTOR_ROWS == 0
     last = 2 * pairs
     size = min(rows, 256)
@@ -1376,11 +1378,15 @@
     due = lag + first_kept
     number = end_kept - first_kept
     grads_of = lambda k: g_buf.at[(k + first_kept) % 2]
-    staged(step, due + 5, number, engine.finish)
-    staged(step, due + 4, number, engine.start_fourth)
-    staged(step, due + 3, number, engine.start_third)
-    staged(step, due + 2, number, lambda k: engine.start_second(k, grads_of(k)))
-    staged(step, due + 1, number, lambda k: engine.start_first(k, grads_of(k)))
+
+    def tick(at):
+        staged(at, due + 5, number, engine.finish)
+        staged(at, due + 4, number, engine.start_fourth)
+        staged(at, due + 3, number, engine.start_third)
+        staged(at, due + 2, number, lambda k: engine.start_second(k, grads_of(k)))
+        staged(at, due + 1, number, lambda k: engine.start_first(k, grads_of(k)))
+
+    tick(step)
 
     chunk = step - lag
     if lag == 0:
@@ -1466,8 +1472,8 @@
     size = min(rows, 256)
     blocks = rows // size
     assert dy_one.shape[0] % size == 0
-    steps = lag + max(chunks + max(2, blocks), kept[1] + 5)
     tail = lag + chunks
+    steps = max(tail + max(2, blocks), lag + kept[1] + 5)
     by_rows = lambda columns: pl.BlockSpec(
         (size, columns), lambda j: (jnp.clip(j - tail, 0, blocks - 1), 0)
     )
@@ -1614,8 +1620,8 @@
         cont_dy = cont_cot[0].reshape(-1, width)
         matrices = (q_weight, k_weight, v_weight, o_weight, gate_weight, up_weight, down_weight)
         (whole, own_feed, x_low, normed_one, kv, bias, queries, attended, log_norm, middle,
-         normed_two, gains) = front(
-            prompt_x[0], cont_x[0].reshape(-1, width), own_gain, matrices, bucket_table, cont_len,
+         normed_two, *gains) = front(
+            prompt_x[0], cont_x[0].reshape(-1, width), own_gain, matrices, bucket_table.T, cont_len,
             shape, sizes, early, 0,
         )
         _, feed_parts, kept_sums, *final, d_middle, d_branch, d_attended, d_gain_two = feed_moving(

time: 616 us -> 609 us (0.989)
  no operation moved by 1% of the time
where the time goes in v8:
time: 609 us
  Pallas kernels  603 us (99%)
    pallas_call x1, Pallas kernels, back(): pl.pallas_call(functools.partial(back_kernel, zs, seq, shape, width, kept...  209 us
    pallas_call x1, Pallas kernels, feed_moving(): pl.pallas_call(functools.partial(feed_moving_kernel, zs, seq, early, kept...  206 us
    pallas_call x1, Pallas kernels, front(): pl.pallas_call(functools.partial(front_kernel, zs, seq, shape, early), gr...  180 us

profile of v8, /device:TPU:0, one launch (start us, length us, event | category | flops | bytes accessed | tf_op | source)
XLA Modules:
  0.0 608.7 jit_solution(8425887010843797182)
XLA Ops:
  0.6 0.7 convert_bitcast_fusion
  1.3 0.7 broadcast_in_dim.6.refs_2_
  2.0 179.6 %shard_map.263 = (bf16[11,2,3,4,2,4,48,128]{7,6,5,4,3,2,1,0:T(8,128)(2,1)}, bf16[16,2,3,48,128]{4,3,2,1,0:T(8,128)(2,1)}, bf16[1024,1536]{1,0:T(8,128)(2,1)}, bf...) custom-call(s32[1,4]{1,0:T(1,128)} %live.3, ...), custom_call_target="tpu_custom_call" | custom-call | tf_op jit(solution)/shard_map/pallas_call | solution.py:723
  181.7 206.5 %shard_map.264 = (bf16[16,2,3,4,2,4,48,128]{7,6,5,4,3,2,1,0:T(8,128)(2,1)}, bf16[16,2,3,4,2,4,48,128]{7,6,5,4,3,2,1,0:T(8,128)(2,1)}, f32[6,2,3,48,128]{4,3,2,1,...) custom-call(bf16[1024,1536]{1,0:T(8,128)(2,1)} %get-tuple-element.56, ...), custom_call_target="tpu_custom_call" | custom-call | tf_op jit(solution)/shard_map/pallas_call | solution.py:1483
  388.2 0.0 copy-start
  388.2 209.4 %shard_map.265 = (bf16[512,1536]{1,0:T(8,128)(2,1)}, bf16[512,1536]{1,0:T(8,128)(2,1)}, f32[48,3968]{1,0:T(8,128)}, f32[48,3968]{1,0:T(8,128)}, f32[48,3968]{1,0...) custom-call(s32[1,4]{1,0:T(1,128)} %live.3, ...), custom_call_target="tpu_custom_call" | custom-call | tf_op jit(solution)/shard_map/pallas_call | solution.py:1128
  597.6 0.8 slice.12
  598.4 0.9 slice_reduce_fusion
  599.3 0.0 copy-done
  599.3 0.9 fusion
  600.2 7.2 %shard_map.266 = (bf16[512,1536]{1,0:T(8,128)(2,1)}, bf16[512,1536]{1,0:T(8,128)(2,1)}, bf16[512,1536]{1,0:T(8,128)(2,1)}, bf16[512,1536]{1,0:T(8,128)(2,1)}, f3...) custom-call(bf16[512,1536]{1,0:T(8,128)(2,1)} %get-tuple-element.61., ...), custom_call_target="tpu_custom_call" | custom-call | tf_op jit(solution)/shard_map/pallas_call | solution.py:1537
  607.4 0.7 slice.11
  608.1 0.1 reshape.63
  608.2 0.5 dynamic-slice_bitcast_fusion
  (5 shorter events, 0.0 us)
Async XLA Ops:
  388.2 211.2 %copy-start = (s32[2]{0:T(128)S(1)}, s32[2]{0:T(128)}, u32[]{:S(2)}) copy-start(s32[2]{0:T(128)} %constant.113) | copy-start | bytes 28

commit v9 on v8

--- a/solution.py
+++ b/solution.py
@@ -1019,10 +1019,13 @@
     def _():
         produce(fed, lambda m: jnp.concatenate([attended[2 * m], attended[2 * m + 1]], axis=1))
 
-    @pl.when(step == last)
+    @pl.when(step == fed)
     def _():
         stage_load(normed_hbm).wait()
         turn()
+
+    @pl.when(step == last)
+    def _():
         produce(fed + 1, lambda m: jnp.concatenate([d_q[2 * m], d_q[2 * m + 1]], axis=1))
 
         def join(p, carry):
@@ -1614,7 +1617,7 @@
     shape = Shape(tiles, local_tiles, conts)
     count = inner // T
     if can_move(sizes, shard):
-        early, kept = 7, (9, 15)
+        early, kept = 7, (8, 14)
         own_gain = jnp.stack([norm1_gain, norm2_gain])[None, :, None, :, None]
         own_gain = jnp.broadcast_to(own_gain, (1, 2, 1, shard, T)).astype(BF)
         cont_dy = cont_cot[0].reshape(-1, width)

time: 609 us -> 604 us (level)
  no operation moved by 1% of the time
where the time goes in v9:
time: 604 us
  Pallas kernels  598 us (99%)
    pallas_call x1, Pallas kernels, back(): pl.pallas_call(functools.partial(back_kernel, zs, seq, shape, width, kept...  208 us
    pallas_call x1, Pallas kernels, feed_moving(): pl.pallas_call(functools.partial(feed_moving_kernel, zs, seq, early, kept...  203 us
    pallas_call x1, Pallas kernels, front(): pl.pallas_call(functools.partial(front_kernel, zs, seq, shape, early), gr...  180 us

profile of v9, /device:TPU:0, one launch (start us, length us, event | category | flops | bytes accessed | tf_op | source)
XLA Modules:
  0.0 603.9 jit_solution(14884856153681849189)
XLA Ops:
  0.6 0.7 convert_bitcast_fusion
  1.3 0.7 broadcast_in_dim.6.refs_2_
  2.0 179.6 %shard_map.263 = (bf16[11,2,3,4,2,4,48,128]{7,6,5,4,3,2,1,0:T(8,128)(2,1)}, bf16[16,2,3,48,128]{4,3,2,1,0:T(8,128)(2,1)}, bf16[1024,1536]{1,0:T(8,128)(2,1)}, bf...) custom-call(s32[1,4]{1,0:T(1,128)} %live.3, ...), custom_call_target="tpu_custom_call" | custom-call | tf_op jit(solution)/shard_map/pallas_call | solution.py:723
  181.7 202.9 %shard_map.264 = (bf16[16,2,3,4,2,4,48,128]{7,6,5,4,3,2,1,0:T(8,128)(2,1)}, bf16[16,2,3,4,2,4,48,128]{7,6,5,4,3,2,1,0:T(8,128)(2,1)}, f32[6,2,3,48,128]{4,3,2,1,...) custom-call(bf16[1024,1536]{1,0:T(8,128)(2,1)} %get-tuple-element.56, ...), custom_call_target="tpu_custom_call" | custom-call | tf_op jit(solution)/shard_map/pallas_call | solution.py:1486
  384.6 0.0 copy-start
  384.6 208.1 %shard_map.265 = (bf16[512,1536]{1,0:T(8,128)(2,1)}, bf16[512,1536]{1,0:T(8,128)(2,1)}, f32[48,3968]{1,0:T(8,128)}, f32[48,3968]{1,0:T(8,128)}, f32[48,3968]{1,0...) custom-call(s32[1,4]{1,0:T(1,128)} %live.3, ...), custom_call_target="tpu_custom_call" | custom-call | tf_op jit(solution)/shard_map/pallas_call | solution.py:1131
  592.7 0.8 slice.12
  593.5 0.9 slice_reduce_fusion
  594.4 0.0 copy-done
  594.5 0.9 fusion
  595.4 7.2 %shard_map.266 = (bf16[512,1536]{1,0:T(8,128)(2,1)}, bf16[512,1536]{1,0:T(8,128)(2,1)}, bf16[512,1536]{1,0:T(8,128)(2,1)}, bf16[512,1536]{1,0:T(8,128)(2,1)}, f3...) custom-call(bf16[512,1536]{1,0:T(8,128)(2,1)} %get-tuple-element.61., ...), custom_call_target="tpu_custom_call" | custom-call | tf_op jit(solution)/shard_map/pallas_call | solution.py:1540
  602.6 0.7 slice.11
  603.3 0.1 reshape.63
  603.3 0.5 dynamic-slice_bitcast_fusion
  (5 shorter events, 0.1 us)
Async XLA Ops:
  384.6 209.9 %copy-start = (s32[2]{0:T(128)S(1)}, s32[2]{0:T(128)}, u32[]{:S(2)}) copy-start(s32[2]{0:T(128)} %constant.113) | copy-start | bytes 28
